TPU v7x, 32 devices: a whole 2x2x4 slice. The times are simulated.
32 devices in a mesh: row: 8 (over z, core), col: 4 (over y, x).
Axes of the slice: x: 2, y: 2, z: 4, core: 2. Of those that a mesh axis runs over, the one named last changes fastest.
Arguments:
- start_panel: bfloat16 [32768, 128], P(('col', 'row')), may hold values from -6 to 6
- block_values: bfloat16 [8, 4, 352, 128, 128], P('row', 'col'), may hold values from -0.078125 to 0.078125
- block_rows: int32 [8, 4, 352], P('row', 'col'), may hold values from 0 to 31, as said below
- block_cols: int32 [8, 4, 352], P('row', 'col'), may hold values from 0 to 63, as said below
- block_counts: int32 [8, 4], P('row', 'col'), may hold values from 141 to 352, as said below
Outputs:
- left_panel: bfloat16 [32768, 128], P(('row', 'col'))
- right_panel: bfloat16 [32768, 128], P(('col', 'row'))
Inputs may be any that keep to these rules, and one draw needn't show every extreme that they name: `block_rows`: block rows lie in 0 to 31 within each tile; low block rows hold more blocks; in every tile some live slot names block row 31. `block_cols`: in every tile some live slot names block column 63; a position may repeat. Only the first block_counts[r, c] slots of tile (r, c) are live; some tile fills all 352 slots.
All inputs are finite; a program needn't handle non-finite values.
Results may differ from a plain program's by a relative error of at most 0.0085.
Values may be sent and summed in bfloat16 or wider, within the bound.
No kernel may reach another device: no remote copies, remote signals or barrier semaphores. Data moves between devices by JAX's collectives and lax.ppermute only.
A program may use at most 128 MiB of HBM per device.

v0:
```python
import jax
import jax.numpy as jnp
from jax import lax
from jax.sharding import PartitionSpec as P


def tile_product(values, index_out, index_in, live_count, panel_in, out_blocks, flipped):
    block_size = values.shape[-1]
    pieces = panel_in.reshape(-1, block_size, panel_in.shape[1])
    selected = jnp.take(pieces, index_in, axis=0)
    if flipped:
        products = jnp.einsum("kij,kip->kjp", values, selected, preferred_element_type=jnp.float32)
    else:
        products = jnp.einsum("kij,kjp->kip", values, selected, preferred_element_type=jnp.float32)
    slots = jnp.arange(values.shape[0], dtype=jnp.int32)
    live = (slots < live_count).astype(jnp.float32)
    targets = jnp.arange(out_blocks, dtype=jnp.int32)
    placement = (targets[:, None] == index_out[None, :]).astype(jnp.float32) * live[None, :]
    summed = jnp.einsum("ok,kip->oip", placement, products, precision=lax.Precision.HIGHEST)
    return summed.reshape(out_blocks * block_size, panel_in.shape[1])


def gram_local(y_rounded, nodes_total):
    return jnp.dot(y_rounded.T, y_rounded, preferred_element_type=jnp.float32) / nodes_total


def apply_factor(y_rounded, gram_total):
    lower = jnp.linalg.cholesky(gram_total)
    identity = jnp.eye(gram_total.shape[0], dtype=jnp.float32)
    inverse = jax.scipy.linalg.solve_triangular(lower, identity, lower=True)
    solved = jnp.dot(y_rounded.astype(jnp.float32), inverse.T, precision=lax.Precision.HIGHEST)
    return solved.astype(jnp.bfloat16)


def global_gram(y_rounded, nodes_total):
    partial_value = gram_local(y_rounded, nodes_total)
    within = lax.psum(partial_value.astype(jnp.bfloat16), "col").astype(jnp.float32)
    return lax.psum(within, "row")


def local(start_panel, block_values, block_rows, block_cols, block_counts):
    group_rows = start_panel.shape[0]
    row_devices = lax.axis_size("row")
    col_devices = lax.axis_size("col")
    nodes_total = group_rows * row_devices * col_devices
    values = block_values[0, 0]
    rows_local = block_rows[0, 0]
    cols_local = block_cols[0, 0]
    live_count = block_counts[0, 0]
    block_size = values.shape[-1]
    row_blocks = group_rows * col_devices // block_size
    col_blocks = group_rows * row_devices // block_size
    column_tile = lax.all_gather(start_panel, "row", axis=0, tiled=True)
    left_partial = tile_product(
        values, rows_local, cols_local, live_count, column_tile, row_blocks, False
    )
    left_group = lax.psum_scatter(left_partial, "col", scatter_dimension=0, tiled=True).astype(
        jnp.bfloat16
    )
    left_panel = apply_factor(left_group, global_gram(left_group, nodes_total))
    row_tile = lax.all_gather(left_panel, "col", axis=0, tiled=True)
    right_partial = tile_product(
        values, cols_local, rows_local, live_count, row_tile, col_blocks, True
    )
    right_group = lax.psum_scatter(right_partial, "row", scatter_dimension=0, tiled=True).astype(
        jnp.bfloat16
    )
    right_panel = apply_factor(right_group, global_gram(right_group, nodes_total))
    return (left_panel, right_panel)


def solution(mesh):
    return jax.shard_map(
        local,
        mesh=mesh,
        in_specs=(
            P(("col", "row"), None),
            P("row", "col", None, None, None),
            P("row", "col", None),
            P("row", "col", None),
            P("row", "col"),
        ),
        out_specs=(P(("row", "col"), None), P(("col", "row"), None)),
        check_vma=False,
    )
```

profile of v0, /device:TPU:0, one launch (start us, length us, event | category | flops | bytes accessed | tf_op | source)
XLA Modules:
  0.0 443.6 jit_solution(17568605688700938867)
XLA Ops:
  7.2 0.0 all-gather.3.cloned.1.call-start
  7.2 0.7 all-gather.3.cloned.1.call-update
  7.9 0.0 reduce-scatter.3.cloned.1.call-start
  8.6 0.7 reduce.4
  9.3 0.7 reduce.5
  10.0 0.7 fusion.41
  10.7 30.8 %all-gather.3.cloned.1.call-done = bf16[8192,128]{1,0:T(8,128)(2,1)} async-done(((bf16[1024,128]{1,0:T(8,128)(2,1)}), bf16[8192,128]{1,0:T(8,128)(2,1)}) %all-gather.3.cloned.1.call-update) | async-done | bytes 2097168 | tf_op jit(solution)/shard_map/all_gather | solution.py:53
  41.5 12.6 %gather_fusion = bf16[352,128,128]{2,1,0:T(8,128)(2,1)} fusion(bf16[64,128,128]{2,1,0:T(8,128)(2,1)} %bitcast.48, s32[1024]{0:T(1024)S(1)} %pad_clamp_fusion.1), kind=kCustom, calls=%fused_computation | custom fusion | bytes 23070080 | tf_op jit(solution)/shard_map/jit(_take)/gather | solution.py:10
  54.1 21.3 %fusion.6 = f32[352,128,128]{2,1,0:T(8,128)} fusion(bf16[1,1,352,128,128]{4,3,2,1,0:T(8,128)(2,1)} %param.9, bf16[352,128,128]{2,1,0:T(8,128)(2,1)} %gather_fusion, pred[352]{0:T(512)(128)(4,1)S(1)} %compare_and_fusion.1), kind=kOutput, calls=%fused_computation.8 | convolution fusion | flops 1482162176 | bytes 46137696 | tf_op jit(solution)/shard_map/kij,kjp->kip/dot_general | solution.py:14
  75.3 23.6 %copy.17 = f32[352,128,128]{1,0,2:T(8,128)} copy(f32[352,128,128]{2,1,0:T(8,128)} %fusion.6) | data formatting | bytes 46137344 | tf_op jit(solution)/shard_map/kij,kjp->kip/dot_general | solution.py:14
  98.9 0.0 copy-start
  98.9 15.9 %fusion.2 = f32[32,128,128]{2,0,1:T(8,128)S(1)} fusion(f32[352,128,128]{1,0,2:T(8,128)} %copy.17, f32[352]{0:T(512)S(1)} %fusion.40, s32[352]{0:T(512)S(1)} %reduce.4), kind=kOutput, calls=%fused_computation.4 | convolution fusion | flops 2214615040 | bytes 25168640 | tf_op jit(solution)/shard_map/ok,kip->oip/dot_general | solution.py:19
  114.8 2.6 copy.11
  117.3 0.0 reduce-scatter.3.cloned.1.call-update
  117.3 0.0 all-gather.5.cloned.1.call-start
  117.4 34.7 %reduce-scatter.3.cloned.1.call-done = f32[1024,128]{1,0:T(8,128)} async-done(((f32[4096,128]{1,0:T(8,128)}), f32[1024,128]{1,0:T(8,128)}) %reduce-scatter.3.cloned.1.call-update) | async-done | bytes 524304 | tf_op jit(solution)/shard_map/reduce_scatter | solution.py:57
  152.1 1.5 fusion.14
  153.6 15.4 %psum.28 = bf16[128,128]{0,1:T(8,128)(2,1)S(1)} all-reduce(bf16[128,128]{0,1:T(8,128)(2,1)S(1)} %fusion.14), channel_id=1, replica_groups=mesh['row'=8,'col'=4] {'col'}, use_global_device_ids=true, to_apply=%region_1.2 | all-reduce | flops 16384 | bytes 65536 | tf_op jit(solution)/shard_map/psum | solution.py:37
  169.0 26.5 %all-reduce.2 = f32[128,128]{0,1:T(8,128)S(1)} all-reduce(bf16[128,128]{0,1:T(8,128)(2,1)S(1)} %psum.28), channel_id=1, replica_groups=mesh['row'=8,'col'=4] {'row'}, use_global_device_ids=true, to_apply=%region_2.3 | all-reduce | flops 16384 | bytes 98304 | tf_op jit(solution)/shard_map/psum | solution.py:38
  195.5 0.1 copy.13
  195.6 11.7 %cholesky.44 = f32[128,128]{1,0:T(8,128)S(1)} custom-call(f32[128,128]{1,0:T(8,128)S(1)} %fusion.31), custom_call_target="Cholesky" | custom-call | tf_op jit(solution)/shard_map/jit(cholesky)/cholesky | solution.py:28
  207.3 0.6 compare_reduce_fusion.1
  208.0 0.7 fusion.26
  208.7 9.8 %custom-call.6 = f32[1,128,128]{1,2,0:T(8,128)S(1)} custom-call(f32[1,128,128]{2,1,0:T(8,128)S(1)} %fusion.26), custom_call_target="InvertDiagBlocksLowerTriangular" | custom-call | tf_op jit(solution)/shard_map/jit(_solve_triangular)/triangular_solve | solution.py:30
  218.5 0.3 fusion.24
  218.8 2.1 convolution_convert_fusion.1
  220.9 0.0 all-gather.5.cloned.1.call-update
  220.9 0.3 reduce-scatter.5.cloned.1.call-start
  221.2 0.0 copy-done
  221.2 23.5 %all-gather.5.cloned.1.call-done = bf16[4096,128]{1,0:T(8,128)(2,1)} async-done(((bf16[1024,128]{1,0:T(8,128)(2,1)}), bf16[4096,128]{1,0:T(8,128)(2,1)}) %all-gather.5.cloned.1.call-update) | async-done | bytes 1048592 | tf_op jit(solution)/shard_map/all_gather | solution.py:61
  244.7 12.1 %gather_fusion.1 = bf16[352,128,128]{2,1,0:T(8,128)(2,1)} fusion(bf16[32,128,128]{2,1,0:T(8,128)(2,1)} %bitcast.47, s32[1024]{0:T(1024)S(1)} %pad_clamp_fusion), kind=kCustom, calls=%fused_computation.1 | custom fusion | bytes 23070080 | tf_op jit(solution)/shard_map/jit(_take)/gather | solution.py:10
  256.9 14.6 %fusion.4 = f32[352,128,128]{2,1,0:T(8,128)} fusion(bf16[1,1,352,128,128]{4,3,2,1,0:T(8,128)(2,1)} %param.9, bf16[352,128,128]{2,1,0:T(8,128)(2,1)} %gather_fusion.1, pred[352]{0:T(512)(128)(4,1)S(1)} %compare_and_fusion), kind=kOutput, calls=%fused_computation.6 | convolution fusion | flops 1482162176 | bytes 46137696 | tf_op jit(solution)/shard_map/kij,kip->kjp/dot_general | solution.py:12
  271.4 23.6 %copy.19 = f32[352,128,128]{1,0,2:T(8,128)} copy(f32[352,128,128]{2,1,0:T(8,128)} %fusion.4) | data formatting | bytes 46137344 | tf_op jit(solution)/shard_map/kij,kip->kjp/dot_general | solution.py:12
  295.0 17.3 %fusion = f32[64,128,128]{2,0,1:T(8,128)S(1)} fusion(f32[352,128,128]{1,0,2:T(8,128)} %copy.19, f32[352]{0:T(512)S(1)} %fusion.40, s32[352]{0:T(512)S(1)} %reduce.5), kind=kOutput, calls=%fused_computation.2 | convolution fusion | flops 4429230080 | bytes 27265792 | tf_op jit(solution)/shard_map/ok,kip->oip/dot_general | solution.py:19
  312.3 4.4 copy.14
  316.7 0.0 reduce-scatter.5.cloned.1.call-update
  316.7 50.1 %reduce-scatter.5.cloned.1.call-done = f32[1024,128]{1,0:T(8,128)} async-done(((f32[8192,128]{1,0:T(8,128)}), f32[1024,128]{1,0:T(8,128)}) %reduce-scatter.5.cloned.1.call-update) | async-done | bytes 524304 | tf_op jit(solution)/shard_map/reduce_scatter | solution.py:65
  366.8 1.5 fusion.15
  368.3 16.6 %psum.30 = bf16[128,128]{0,1:T(8,128)(2,1)S(1)} all-reduce(bf16[128,128]{0,1:T(8,128)(2,1)S(1)} %fusion.15), channel_id=1, replica_groups=mesh['row'=8,'col'=4] {'col'}, use_global_device_ids=true, to_apply=%region_6.9 | all-reduce | flops 16384 | bytes 65536 | tf_op jit(solution)/shard_map/psum | solution.py:37
  384.9 26.4 %all-reduce.3 = f32[128,128]{0,1:T(8,128)S(1)} all-reduce(bf16[128,128]{0,1:T(8,128)(2,1)S(1)} %psum.30), channel_id=1, replica_groups=mesh['row'=8,'col'=4] {'row'}, use_global_device_ids=true, to_apply=%region_7.10 | all-reduce | flops 16384 | bytes 98304 | tf_op jit(solution)/shard_map/psum | solution.py:38
  411.2 0.1 copy.16
  411.4 11.7 %cholesky.55 = f32[128,128]{1,0:T(8,128)S(1)} custom-call(f32[128,128]{1,0:T(8,128)S(1)} %fusion.29), custom_call_target="Cholesky" | custom-call | tf_op jit(solution)/shard_map/jit(cholesky)/cholesky | solution.py:28
  423.1 0.6 compare_reduce_fusion
  423.8 0.7 fusion.27
  424.4 9.8 %custom-call.7 = f32[1,128,128]{1,2,0:T(8,128)S(1)} custom-call(f32[1,128,128]{2,1,0:T(8,128)S(1)} %fusion.27), custom_call_target="InvertDiagBlocksLowerTriangular" | custom-call | tf_op jit(solution)/shard_map/jit(_solve_triangular)/triangular_solve | solution.py:30
  434.2 0.3 fusion.22
  434.5 2.1 convolution_convert_fusion
  (10 shorter events, 0.2 us)
Async XLA Ops:
  7.2 34.3 %all-gather.3.cloned.1.call-start = ((), (), s32[]{:S(2)}) async-start(), calls=%async_computation.2 | async-start | bytes 2359296 | tf_op jit(solution)/shard_map/all_gather | solution.py:53
  7.9 144.2 %reduce-scatter.3.cloned.1.call-start = ((), (), s32[]{:S(2)}) async-start(), calls=%async_computation.3 | async-start | bytes 2621440 | tf_op jit(solution)/shard_map/reduce_scatter | solution.py:57
  98.9 122.3 %copy-start = (s32[1,1,352]{2,1,0:T(1,128)S(1)}, s32[1,1,352]{2,1,0:T(1,128)}, u32[]{:S(2)}) copy-start(s32[1,1,352]{2,1,0:T(1,128)} %param.10) | copy-start | bytes 4228
  117.3 127.4 %all-gather.5.cloned.1.call-start = ((), (), s32[]{:S(2)}) async-start(), calls=%async_computation.4 | async-start | bytes 1310720 | tf_op jit(solution)/shard_map/all_gather | solution.py:61
  220.9 145.9 %reduce-scatter.5.cloned.1.call-start = ((), (), s32[]{:S(2)}) async-start(), calls=%async_computation.5 | async-start | bytes 4718592 | tf_op jit(solution)/shard_map/reduce_scatter | solution.py:65
Sparse Core Ops, SparseCore 0:
  9.6 31.8 all-gather.2
  117.5 34.5 reduce-scatter.2
  221.0 23.6 all-gather.4
  316.8 49.9 reduce-scatter.4
where the time goes:
time: 452 us; the launch traced here: 444 us
  waiting for transfers between devices  140 us (31%)
  blocking collectives  84.8 us (19%)
  local copies, waits for them, and re-layouts  79 us (17%)
  matrix products  76.8 us (17%)
  other arithmetic  47.9 us (11%)
  between operations  15 us (3%)
    psum x2, blocking collectives, global_gram(): return lax.psum(within, 'row')  52.9 us
    reduce_scatter x1, waiting for transfers between devices, local(): lax.psum_scatter(right_partial, 'row', scatter_dimension=0, tiled=True)  50.1 us
    reduce_scatter x1, waiting for transfers between devices, local(): lax.psum_scatter(left_partial, 'col', scatter_dimension=0, tiled=True)  34.7 us
    dot_general x2, matrix products, tile_product(): jnp.einsum('ok,kip->oip', placement, products, precision=lax.Precision.HI...  33.2 us
    psum x2, blocking collectives, global_gram(): lax.psum(partial_value.astype(jnp.bfloat16), 'col').astype(jnp.float32)  32 us
    all_gather x1, waiting for transfers between devices, local(): column_tile = lax.all_gather(start_panel, 'row', axis=0, tiled=True)  30.8 us
    another operation x6, other arithmetic, apply_factor(): lower = jnp.linalg.cholesky(gram_total)  24.8 us
    gather x2, local copies, waits for them, and re-layouts, tile_product(): selected = jnp.take(pieces, index_in, axis=0)  24.7 us
  transfers between devices with their start and end apart: 4, of which 4 were waited for; matrix products, arithmetic and copies ran while one was open for 0% of the time, Pallas kernels for 0%

commit v1 on v0

v1 whole, which is shorter than its diff:
```python
import functools

import jax
import jax.numpy as jnp
from jax import lax
from jax.experimental import pallas as pl
from jax.experimental.pallas import tpu as pltpu
from jax.sharding import PartitionSpec as P

F32 = jnp.float32
BF16 = jnp.bfloat16
UNROLL = 8
VMEM = pl.BlockSpec(memory_space=pltpu.VMEM)
SMEM = pl.BlockSpec(memory_space=pltpu.SMEM)
ANY = pl.BlockSpec(memory_space=pl.ANY)
HIGH = lax.Precision.HIGHEST


def params():
    return pltpu.CompilerParams(vmem_limit_bytes=60 * 1024 * 1024)


def swap(value, axis, mask):
    size = lax.axis_size(axis)
    return lax.ppermute(value, axis, [(i, i ^ mask) for i in range(size)])


def chunk_of(slots):
    for size in (32, 16, 8):
        if slots % size == 0:
            return size
    return slots


def product_body(axis_size, forward, meta, out_index, in_index, values, shards, panel, vbuf, acc, sems):
    in_me, count = meta[0], meta[2]
    slots = values.shape[0]
    chunk = chunk_of(slots)
    group = min(UNROLL, chunk)
    chunks = slots // chunk
    per_shard = panel.shape[0] // axis_size
    out_blocks = acc.shape[0] - 1

    def panel_copy(k):
        slot = (in_me ^ k) * per_shard
        return pltpu.make_async_copy(shards[k], panel.at[pl.ds(slot, per_shard)], sems.at[chunks + k])

    def value_copy(c):
        span = pl.ds(c * chunk, chunk)
        return pltpu.make_async_copy(values.at[span], vbuf.at[span], sems.at[c])

    for k in range(axis_size):
        panel_copy(k).start()
    for c in range(chunks):
        value_copy(c).start()
    acc[...] = jnp.zeros_like(acc)
    for k in range(axis_size):
        panel_copy(k).wait()

    def one_group(g, carry):
        first = g * group
        products = []
        targets = []
        for u in range(group):
            k = first + u
            block = vbuf[k]
            piece = panel[in_index[k]]
            if forward:
                products.append(jnp.dot(block, piece, preferred_element_type=F32))
            else:
                products.append(jnp.dot(piece, block, preferred_element_type=F32))
            targets.append(jnp.where(k < count, out_index[k], out_blocks))
        for target, product in zip(targets, products):
            acc[target] += product
        return carry

    def one_chunk(c, carry):
        value_copy(c).wait()
        low = c * (chunk // group)
        live = (count + group - 1) // group
        high = jnp.clip(live, low, low + chunk // group)
        return lax.fori_loop(low, high, one_group, carry)

    lax.fori_loop(0, chunks, one_chunk, 0)


def left_kernel(row_size, col_size, meta, rows, cols, values, *refs):
    shards, outs, scratch = refs[:row_size], refs[row_size:-4], refs[-4:]
    panel, vbuf, acc, sems = scratch
    product_body(row_size, True, meta, rows, cols, values, shards, panel, vbuf, acc, sems)
    per = (acc.shape[0] - 1) // col_size
    me = meta[1]
    for k in range(col_size):
        part = acc[pl.ds((me ^ k) * per, per)]
        outs[k][...] = part.astype(outs[k].dtype)


def right_kernel(row_size, col_size, meta, rows, cols, values, *refs):
    shards, (keep, send), scratch = refs[:col_size], refs[col_size:-4], refs[-4:]
    panel, vbuf, acc, sems = scratch
    product_body(col_size, False, meta, cols, rows, values, shards, panel, vbuf, acc, sems)
    per = (acc.shape[0] - 1) // row_size
    me = meta[1]
    for k in range(0, row_size, 2):
        keep[k // 2] = acc[pl.ds((me ^ k) * per, per)]
        send[k // 2] = acc[pl.ds((me ^ (k + 1)) * per, per)].astype(BF16)


def run_product(kernel, meta, rows, cols, values, shards, panel_blocks, out_blocks, out_shape):
    slots, size = values.shape[0], values.shape[-1]
    width = shards[0].shape[-1]
    chunks = slots // chunk_of(slots)
    return pl.pallas_call(
        kernel,
        out_shape=out_shape,
        in_specs=[SMEM, SMEM, SMEM, ANY] + [ANY] * len(shards),
        out_specs=jax.tree.map(lambda _: VMEM, out_shape),
        scratch_shapes=[
            pltpu.VMEM((panel_blocks, size, width), BF16),
            pltpu.VMEM(values.shape, BF16),
            pltpu.VMEM((out_blocks + 1, size, width), F32),
            pltpu.SemaphoreType.DMA((chunks + len(shards),)),
        ],
        compiler_params=params(),
        cost_estimate=pl.CostEstimate(
            flops=2 * slots * size * size * width, bytes_accessed=2 * values.size, transcendentals=0
        ),
    )(meta, rows, cols, values, *shards)


def left_sum_kernel(nodes_total, own, *refs):
    parts, (natural, flipped, gram) = refs[:-3], refs[-3:]
    total = jnp.zeros(gram.shape, F32)
    for b in range(own.shape[0]):
        summed = own[b]
        for part in parts:
            summed = summed + part[b].astype(F32)
        rounded = summed.astype(BF16)
        turned = summed.T.astype(BF16)
        natural[b] = rounded
        flipped[b] = turned
        total = total + jnp.dot(turned, rounded, preferred_element_type=F32)
    gram[...] = total / nodes_total


def core_sum_kernel(keep, came, *outs):
    for k, out in enumerate(outs):
        out[...] = (keep[k] + came[k].astype(F32)).astype(out.dtype)


def right_sum_kernel(nodes_total, inverse, own, *refs):
    parts, (flipped, gram) = refs[:-2], refs[-2:]
    factor = inverse[...]
    total = jnp.zeros(gram.shape, F32)
    for b in range(own.shape[0]):
        summed = own[b]
        for part in parts:
            summed = summed + part[b].astype(F32)
        scaled = jnp.dot(factor, summed, precision=HIGH, preferred_element_type=F32)
        rounded = scaled.astype(BF16)
        flipped[b] = rounded
        total = total + lax.dot_general(rounded, rounded, (((1,), (1,)), ((), ())), preferred_element_type=F32)
    gram[...] = total / nodes_total


def left_apply_kernel(inverse, natural, out):
    factor = inverse[...]
    for b in range(natural.shape[0]):
        solved = lax.dot_general(
            natural[b].astype(F32), factor, (((1,), (1,)), ((), ())), precision=HIGH, preferred_element_type=F32
        )
        out[b] = solved.astype(BF16)


def right_apply_kernel(inverse, flipped, out):
    factor = inverse[...]
    for b in range(flipped.shape[0]):
        solved = jnp.dot(factor, flipped[b].astype(F32), precision=HIGH, preferred_element_type=F32)
        out[b] = solved.T.astype(BF16)


def call(kernel, out_shape, *args):
    return pl.pallas_call(
        kernel,
        out_shape=out_shape,
        in_specs=[VMEM] * len(args),
        out_specs=jax.tree.map(lambda _: VMEM, out_shape),
        compiler_params=params(),
    )(*args)


def shape(dims, kind):
    return jax.ShapeDtypeStruct(dims, kind)


def inverse_factor(gram_total):
    lower = jnp.linalg.cholesky(gram_total)
    identity = jnp.eye(gram_total.shape[0], dtype=F32)
    return jax.scipy.linalg.solve_triangular(lower, identity, lower=True)


def total_gram(gram):
    row_size = lax.axis_size("row")
    col_size = lax.axis_size("col")
    gram = gram + swap(gram, "row", 1)
    came = [swap(gram, "col", k) for k in range(1, col_size)]
    gram = functools.reduce(jnp.add, came, gram)
    came = [swap(gram, "row", k) for k in range(2, row_size, 2)]
    return functools.reduce(jnp.add, came, gram)


def gather_row(shard):
    row_size = lax.axis_size("row")
    have = {0: shard}
    bit = row_size // 2
    while bit:
        for k in sorted(have):
            have[k | bit] = swap(have[k], "row", bit)
        bit //= 2
    return [have[k] for k in range(row_size)]


def local(start_panel, block_values, block_rows, block_cols, block_counts):
    group_rows, width = start_panel.shape
    row_size = lax.axis_size("row")
    col_size = lax.axis_size("col")
    nodes_total = group_rows * row_size * col_size
    values = block_values[0, 0]
    rows, cols = block_rows[0, 0], block_cols[0, 0]
    count = block_counts[0, 0]
    size = values.shape[-1]
    per = group_rows // size
    row_blocks, col_blocks = per * col_size, per * row_size
    row_me = lax.axis_index("row").astype(jnp.int32)
    col_me = lax.axis_index("col").astype(jnp.int32)
    block = (per, size, width)
    square = shape((width, width), F32)

    shards = gather_row(start_panel.reshape(block))
    parts = run_product(
        functools.partial(left_kernel, row_size, col_size),
        jnp.stack([row_me, col_me, count]), rows, cols, values, shards, col_blocks, row_blocks,
        [shape(block, F32)] + [shape(block, BF16)] * (col_size - 1),
    )
    came = [swap(parts[k], "col", k) for k in range(1, col_size)]
    natural, flipped, gram = call(
        functools.partial(left_sum_kernel, nodes_total),
        (shape(block, BF16), shape(block, BF16), square), parts[0], *came,
    )
    turned = [flipped] + [swap(flipped, "col", k) for k in range(1, col_size)]
    inverse = inverse_factor(total_gram(gram))
    left_panel = call(left_apply_kernel, shape(block, BF16), inverse, natural)

    half = (row_size // 2,) + block
    keep, send = run_product(
        functools.partial(right_kernel, row_size, col_size),
        jnp.stack([col_me, row_me, count]), rows, cols, values, turned, row_blocks, col_blocks,
        [shape(half, F32), shape(half, BF16)],
    )
    sums = call(
        core_sum_kernel, [shape(block, F32)] + [shape(block, BF16)] * (row_size // 2 - 1),
        keep, swap(send, "row", 1),
    )
    came = [swap(sums[k // 2], "row", k) for k in range(2, row_size, 2)]
    right_flipped, gram = call(
        functools.partial(right_sum_kernel, nodes_total), (shape(block, BF16), square), inverse, sums[0], *came
    )
    inverse = inverse_factor(total_gram(gram))
    right_panel = call(right_apply_kernel, shape(block, BF16), inverse, right_flipped)
    return (left_panel.reshape(group_rows, width), right_panel.reshape(group_rows, width))


def solution(mesh):
    return jax.shard_map(
        local,
        mesh=mesh,
        in_specs=(
            P(("col", "row"), None),
            P("row", "col", None, None, None),
            P("row", "col", None),
            P("row", "col", None),
            P("row", "col"),
        ),
        out_specs=(P(("row", "col"), None), P(("col", "row"), None)),
        check_vma=False,
    )
```

time: 452 us -> 192 us (0.42); the launches traced: 444 us -> 191 us
  waiting for transfers between devices: 140 us -> 52.9 us
  blocking collectives: 84.8 us -> 0 us
  matrix products: 76.8 us -> 1.81 us
  local copies, waits for them, and re-layouts: 79 us -> 6.8 us
  starting transfers between devices: 0.37 us -> 44 us
  Pallas kernels: 0 us -> 34.5 us
  between operations: 15 us -> 1.54 us
    psum x4 -> x0, blocking collectives: 84.8 us -> none  [the longest x2 52.9 us: global_gram(): return lax.psum(within, 'row')]
    reduce_scatter x2 -> x0, waiting for transfers between devices: 84.8 us -> none  [the longest x1 50.1 us: local(): lax.psum_scatter(right_partial, 'row', scatter_dimension=0, tiled=True)]
    dot_general x8 -> x0, matrix products: 76.2 us -> none  [the longest x2 33.2 us: tile_product(): jnp.einsum('ok,kip->oip', placement, products, precision=lax.Precision.HI...]
    all_gather x2 -> x0, waiting for transfers between devices: 54.2 us -> none  [the longest x1 30.8 us: local(): column_tile = lax.all_gather(start_panel, 'row', axis=0, tiled=True)]
    dot_general x4 -> x0, local copies, waits for them, and re-layouts: 54.1 us -> none  [the longest x1 23.6 us: tile_product(): jnp.einsum('kij,kjp->kip', values, selected, preferred_element_type=jnp.f...]
    ppermute x0 -> x31, waiting for transfers between devices: none -> 52.9 us  [swap(): return lax.ppermute(value, axis, [(i, i ^ mask) for i in range(size)])]
    ppermute x0 -> x31, starting transfers between devices: none -> 44 us  [swap(): return lax.ppermute(value, axis, [(i, i ^ mask) for i in range(size)])]
    pallas_call x0 -> x7, Pallas kernels: none -> 34.5 us  [the longest x2 20.9 us: run_product(): pl.pallas_call(kernel, out_shape=out_shape, in_specs=[SMEM, SMEM, SMEM, A...]
  transfers between devices with their start and end apart: 4 -> 31, of which waited for: 4 -> 17; matrix products, arithmetic and copies ran while one was open for 0% -> 15% of each run, Pallas kernels for 0% -> 7%
where the time goes in v1:
time: 192 us; the launch traced here: 191 us
  waiting for transfers between devices  52.9 us (28%)
  other arithmetic  49.8 us (26%)
  starting transfers between devices  44 us (23%)
  Pallas kernels  34.5 us (18%)
  local copies, waits for them, and re-layouts  6.8 us (4%)
    ppermute x31, waiting for transfers between devices, swap(): return lax.ppermute(value, axis, [(i, i ^ mask) for i in range(size)])  52.9 us
    ppermute x31, starting transfers between devices, swap(): return lax.ppermute(value, axis, [(i, i ^ mask) for i in range(size)])  44 us
    another operation x6, other arithmetic, inverse_factor(): lower = jnp.linalg.cholesky(gram_total)  25 us
    another operation x4, other arithmetic, inverse_factor(): return jax.scipy.linalg.solve_triangular(lower, identity, lower=True)  20.9 us
    pallas_call x2, Pallas kernels, run_product(): pl.pallas_call(kernel, out_shape=out_shape, in_specs=[SMEM, SMEM, SMEM, A...  20.9 us
    pallas_call x5, Pallas kernels, call(): pl.pallas_call(kernel, out_shape=out_shape, in_specs=[VMEM] * len(args),...  13.6 us
    unnamed x34, local copies, waits for them, and re-layouts  4.77 us
  transfers between devices with their start and end apart: 31, of which 17 were waited for; matrix products, arithmetic and copies ran while one was open for 15% of the time, Pallas kernels for 7%

profile of v1, /device:TPU:0, one launch (start us, length us, event | category | flops | bytes accessed | tf_op | source)
XLA Modules:
  0.0 191.4 jit_solution(5043933493322051259)
XLA Ops:
  0.6 4.1 %collective-permute-start.3 = (bf16[8,128,128]{2,1,0:T(8,128)(2,1)}, bf16[8,128,128]{2,1,0:T(8,128)(2,1)S(1)}, u32[]{:S(2)}, u32[]{:S(2)}) collective-permute-start(bf16[8,128,128]{2,1,0:T(8,128)(2,1)} %bitcast.29), channel_id=1, source_target_pairs={{0,16},{4,20},{8,24},{12,28},{16,0},{20,4},{24,8},{28,12},{1,17},{... | collective-permute-start | bytes 786440 | tf_op jit(solution)/shard_map/ppermute | solution.py:25
  4.8 1.6 collective-permute-start.1
  6.3 10.7 %collective-permute-done.3.refs_4_ = bf16[8,128,128]{2,1,0:T(8,128)(2,1)S(1)} collective-permute-done((bf16[8,128,128]{2,1,0:T(8,128)(2,1)}, bf16[8,128,128]{2,1,0:T(8,128)(2,1)S(1)}, u32[]{:S(2)}, u32[]{:S(2)}) %collective-permute-start.3) | collective-permute-done | bytes 262176 | tf_op jit(solution)/shard_map/ppermute | solution.py:25
  17.0 0.7 collective-permute-start.5
  18.3 6.1 %collective-permute-done.5.refs_6_ = bf16[8,128,128]{2,1,0:T(8,128)(2,1)S(1)} collective-permute-done((bf16[8,128,128]{2,1,0:T(8,128)(2,1)S(1)}, bf16[8,128,128]{2,1,0:T(8,128)(2,1)S(1)}, u32[]{:S(2)}, u32[]{:S(2)}) %collective-permute-start.5) | collective-permute-done | bytes 262176 | tf_op jit(solution)/shard_map/ppermute | solution.py:25
  25.1 1.3 reduce.4.rows
  26.3 1.3 reduce.5.cols
  27.6 0.6 add_add_fusion.4.meta
  28.3 0.6 copy-done.4
  29.2 10.2 %shard_map.68 = (f32[8,128,128]{2,1,0:T(8,128)}, bf16[8,128,128]{2,1,0:T(8,128)(2,1)}, bf16[8,128,128]{2,1,0:T(8,128)(2,1)}, bf16[8,128,128]{2,1,0:T(8,128)(2,1)}) custom-call(s32[3]{0:T(128)} %add_add_fusion.4.meta, s32[352]{0:T(512)} %reduce.4.rows, s32[352]{0:T(512)} %reduce.5.cols, bf16[352,128,128]{2,1,0:T(8,128)(2,1)} %bitcast.27, ...), custom_call_target="tpu_custom_call" | custom-call | flops 1476395008 | bytes 11534336 | tf_op jit(solution)/shard_map/pallas_call | solution.py:113
  39.4 1.1 collective-permute-start.7
  40.6 4.3 %collective-permute-start.8 = (bf16[8,128,128]{2,1,0:T(8,128)(2,1)}, bf16[8,128,128]{2,1,0:T(8,128)(2,1)S(1)}, u32[]{:S(2)}, u32[]{:S(2)}) collective-permute-start(bf16[8,128,128]{2,1,0:T(8,128)(2,1)} %get-tuple-element.21), channel_id=1, source_target_pairs={{0,2},{1,3},{2,0},{3,1},{4,6},{5,7},{6,4},{7,5},{8,10},{9,11},{10,... | collective-permute-start | bytes 786440 | tf_op jit(solution)/shard_map/ppermute | solution.py:25
  44.9 0.9 collective-permute-start.9
  46.1 10.2 %collective-permute-done.8.refs_1_ = bf16[8,128,128]{2,1,0:T(8,128)(2,1)S(1)} collective-permute-done((bf16[8,128,128]{2,1,0:T(8,128)(2,1)}, bf16[8,128,128]{2,1,0:T(8,128)(2,1)S(1)}, u32[]{:S(2)}, u32[]{:S(2)}) %collective-permute-start.8) | collective-permute-done | bytes 262176 | tf_op jit(solution)/shard_map/ppermute | solution.py:25
  56.3 1.5 collective-permute-done.9.refs_2_
  57.7 0.7 copy-done.13
  58.4 2.2 %shard_map.69 = (bf16[8,128,128]{2,1,0:T(8,128)(2,1)}, bf16[8,128,128]{2,1,0:T(8,128)(2,1)}, f32[128,128]{1,0:T(8,128)}) custom-call(f32[8,128,128]{2,1,0:T(8,128)} %get-tuple-element.19.own, bf16[8,128,128]{2,1,0:T(8,128)(2,1)} %copy-done.11, bf16[8,128,128]{2,1,0:T(8,128)(2,1)} %copy-done.12, bf16[8,128,128]{2,1,0:T(8,128)(2,1)} %copy-done.13), custom_call_target="tpu_custom_call" | custom-call | tf_op jit(solution)/shard_map/pallas_call | solution.py:183
  60.7 2.1 %collective-permute-start.19 = (bf16[8,128,128]{2,1,0:T(8,128)(2,1)}, bf16[8,128,128]{2,1,0:T(8,128)(2,1)S(1)}, u32[]{:S(2)}, u32[]{:S(2)}) collective-permute-start(bf16[8,128,128]{2,1,0:T(8,128)(2,1)} %get-tuple-element.25.refs_0_), channel_id=1, source_target_pairs={{0,3},{1,2},{2,1},{3,0},{4,7},{5,6},{6,5},{7,4},{8,11},{9,10},{10,... | collective-permute-start | bytes 786440 | tf_op jit(solution)/shard_map/ppermute | solution.py:25
  63.2 1.0 collective-permute-start.17
  64.1 0.9 copy.8
  65.2 0.7 add_add_fusion.5.meta
  65.8 0.6 collective-permute-done.10
  66.4 2.2 %collective-permute-start.13 = (f32[128,128]{0,1:T(8,128)S(1)}, f32[128,128]{0,1:T(8,128)S(1)}, u32[]{:S(2)}, u32[]{:S(2)}) collective-permute-start(f32[128,128]{0,1:T(8,128)S(1)} %add.51), channel_id=1, source_target_pairs={{0,3},{1,2},{2,1},{3,0},{4,7},{5,6},{6,5},{7,4},{8,11},{9,10},{10,... | collective-permute-start | bytes 196616 | tf_op jit(solution)/shard_map/ppermute | solution.py:25
  69.0 2.0 %collective-permute-done.19.refs_3_ = bf16[8,128,128]{2,1,0:T(8,128)(2,1)S(1)} collective-permute-done((bf16[8,128,128]{2,1,0:T(8,128)(2,1)}, bf16[8,128,128]{2,1,0:T(8,128)(2,1)S(1)}, u32[]{:S(2)}, u32[]{:S(2)}) %collective-permute-start.19) | collective-permute-done | bytes 262176 | tf_op jit(solution)/shard_map/ppermute | solution.py:25
  71.0 1.0 collective-permute-start.11
  72.0 4.5 %collective-permute-done.18.refs_2_ = bf16[8,128,128]{2,1,0:T(8,128)(2,1)S(1)} collective-permute-done((bf16[8,128,128]{2,1,0:T(8,128)(2,1)}, bf16[8,128,128]{2,1,0:T(8,128)(2,1)S(1)}, u32[]{:S(2)}, u32[]{:S(2)}) %collective-permute-start.18) | collective-permute-done | bytes 262176 | tf_op jit(solution)/shard_map/ppermute | solution.py:25
  76.6 0.7 copy-done.7
  77.2 0.7 copy-done.9
  77.9 10.6 %shard_map.71 = (f32[4,8,128,128]{3,2,1,0:T(8,128)}, bf16[4,8,128,128]{3,2,1,0:T(8,128)(2,1)}) custom-call(s32[3]{0:T(128)} %add_add_fusion.5.meta, s32[352]{0:T(512)} %reduce.4.rows, s32[352]{0:T(512)} %reduce.5.cols, bf16[352,128,128]{2,1,0:T(8,128)(2,1)} %bitcast.28, bf16[8,128,128]{2,1,0:T(8,128)(2,1)} %get-tuple-element.25.refs_0_, ...), custom_call_target="tpu_custom_call" | custom-call | flops 1476395008 | bytes 11534336 | tf_op jit(solution)/shard_map/pallas_call | solution.py:113
  88.6 3.9 %collective-permute-start.20 = (bf16[4,8,128,128]{3,2,1,0:T(8,128)(2,1)}, bf16[4,8,128,128]{3,2,1,0:T(8,128)(2,1)S(1)}, u32[]{:S(2)}, u32[]{:S(2)}) collective-permute-start(bf16[4,8,128,128]{3,2,1,0:T(8,128)(2,1)} %get-tuple-element.27), channel_id=1, source_target_pairs={{0,4},{4,0},{8,12},{12,8},{16,20},{20,16},{24,28},{28,24},{1,5},{5... | collective-permute-start | bytes 3145736 | tf_op jit(solution)/shard_map/ppermute | solution.py:25
  92.5 2.4 %collective-permute-start.16 = (f32[128,128]{0,1:T(8,128)S(1)}, f32[128,128]{0,1:T(8,128)S(1)}, u32[]{:S(2)}, u32[]{:S(2)}) collective-permute-start(f32[128,128]{0,1:T(8,128)S(1)} %add_add_fusion.3), channel_id=1, source_target_pairs={{0,24},{4,28},{8,16},{12,20},{16,8},{20,12},{24,0},{28,4},{1,25},{... | collective-permute-start | bytes 196616 | tf_op jit(solution)/shard_map/ppermute | solution.py:25
  95.1 1.9 collective-permute-start.14
  97.0 2.2 %collective-permute-done.16 = f32[128,128]{0,1:T(8,128)S(1)} collective-permute-done((f32[128,128]{0,1:T(8,128)S(1)}, f32[128,128]{0,1:T(8,128)S(1)}, u32[]{:S(2)}, u32[]{:S(2)}) %collective-permute-start.16) | collective-permute-done | bytes 65568 | tf_op jit(solution)/shard_map/ppermute | solution.py:25
  99.2 2.3 %collective-permute-done.15 = f32[128,128]{0,1:T(8,128)S(1)} collective-permute-done((f32[128,128]{0,1:T(8,128)S(1)}, f32[128,128]{0,1:T(8,128)S(1)}, u32[]{:S(2)}, u32[]{:S(2)}) %collective-permute-start.15) | collective-permute-done | bytes 65568 | tf_op jit(solution)/shard_map/ppermute | solution.py:25
  101.7 11.7 %cholesky.44 = f32[128,128]{1,0:T(8,128)S(1)} custom-call(f32[128,128]{1,0:T(8,128)S(1)} %fusion.9), custom_call_target="Cholesky" | custom-call | tf_op jit(solution)/shard_map/jit(cholesky)/cholesky | solution.py:197
  113.4 0.7 compare_reduce_fusion.1
  114.1 1.0 copy-done
  115.1 3.0 %shard_map.72 = (f32[8,128,128]{2,1,0:T(8,128)}, bf16[8,128,128]{2,1,0:T(8,128)(2,1)}, bf16[8,128,128]{2,1,0:T(8,128)(2,1)}, bf16[8,128,128]{2,1,0:T(8,128)(2,1)}) custom-call(f32[4,8,128,128]{3,2,1,0:T(8,128)} %get-tuple-element.26.keep, bf16[4,8,128,128]{3,2,1,0:T(8,128)(2,1)} %copy-done), custom_call_target="tpu_custom_call" | custom-call | tf_op jit(solution)/shard_map/pallas_call | solution.py:183
  118.5 2.3 %collective-permute-start.22 = (bf16[8,128,128]{2,1,0:T(8,128)(2,1)}, bf16[8,128,128]{2,1,0:T(8,128)(2,1)S(1)}, u32[]{:S(2)}, u32[]{:S(2)}) collective-permute-start(bf16[8,128,128]{2,1,0:T(8,128)(2,1)} %get-tuple-element.30), channel_id=1, source_target_pairs={{0,16},{4,20},{8,24},{12,28},{16,0},{20,4},{24,8},{28,12},{1,17},{... | collective-permute-start | bytes 786440 | tf_op jit(solution)/shard_map/ppermute | solution.py:25
  120.9 1.6 collective-permute-start.23
  122.5 0.6 fusion.4
  123.1 9.8 %custom-call.6 = f32[1,128,128]{1,2,0:T(8,128)S(1)} custom-call(f32[1,128,128]{2,1,0:T(8,128)S(1)} %fusion.4), custom_call_target="InvertDiagBlocksLowerTriangular" | custom-call | tf_op jit(solution)/shard_map/jit(_solve_triangular)/triangular_solve | solution.py:199
  132.9 0.9 fusion.2.inverse
  133.8 6.2 %collective-permute-done.22.refs_1_ = bf16[8,128,128]{2,1,0:T(8,128)(2,1)S(1)} collective-permute-done((bf16[8,128,128]{2,1,0:T(8,128)(2,1)}, bf16[8,128,128]{2,1,0:T(8,128)(2,1)S(1)}, u32[]{:S(2)}, u32[]{:S(2)}) %collective-permute-start.22) | collective-permute-done | bytes 262176 | tf_op jit(solution)/shard_map/ppermute | solution.py:25
  140.1 0.7 copy-done.15
  140.8 3.2 %shard_map.73 = (bf16[8,128,128]{2,1,0:T(8,128)(2,1)}, f32[128,128]{1,0:T(8,128)}) custom-call(f32[128,128]{1,0:T(8,128)} %fusion.2.inverse, f32[8,128,128]{2,1,0:T(8,128)} %get-tuple-element.28.own, bf16[8,128,128]{2,1,0:T(8,128)(2,1)} %copy-done.14, bf16[8,128,128]{2,1,0:T(8,128)(2,1)} %copy-done.15, bf16[8,128,128]{2,1,0:T(8,128)(2,1)} %copy-done.16), custom_call_target="tpu_custom_call" | custom-call | tf_op jit(solution)/shard_map/pallas_call | solution.py:183
  144.0 0.9 copy.11
  145.0 1.2 collective-permute-done.24
  146.3 2.2 %collective-permute-start.27 = (f32[128,128]{0,1:T(8,128)S(1)}, f32[128,128]{0,1:T(8,128)S(1)}, u32[]{:S(2)}, u32[]{:S(2)}) collective-permute-start(f32[128,128]{0,1:T(8,128)S(1)} %add.58), channel_id=1, source_target_pairs={{0,3},{1,2},{2,1},{3,0},{4,7},{5,6},{6,5},{7,4},{8,11},{9,10},{10,... | collective-permute-start | bytes 196616 | tf_op jit(solution)/shard_map/ppermute | solution.py:25
  148.5 1.5 collective-permute-start.26
  150.5 1.0 collective-permute-done.27
  151.6 1.3 collective-permute-done.26
  152.9 1.4 collective-permute-done.25
  154.3 2.1 %collective-permute-start.30 = (f32[128,128]{0,1:T(8,128)S(1)}, f32[128,128]{0,1:T(8,128)S(1)}, u32[]{:S(2)}, u32[]{:S(2)}) collective-permute-start(f32[128,128]{0,1:T(8,128)S(1)} %add_add_fusion.1), channel_id=1, source_target_pairs={{0,24},{4,28},{8,16},{12,20},{16,8},{20,12},{24,0},{28,4},{1,25},{... | collective-permute-start | bytes 196616 | tf_op jit(solution)/shard_map/ppermute | solution.py:25
  156.4 4.3 %collective-permute-start.29 = (f32[128,128]{0,1:T(8,128)S(1)}, f32[128,128]{0,1:T(8,128)S(1)}, u32[]{:S(2)}, u32[]{:S(2)}) collective-permute-start(f32[128,128]{0,1:T(8,128)S(1)} %add_add_fusion.1), channel_id=1, source_target_pairs={{0,16},{4,20},{8,24},{12,28},{16,0},{20,4},{24,8},{28,12},{1,17},{... | collective-permute-start | bytes 196616 | tf_op jit(solution)/shard_map/ppermute | solution.py:25
  160.7 2.9 %shard_map.70 = bf16[8,128,128]{2,1,0:T(8,128)(2,1)} custom-call(f32[128,128]{1,0:T(8,128)} %fusion.2.inverse, bf16[8,128,128]{2,1,0:T(8,128)(2,1)} %get-tuple-element.24.natural), custom_call_target="tpu_custom_call" | custom-call | tf_op jit(solution)/shard_map/pallas_call | solution.py:183
  163.6 0.6 collective-permute-done.29
  164.2 0.8 collective-permute-done.28
  165.1 11.9 %cholesky.55 = f32[128,128]{1,0:T(8,128)S(1)} custom-call(f32[128,128]{1,0:T(8,128)S(1)} %fusion.7), custom_call_target="Cholesky" | custom-call | tf_op jit(solution)/shard_map/jit(cholesky)/cholesky | solution.py:197
  177.0 0.6 compare_reduce_fusion
  177.7 0.7 fusion.5
  178.3 9.8 %custom-call.7 = f32[1,128,128]{1,2,0:T(8,128)S(1)} custom-call(f32[1,128,128]{2,1,0:T(8,128)S(1)} %fusion.5), custom_call_target="InvertDiagBlocksLowerTriangular" | custom-call | tf_op jit(solution)/shard_map/jit(_solve_triangular)/triangular_solve | solution.py:199
  188.1 0.9 fusion.inverse
  189.0 2.4 %shard_map.74 = bf16[8,128,128]{2,1,0:T(8,128)(2,1)} custom-call(f32[128,128]{1,0:T(8,128)} %fusion.inverse, bf16[8,128,128]{2,1,0:T(8,128)(2,1)} %get-tuple-element.33.flipped), custom_call_target="tpu_custom_call" | custom-call | tf_op jit(solution)/shard_map/pallas_call | solution.py:183
  (67 shorter events, 3.8 us)
Async XLA Ops:
  0.6 16.4 %collective-permute-start.3 = (bf16[8,128,128]{2,1,0:T(8,128)(2,1)}, bf16[8,128,128]{2,1,0:T(8,128)(2,1)S(1)}, u32[]{:S(2)}, u32[]{:S(2)}) collective-permute-start(bf16[8,128,128]{2,1,0:T(8,128)(2,1)} %bitcast.29), channel_id=1, source_target_pairs={{0,16},{4,20},{8,24},{12,28},{16,0},{20,4},{24,8},{28,12},{1,17},{... | collective-permute-start | bytes 786440 | tf_op jit(solution)/shard_map/ppermute | solution.py:25
  4.8 13.5 %collective-permute-start.1 = (bf16[8,128,128]{2,1,0:T(8,128)(2,1)}, bf16[8,128,128]{2,1,0:T(8,128)(2,1)S(1)}, u32[]{:S(2)}, u32[]{:S(2)}) collective-permute-start(bf16[8,128,128]{2,1,0:T(8,128)(2,1)} %bitcast.30), channel_id=1, source_target_pairs={{0,8},{4,12},{8,0},{12,4},{16,24},{20,28},{24,16},{28,20},{1,9},{5... | collective-permute-start | bytes 786440 | tf_op jit(solution)/shard_map/ppermute | solution.py:25
  17.0 11.3 %copy-start.1 = (bf16[8,128,128]{2,1,0:T(8,128)(2,1)}, bf16[8,128,128]{2,1,0:T(8,128)(2,1)S(1)}, u32[]{:S(2)}) copy-start(bf16[8,128,128]{2,1,0:T(8,128)(2,1)S(1)} %collective-permute-done.3.refs_4_) | copy-start | bytes 786436
  17.0 7.4 %collective-permute-start.5 = (bf16[8,128,128]{2,1,0:T(8,128)(2,1)S(1)}, bf16[8,128,128]{2,1,0:T(8,128)(2,1)S(1)}, u32[]{:S(2)}, u32[]{:S(2)}) collective-permute-start(bf16[8,128,128]{2,1,0:T(8,128)(2,1)S(1)} %collective-permute-done.3.refs_4_), channel_id=1, source_target_pairs={{0,8},{4,12},{8,0},{12,4},{16,24},{20,28},{24,16},{28,20},{1,9},{5... | collective-permute-start | bytes 786440 | tf_op jit(solution)/shard_map/ppermute | solution.py:25
  17.7 10.5 %collective-permute-start = (bf16[8,128,128]{2,1,0:T(8,128)(2,1)}, bf16[8,128,128]{2,1,0:T(8,128)(2,1)S(1)}, u32[]{:S(2)}, u32[]{:S(2)}) collective-permute-start(bf16[8,128,128]{2,1,0:T(8,128)(2,1)} %bitcast.31), channel_id=1, source_target_pairs={{0,4},{4,0},{8,12},{12,8},{16,20},{20,16},{24,28},{28,24},{1,5},{5... | collective-permute-start | bytes 786440 | tf_op jit(solution)/shard_map/ppermute | solution.py:25
  17.7 10.5 %collective-permute-start.4 = (bf16[8,128,128]{2,1,0:T(8,128)(2,1)S(1)}, bf16[8,128,128]{2,1,0:T(8,128)(2,1)S(1)}, u32[]{:S(2)}, u32[]{:S(2)}) collective-permute-start(bf16[8,128,128]{2,1,0:T(8,128)(2,1)S(1)} %collective-permute-done.3.refs_4_), channel_id=1, source_target_pairs={{0,4},{4,0},{8,12},{12,8},{16,20},{20,16},{24,28},{28,24},{1,5},{5... | collective-permute-start | bytes 786440 | tf_op jit(solution)/shard_map/ppermute | solution.py:25
  18.2 10.0 %copy-start.2 = (bf16[8,128,128]{2,1,0:T(8,128)(2,1)}, bf16[8,128,128]{2,1,0:T(8,128)(2,1)S(1)}, u32[]{:S(2)}) copy-start(bf16[8,128,128]{2,1,0:T(8,128)(2,1)S(1)} %collective-permute-done.1.refs_2_) | copy-start | bytes 786436
  18.2 10.0 %collective-permute-start.2 = (bf16[8,128,128]{2,1,0:T(8,128)(2,1)S(1)}, bf16[8,128,128]{2,1,0:T(8,128)(2,1)S(1)}, u32[]{:S(2)}, u32[]{:S(2)}) collective-permute-start(bf16[8,128,128]{2,1,0:T(8,128)(2,1)S(1)} %collective-permute-done.1.refs_2_), channel_id=1, source_target_pairs={{0,4},{4,0},{8,12},{12,8},{16,20},{20,16},{24,28},{28,24},{1,5},{5... | collective-permute-start | bytes 786440 | tf_op jit(solution)/shard_map/ppermute | solution.py:25
  24.4 3.9 %copy-start.3 = (bf16[8,128,128]{2,1,0:T(8,128)(2,1)}, bf16[8,128,128]{2,1,0:T(8,128)(2,1)S(1)}, u32[]{:S(2)}) copy-start(bf16[8,128,128]{2,1,0:T(8,128)(2,1)S(1)} %collective-permute-done.5.refs_6_) | copy-start | bytes 786436
  24.4 3.8 %collective-permute-start.6 = (bf16[8,128,128]{2,1,0:T(8,128)(2,1)S(1)}, bf16[8,128,128]{2,1,0:T(8,128)(2,1)S(1)}, u32[]{:S(2)}, u32[]{:S(2)}) collective-permute-start(bf16[8,128,128]{2,1,0:T(8,128)(2,1)S(1)} %collective-permute-done.5.refs_6_), channel_id=1, source_target_pairs={{0,4},{4,0},{8,12},{12,8},{16,20},{20,16},{24,28},{28,24},{1,5},{5... | collective-permute-start | bytes 786440 | tf_op jit(solution)/shard_map/ppermute | solution.py:25
  28.2 0.7 copy-start.4
  28.2 0.8 copy-start.5
  28.2 0.8 copy-start.8
  28.3 0.9 copy-start.10
  39.4 6.6 %collective-permute-start.7 = (bf16[8,128,128]{2,1,0:T(8,128)(2,1)}, bf16[8,128,128]{2,1,0:T(8,128)(2,1)S(1)}, u32[]{:S(2)}, u32[]{:S(2)}) collective-permute-start(bf16[8,128,128]{2,1,0:T(8,128)(2,1)} %get-tuple-element.20), channel_id=1, source_target_pairs={{0,1},{1,0},{2,3},{3,2},{4,5},{5,4},{6,7},{7,6},{8,9},{9,8},{10,11... | collective-permute-start | bytes 786440 | tf_op jit(solution)/shard_map/ppermute | solution.py:25
  40.6 15.7 %collective-permute-start.8 = (bf16[8,128,128]{2,1,0:T(8,128)(2,1)}, bf16[8,128,128]{2,1,0:T(8,128)(2,1)S(1)}, u32[]{:S(2)}, u32[]{:S(2)}) collective-permute-start(bf16[8,128,128]{2,1,0:T(8,128)(2,1)} %get-tuple-element.21), channel_id=1, source_target_pairs={{0,2},{1,3},{2,0},{3,1},{4,6},{5,7},{6,4},{7,5},{8,10},{9,11},{10,... | collective-permute-start | bytes 786440 | tf_op jit(solution)/shard_map/ppermute | solution.py:25
  44.9 12.8 %collective-permute-start.9 = (bf16[8,128,128]{2,1,0:T(8,128)(2,1)}, bf16[8,128,128]{2,1,0:T(8,128)(2,1)S(1)}, u32[]{:S(2)}, u32[]{:S(2)}) collective-permute-start(bf16[8,128,128]{2,1,0:T(8,128)(2,1)} %get-tuple-element.22), channel_id=1, source_target_pairs={{0,3},{1,2},{2,1},{3,0},{4,7},{5,6},{6,5},{7,4},{8,11},{9,10},{10,... | collective-permute-start | bytes 786440 | tf_op jit(solution)/shard_map/ppermute | solution.py:25
  46.1 11.6 %copy-start.11 = (bf16[8,128,128]{2,1,0:T(8,128)(2,1)}, bf16[8,128,128]{2,1,0:T(8,128)(2,1)S(1)}, u32[]{:S(2)}) copy-start(bf16[8,128,128]{2,1,0:T(8,128)(2,1)S(1)} %collective-permute-done.7.refs_0_) | copy-start | bytes 786436
  56.3 1.5 copy-start.12
  57.7 0.7 copy-start.13
  60.7 10.3 %collective-permute-start.19 = (bf16[8,128,128]{2,1,0:T(8,128)(2,1)}, bf16[8,128,128]{2,1,0:T(8,128)(2,1)S(1)}, u32[]{:S(2)}, u32[]{:S(2)}) collective-permute-start(bf16[8,128,128]{2,1,0:T(8,128)(2,1)} %get-tuple-element.25.refs_0_), channel_id=1, source_target_pairs={{0,3},{1,2},{2,1},{3,0},{4,7},{5,6},{6,5},{7,4},{8,11},{9,10},{10,... | collective-permute-start | bytes 786440 | tf_op jit(solution)/shard_map/ppermute | solution.py:25
  62.8 13.8 %collective-permute-start.18 = (bf16[8,128,128]{2,1,0:T(8,128)(2,1)}, bf16[8,128,128]{2,1,0:T(8,128)(2,1)S(1)}, u32[]{:S(2)}, u32[]{:S(2)}) collective-permute-start(bf16[8,128,128]{2,1,0:T(8,128)(2,1)} %get-tuple-element.25.refs_0_), channel_id=1, source_target_pairs={{0,2},{1,3},{2,0},{3,1},{4,6},{5,7},{6,4},{7,5},{8,10},{9,11},{10,... | collective-permute-start | bytes 786440 | tf_op jit(solution)/shard_map/ppermute | solution.py:25
  63.2 13.4 %collective-permute-start.17 = (bf16[8,128,128]{2,1,0:T(8,128)(2,1)}, bf16[8,128,128]{2,1,0:T(8,128)(2,1)S(1)}, u32[]{:S(2)}, u32[]{:S(2)}) collective-permute-start(bf16[8,128,128]{2,1,0:T(8,128)(2,1)} %get-tuple-element.25.refs_0_), channel_id=1, source_target_pairs={{0,1},{1,0},{2,3},{3,2},{4,5},{5,4},{6,7},{7,6},{8,9},{9,8},{10,11... | collective-permute-start | bytes 786440 | tf_op jit(solution)/shard_map/ppermute | solution.py:25
  65.1 1.3 collective-permute-start.10
  66.4 26.1 %collective-permute-start.13 = (f32[128,128]{0,1:T(8,128)S(1)}, f32[128,128]{0,1:T(8,128)S(1)}, u32[]{:S(2)}, u32[]{:S(2)}) collective-permute-start(f32[128,128]{0,1:T(8,128)S(1)} %add.51), channel_id=1, source_target_pairs={{0,3},{1,2},{2,1},{3,0},{4,7},{5,6},{6,5},{7,4},{8,11},{9,10},{10,... | collective-permute-start | bytes 196616 | tf_op jit(solution)/shard_map/ppermute | solution.py:25
  68.6 23.9 %collective-permute-start.12 = (f32[128,128]{0,1:T(8,128)S(1)}, f32[128,128]{0,1:T(8,128)S(1)}, u32[]{:S(2)}, u32[]{:S(2)}) collective-permute-start(f32[128,128]{0,1:T(8,128)S(1)} %add.51), channel_id=1, source_target_pairs={{0,2},{1,3},{2,0},{3,1},{4,6},{5,7},{6,4},{7,5},{8,10},{9,11},{10,... | collective-permute-start | bytes 196616 | tf_op jit(solution)/shard_map/ppermute | solution.py:25
  71.0 5.6 %copy-start.6 = (bf16[8,128,128]{2,1,0:T(8,128)(2,1)}, bf16[8,128,128]{2,1,0:T(8,128)(2,1)S(1)}, u32[]{:S(2)}) copy-start(bf16[8,128,128]{2,1,0:T(8,128)(2,1)S(1)} %collective-permute-done.19.refs_3_) | copy-start | bytes 786436
  71.0 21.5 %collective-permute-start.11 = (f32[128,128]{0,1:T(8,128)S(1)}, f32[128,128]{0,1:T(8,128)S(1)}, u32[]{:S(2)}, u32[]{:S(2)}) collective-permute-start(f32[128,128]{0,1:T(8,128)S(1)} %add.51), channel_id=1, source_target_pairs={{0,1},{1,0},{2,3},{3,2},{4,5},{5,4},{6,7},{7,6},{8,9},{9,8},{10,11... | collective-permute-start | bytes 196616 | tf_op jit(solution)/shard_map/ppermute | solution.py:25
  76.5 0.7 copy-start.7
  77.2 0.7 copy-start.9
  88.6 25.5 %collective-permute-start.20 = (bf16[4,8,128,128]{3,2,1,0:T(8,128)(2,1)}, bf16[4,8,128,128]{3,2,1,0:T(8,128)(2,1)S(1)}, u32[]{:S(2)}, u32[]{:S(2)}) collective-permute-start(bf16[4,8,128,128]{3,2,1,0:T(8,128)(2,1)} %get-tuple-element.27), channel_id=1, source_target_pairs={{0,4},{4,0},{8,12},{12,8},{16,20},{20,16},{24,28},{28,24},{1,5},{5... | collective-permute-start | bytes 3145736 | tf_op jit(solution)/shard_map/ppermute | solution.py:25
  92.5 6.7 %collective-permute-start.16 = (f32[128,128]{0,1:T(8,128)S(1)}, f32[128,128]{0,1:T(8,128)S(1)}, u32[]{:S(2)}, u32[]{:S(2)}) collective-permute-start(f32[128,128]{0,1:T(8,128)S(1)} %add_add_fusion.3), channel_id=1, source_target_pairs={{0,24},{4,28},{8,16},{12,20},{16,8},{20,12},{24,0},{28,4},{1,25},{... | collective-permute-start | bytes 196616 | tf_op jit(solution)/shard_map/ppermute | solution.py:25
  94.9 6.6 %collective-permute-start.15 = (f32[128,128]{0,1:T(8,128)S(1)}, f32[128,128]{0,1:T(8,128)S(1)}, u32[]{:S(2)}, u32[]{:S(2)}) collective-permute-start(f32[128,128]{0,1:T(8,128)S(1)} %add_add_fusion.3), channel_id=1, source_target_pairs={{0,16},{4,20},{8,24},{12,28},{16,0},{20,4},{24,8},{28,12},{1,17},{... | collective-permute-start | bytes 196616 | tf_op jit(solution)/shard_map/ppermute | solution.py:25
  95.1 6.5 %collective-permute-start.14 = (f32[128,128]{0,1:T(8,128)S(1)}, f32[128,128]{0,1:T(8,128)S(1)}, u32[]{:S(2)}, u32[]{:S(2)}) collective-permute-start(f32[128,128]{0,1:T(8,128)S(1)} %add_add_fusion.3), channel_id=1, source_target_pairs={{0,8},{4,12},{8,0},{12,4},{16,24},{20,28},{24,16},{28,20},{1,9},{5... | collective-permute-start | bytes 196616 | tf_op jit(solution)/shard_map/ppermute | solution.py:25
  114.1 1.0 copy-start
  118.1 15.8 %collective-permute-start.21 = (bf16[8,128,128]{2,1,0:T(8,128)(2,1)}, bf16[8,128,128]{2,1,0:T(8,128)(2,1)S(1)}, u32[]{:S(2)}, u32[]{:S(2)}) collective-permute-start(bf16[8,128,128]{2,1,0:T(8,128)(2,1)} %get-tuple-element.29), channel_id=1, source_target_pairs={{0,8},{4,12},{8,0},{12,4},{16,24},{20,28},{24,16},{28,20},{1,9},{5... | collective-permute-start | bytes 786440 | tf_op jit(solution)/shard_map/ppermute | solution.py:25
  118.5 21.5 %collective-permute-start.22 = (bf16[8,128,128]{2,1,0:T(8,128)(2,1)}, bf16[8,128,128]{2,1,0:T(8,128)(2,1)S(1)}, u32[]{:S(2)}, u32[]{:S(2)}) collective-permute-start(bf16[8,128,128]{2,1,0:T(8,128)(2,1)} %get-tuple-element.30), channel_id=1, source_target_pairs={{0,16},{4,20},{8,24},{12,28},{16,0},{20,4},{24,8},{28,12},{1,17},{... | collective-permute-start | bytes 786440 | tf_op jit(solution)/shard_map/ppermute | solution.py:25
  120.9 19.2 %collective-permute-start.23 = (bf16[8,128,128]{2,1,0:T(8,128)(2,1)}, bf16[8,128,128]{2,1,0:T(8,128)(2,1)S(1)}, u32[]{:S(2)}, u32[]{:S(2)}) collective-permute-start(bf16[8,128,128]{2,1,0:T(8,128)(2,1)} %get-tuple-element.31), channel_id=1, source_target_pairs={{0,24},{4,28},{8,16},{12,20},{16,8},{20,12},{24,0},{28,4},{1,25},{... | collective-permute-start | bytes 786440 | tf_op jit(solution)/shard_map/ppermute | solution.py:25
  133.8 6.2 %copy-start.14 = (bf16[8,128,128]{2,1,0:T(8,128)(2,1)}, bf16[8,128,128]{2,1,0:T(8,128)(2,1)S(1)}, u32[]{:S(2)}) copy-start(bf16[8,128,128]{2,1,0:T(8,128)(2,1)S(1)} %collective-permute-done.21.refs_0_) | copy-start | bytes 786436
  140.1 0.7 copy-start.15
  140.1 0.8 copy-start.16
  144.9 1.3 collective-permute-start.24
  146.3 5.3 %collective-permute-start.27 = (f32[128,128]{0,1:T(8,128)S(1)}, f32[128,128]{0,1:T(8,128)S(1)}, u32[]{:S(2)}, u32[]{:S(2)}) collective-permute-start(f32[128,128]{0,1:T(8,128)S(1)} %add.58), channel_id=1, source_target_pairs={{0,3},{1,2},{2,1},{3,0},{4,7},{5,6},{6,5},{7,4},{8,11},{9,10},{10,... | collective-permute-start | bytes 196616 | tf_op jit(solution)/shard_map/ppermute | solution.py:25
  148.5 4.4 %collective-permute-start.26 = (f32[128,128]{0,1:T(8,128)S(1)}, f32[128,128]{0,1:T(8,128)S(1)}, u32[]{:S(2)}, u32[]{:S(2)}) collective-permute-start(f32[128,128]{0,1:T(8,128)S(1)} %add.58), channel_id=1, source_target_pairs={{0,2},{1,3},{2,0},{3,1},{4,6},{5,7},{6,4},{7,5},{8,10},{9,11},{10,... | collective-permute-start | bytes 196616 | tf_op jit(solution)/shard_map/ppermute | solution.py:25
  150.0 4.3 %collective-permute-start.25 = (f32[128,128]{0,1:T(8,128)S(1)}, f32[128,128]{0,1:T(8,128)S(1)}, u32[]{:S(2)}, u32[]{:S(2)}) collective-permute-start(f32[128,128]{0,1:T(8,128)S(1)} %add.58), channel_id=1, source_target_pairs={{0,1},{1,0},{2,3},{3,2},{4,5},{5,4},{6,7},{7,6},{8,9},{9,8},{10,11... | collective-permute-start | bytes 196616 | tf_op jit(solution)/shard_map/ppermute | solution.py:25
  154.3 9.3 %collective-permute-start.30 = (f32[128,128]{0,1:T(8,128)S(1)}, f32[128,128]{0,1:T(8,128)S(1)}, u32[]{:S(2)}, u32[]{:S(2)}) collective-permute-start(f32[128,128]{0,1:T(8,128)S(1)} %add_add_fusion.1), channel_id=1, source_target_pairs={{0,24},{4,28},{8,16},{12,20},{16,8},{20,12},{24,0},{28,4},{1,25},{... | collective-permute-start | bytes 196616 | tf_op jit(solution)/shard_map/ppermute | solution.py:25
  156.4 7.8 %collective-permute-start.29 = (f32[128,128]{0,1:T(8,128)S(1)}, f32[128,128]{0,1:T(8,128)S(1)}, u32[]{:S(2)}, u32[]{:S(2)}) collective-permute-start(f32[128,128]{0,1:T(8,128)S(1)} %add_add_fusion.1), channel_id=1, source_target_pairs={{0,16},{4,20},{8,24},{12,28},{16,0},{20,4},{24,8},{28,12},{1,17},{... | collective-permute-start | bytes 196616 | tf_op jit(solution)/shard_map/ppermute | solution.py:25
  160.7 4.3 %collective-permute-start.28 = (f32[128,128]{0,1:T(8,128)S(1)}, f32[128,128]{0,1:T(8,128)S(1)}, u32[]{:S(2)}, u32[]{:S(2)}) collective-permute-start(f32[128,128]{0,1:T(8,128)S(1)} %add_add_fusion.1), channel_id=1, source_target_pairs={{0,8},{4,12},{8,0},{12,4},{16,24},{20,28},{24,16},{28,20},{1,9},{5... | collective-permute-start | bytes 196616 | tf_op jit(solution)/shard_map/ppermute | solution.py:25

commit v2 on v1

v2 whole, which is shorter than its diff:
```python
import functools

import jax
import jax.numpy as jnp
from jax import lax
from jax.experimental import pallas as pl
from jax.experimental.pallas import tpu as pltpu
from jax.sharding import PartitionSpec as P

F32 = jnp.float32
BF16 = jnp.bfloat16
UNROLL = 32
STEP = 8
VMEM = pl.BlockSpec(memory_space=pltpu.VMEM)
SMEM = pl.BlockSpec(memory_space=pltpu.SMEM)
ANY = pl.BlockSpec(memory_space=pl.ANY)
HIGH = lax.Precision.HIGHEST


def params():
    return pltpu.CompilerParams(vmem_limit_bytes=60 * 1024 * 1024)


def swap(value, axis, mask):
    size = lax.axis_size(axis)
    return lax.ppermute(value, axis, [(i, i ^ mask) for i in range(size)])


def chunk_of(slots):
    for size in (32, 16, 8):
        if slots % size == 0:
            return size
    return slots


def product_body(in_axis, forward, counts, out_index, in_index, values, shards, panel, vbuf, acc, sems):
    axis_size = len(shards)
    in_me, count = lax.axis_index(in_axis), counts[0, 0]
    slots = values.shape[2]
    chunk = chunk_of(slots)
    group = min(UNROLL, chunk)
    chunks = slots // chunk
    per_shard = panel.shape[0] // axis_size
    out_blocks = acc.shape[0] - 1

    def panel_copy(k):
        slot = (in_me ^ k) * per_shard
        return pltpu.make_async_copy(shards[k], panel.at[pl.ds(slot, per_shard)], sems.at[chunks + k])

    def value_copy(c):
        span = pl.ds(c * chunk, chunk)
        return pltpu.make_async_copy(values.at[0, 0, span], vbuf.at[span], sems.at[c])

    for k in range(axis_size):
        panel_copy(k).start()
    for c in range(chunks):
        value_copy(c).start()
    acc[...] = jnp.zeros_like(acc)
    for k in range(axis_size):
        panel_copy(k).wait()

    def one_group(g, carry):
        first = g * group
        products = []
        targets = []
        for u in range(group):
            k = first + u
            block = vbuf[k]
            piece = panel[in_index[0, 0, k]]
            if forward:
                products.append(jnp.dot(block, piece, preferred_element_type=F32))
            else:
                products.append(jnp.dot(piece, block, preferred_element_type=F32))
            targets.append(jnp.where(k < count, out_index[0, 0, k], out_blocks))
        for target, product in zip(targets, products):
            acc[target] += product
        return carry

    def one_chunk(c, carry):
        value_copy(c).wait()
        low = c * (chunk // group)
        live = (count + group - 1) // group
        high = jnp.clip(live, low, low + chunk // group)
        return lax.fori_loop(low, high, one_group, carry)

    lax.fori_loop(0, chunks, one_chunk, 0)


def left_kernel(row_size, col_size, counts, rows, cols, values, *refs):
    shards, outs, scratch = refs[:row_size], refs[row_size:-4], refs[-4:]
    panel, vbuf, acc, sems = scratch
    product_body("row", True, counts, rows, cols, values, shards, panel, vbuf, acc, sems)
    per = (acc.shape[0] - 1) // col_size
    me = lax.axis_index("col")
    for k in range(col_size):
        part = acc[pl.ds((me ^ k) * per, per)]
        outs[k][...] = part.astype(outs[k].dtype)


def right_kernel(row_size, col_size, counts, rows, cols, values, *refs):
    shards, (keep, send), scratch = refs[:col_size], refs[col_size:-4], refs[-4:]
    panel, vbuf, acc, sems = scratch
    product_body("col", False, counts, cols, rows, values, shards, panel, vbuf, acc, sems)
    per = (acc.shape[0] - 1) // row_size
    me = lax.axis_index("row")
    for k in range(0, row_size, 2):
        keep[k // 2] = acc[pl.ds((me ^ k) * per, per)]
        send[k // 2] = acc[pl.ds((me ^ (k + 1)) * per, per)].astype(BF16)


def run_product(kernel, counts, rows, cols, values, shards, panel_blocks, out_blocks, out_shape):
    slots, size = values.shape[2], values.shape[-1]
    width = shards[0].shape[-1]
    chunks = slots // chunk_of(slots)
    return pl.pallas_call(
        kernel,
        out_shape=out_shape,
        in_specs=[SMEM, SMEM, SMEM, ANY] + [ANY] * len(shards),
        out_specs=jax.tree.map(lambda _: VMEM, out_shape),
        scratch_shapes=[
            pltpu.VMEM((panel_blocks, size, width), BF16),
            pltpu.VMEM(values.shape[2:], BF16),
            pltpu.VMEM((out_blocks + 1, size, width), F32),
            pltpu.SemaphoreType.DMA((chunks + len(shards),)),
        ],
        compiler_params=params(),
        cost_estimate=pl.CostEstimate(
            flops=2 * slots * size * size * width, bytes_accessed=2 * values.size, transcendentals=0
        ),
    )(counts, rows, cols, values, *shards)


def left_sum_kernel(nodes_total, own, *refs):
    parts, (natural, flipped, gram) = refs[:-3], refs[-3:]
    total = jnp.zeros(gram.shape, F32)
    for b in range(own.shape[0]):
        summed = own[b]
        for part in parts:
            summed = summed + part[b].astype(F32)
        rounded = summed.astype(BF16)
        turned = summed.T.astype(BF16)
        natural[b] = rounded
        flipped[b] = turned
        total = total + jnp.dot(turned, rounded, preferred_element_type=F32)
    gram[...] = total / nodes_total


def core_sum_kernel(keep, came, *outs):
    for k, out in enumerate(outs):
        out[...] = (keep[k] + came[k].astype(F32)).astype(out.dtype)


def inverse_lower(gram):
    order = gram.shape[0]
    panels = order // STEP
    lanes = lax.broadcasted_iota(jnp.int32, (STEP, order), 1)
    strips = [gram[t * STEP:(t + 1) * STEP, :] for t in range(panels)]
    finals = []

    def column(strip, lane):
        return jnp.broadcast_to(strip[:, lane:lane + 1], strip.shape)

    def row(strip, sub):
        return jnp.broadcast_to(strip[sub:sub + 1, :], strip.shape)

    for t in range(panels):
        base = t * STEP
        strip = strips[t]
        cols = [column(strip, base + s) for s in range(STEP)]
        scales, weights, rows_done = [], [], []
        for s in range(STEP):
            scale = lax.rsqrt(row(cols[s], s))
            lower = cols[s] * scale
            scales.append(scale)
            picks = [None] * STEP
            for u in range(s + 1, STEP):
                picks[u] = row(lower, u)
                cols[u] = cols[u] - lower * picks[u]
            weights.append(picks)
            done = jnp.where(lanes == base + s, scale, row(strip, s) * scale)
            done = jnp.where((lanes > base + s) & (lanes < base + STEP), 0.0, done)
            rows_done.append(done)
            if s + 1 < STEP:
                strip = jnp.where(lanes == base + s, 0.0, strip) - lower * done
        sub = lax.broadcasted_iota(jnp.int32, (STEP, order), 0)
        final = rows_done[0]
        for s in range(1, STEP):
            final = jnp.where(sub == s, rows_done[s], final)
        finals.append(jnp.where(lanes <= base + sub, final, 0.0))
        inside = (lanes >= base) & (lanes < base + STEP)
        for v in range(t + 1, panels):
            below = strips[v]
            parts = [column(below, base + s) for s in range(STEP)]
            update = jnp.where(inside, 0.0, below)
            for s in range(STEP):
                part = parts[s] * scales[s]
                for u in range(s + 1, STEP):
                    parts[u] = parts[u] - part * weights[s][u]
                update = update - part * rows_done[s]
            strips[v] = update
    return finals


def limbs(value, depth):
    terms = []
    for _ in range(depth):
        term = value.astype(BF16)
        value = value - term.astype(F32)
        terms.append(term)
    return terms


def fold(stacked, order):
    total = stacked[-order:]
    for low in range(stacked.shape[0] - 2 * order, -1, -order):
        total = stacked[low:low + order] + total
    return total


def factor_of(parts, scratch):
    total = parts[0][...]
    for part in parts[1:]:
        total = total + part[...]
    for t, strip in enumerate(inverse_lower(total)):
        scratch[t * STEP:(t + 1) * STEP, :] = strip
    return scratch[...]


def right_sum_kernel(nodes_total, inverse, own, *refs):
    parts, (flipped, gram) = refs[:-2], refs[-2:]
    order = inverse.shape[0]
    factor = limbs(inverse[...], 3)
    full, head = jnp.concatenate(factor, 0), jnp.concatenate(factor[:2], 0)
    total = jnp.zeros(gram.shape, F32)
    for b in range(own.shape[0]):
        summed = own[b]
        for part in parts:
            summed = summed + part[b].astype(F32)
        first, second = limbs(summed, 2)
        scaled = fold(jnp.dot(head, second, preferred_element_type=F32), order)
        scaled = scaled + fold(jnp.dot(full, first, preferred_element_type=F32), order)
        rounded = scaled.astype(BF16)
        flipped[b] = rounded
        total = total + lax.dot_general(rounded, rounded, (((1,), (1,)), ((), ())), preferred_element_type=F32)
    gram[...] = total / nodes_total


def left_factor_kernel(*refs):
    parts, natural, inverse, out = refs[:-3], refs[-3], refs[-2], refs[-1]
    factor = factor_of(parts, inverse)
    order = factor.shape[0]
    terms = limbs(factor, 3)
    for b in range(natural.shape[0]):
        solved = jnp.zeros(out.shape[1:], F32)
        for term in reversed(terms):
            solved = solved + lax.dot_general(
                natural[b], term, (((1,), (1,)), ((), ())), preferred_element_type=F32
            )
        out[b] = solved.astype(BF16)


def right_factor_kernel(*refs):
    parts, flipped, out, scratch = refs[:-3], refs[-3], refs[-2], refs[-1]
    factor = factor_of(parts, scratch)
    stacked = jnp.concatenate(limbs(factor, 3), 0)
    for b in range(flipped.shape[0]):
        solved = fold(jnp.dot(stacked, flipped[b], preferred_element_type=F32), factor.shape[0])
        out[b] = solved.T.astype(BF16)


def call(kernel, out_shape, *args, scratch=()):
    return pl.pallas_call(
        kernel,
        out_shape=out_shape,
        in_specs=[VMEM] * len(args),
        out_specs=jax.tree.map(lambda _: VMEM, out_shape),
        scratch_shapes=scratch,
        compiler_params=params(),
    )(*args)


def shape(dims, kind):
    return jax.ShapeDtypeStruct(dims, kind)


def exchange(value, axis, first, step=1):
    return [value] + [swap(value, axis, k) for k in range(first, lax.axis_size(axis), step)]


def gather_row(shard):
    row_size = lax.axis_size("row")
    have = {0: shard}
    bit = row_size // 2
    while bit:
        for k in sorted(have):
            have[k | bit] = swap(have[k], "row", bit)
        bit //= 2
    return [have[k] for k in range(row_size)]


def local(start_panel, block_values, block_rows, block_cols, block_counts):
    group_rows, width = start_panel.shape
    row_size = lax.axis_size("row")
    col_size = lax.axis_size("col")
    nodes_total = group_rows * row_size * col_size
    size = block_values.shape[-1]
    lists = (block_counts, block_rows, block_cols, block_values)
    per = group_rows // size
    row_blocks, col_blocks = per * col_size, per * row_size
    block = (per, size, width)
    square = shape((width, width), F32)

    shards = gather_row(start_panel.reshape(block))
    parts = run_product(
        functools.partial(left_kernel, row_size, col_size),
        *lists, shards, col_blocks, row_blocks,
        [shape(block, F32)] + [shape(block, BF16)] * (col_size - 1),
    )
    came = [swap(parts[k], "col", k) for k in range(1, col_size)]
    natural, flipped, gram = call(
        functools.partial(left_sum_kernel, nodes_total),
        (shape(block, BF16), shape(block, BF16), square), parts[0], *came,
    )
    turned = exchange(flipped, "col", 1)
    gram = gram + swap(gram, "row", 1)
    gram = functools.reduce(jnp.add, exchange(gram, "row", 2, 2))

    half = (row_size // 2,) + block
    keep, send = run_product(
        functools.partial(right_kernel, row_size, col_size),
        *lists, turned, row_blocks, col_blocks,
        [shape(half, F32), shape(half, BF16)],
    )
    sums = call(
        core_sum_kernel, [shape(block, F32)] + [shape(block, BF16)] * (row_size // 2 - 1),
        keep, swap(send, "row", 1),
    )
    came = [swap(sums[k // 2], "row", k) for k in range(2, row_size, 2)]
    gram, _ = lax.optimization_barrier((gram, sums[-1]))
    inverse, left_panel = call(
        left_factor_kernel, (square, shape(block, BF16)), *exchange(gram, "col", 1), natural
    )
    right_flipped, gram = call(
        functools.partial(right_sum_kernel, nodes_total), (shape(block, BF16), square), inverse, sums[0], *came
    )
    gram = gram + swap(gram, "row", 1)
    gram = functools.reduce(jnp.add, exchange(gram, "col", 1))
    right_panel = call(
        right_factor_kernel, shape(block, BF16), *exchange(gram, "row", 2, 2), right_flipped,
        scratch=[pltpu.VMEM((width, width), F32)],
    )
    return (left_panel.reshape(group_rows, width), right_panel.reshape(group_rows, width))


def solution(mesh):
    return jax.shard_map(
        local,
        mesh=mesh,
        in_specs=(
            P(("col", "row"), None),
            P("row", "col", None, None, None),
            P("row", "col", None),
            P("row", "col", None),
            P("row", "col"),
        ),
        out_specs=(P(("row", "col"), None), P(("col", "row"), None)),
        check_vma=False,
    )
```

time: 192 us -> 145 us (0.76)
  other arithmetic: 49.8 us -> 0.89 us
  waiting for transfers between devices: 52.9 us -> 61.2 us
  starting transfers between devices: 44 us -> 39.6 us
    another operation x12 -> x0, other arithmetic: 47.1 us -> none  [the longest x6 25 us: inverse_factor(): lower = jnp.linalg.cholesky(gram_total)]
    ppermute x31, waiting for transfers between devices: 52.9 us -> 61.2 us  [swap(): return lax.ppermute(value, axis, [(i, i ^ mask) for i in range(size)])]
    pallas_call x5, Pallas kernels: 13.6 us -> 21.1 us  [call(): pl.pallas_call(kernel, out_shape=out_shape, in_specs=[VMEM] * len(args),...]
    pallas_call x2, Pallas kernels: 20.9 us -> 14.3 us  [run_product(): pl.pallas_call(kernel, out_shape=out_shape, in_specs=[SMEM, SMEM, SMEM, A...]
    ppermute x31, starting transfers between devices: 44 us -> 39.6 us  [swap(): return lax.ppermute(value, axis, [(i, i ^ mask) for i in range(size)])]
    unnamed x2 -> x0, other arithmetic: 2.55 us -> none
    unnamed x34 -> x52, local copies, waits for them, and re-layouts: 4.77 us -> 5.98 us
  transfers between devices with their start and end apart: 31 -> 31, of which waited for: 17 -> 19; matrix products, arithmetic and copies ran while one was open for 15% -> 0% of each run, Pallas kernels for 7% -> 7%
where the time goes in v2:
time: 145 us
  waiting for transfers between devices  61.2 us (42%)
  starting transfers between devices  39.6 us (27%)
  Pallas kernels  35.4 us (24%)
  local copies, waits for them, and re-layouts  5.98 us (4%)
  between operations  1.48 us (1%)
    ppermute x31, waiting for transfers between devices, swap(): return lax.ppermute(value, axis, [(i, i ^ mask) for i in range(size)])  61.2 us
    ppermute x31, starting transfers between devices, swap(): return lax.ppermute(value, axis, [(i, i ^ mask) for i in range(size)])  39.6 us
    pallas_call x5, Pallas kernels, call(): pl.pallas_call(kernel, out_shape=out_shape, in_specs=[VMEM] * len(args),...  21.1 us
    pallas_call x2, Pallas kernels, run_product(): pl.pallas_call(kernel, out_shape=out_shape, in_specs=[SMEM, SMEM, SMEM, A...  14.3 us
    unnamed x52, local copies, waits for them, and re-layouts  5.98 us
  transfers between devices with their start and end apart: 31, of which 19 were waited for; matrix products, arithmetic and copies ran while one was open for 0% of the time, Pallas kernels for 7%

profile of v2, /device:TPU:0, one launch (start us, length us, event | category | flops | bytes accessed | tf_op | source)
XLA Modules:
  0.0 144.5 jit_solution(10700973176428536796)
XLA Ops:
  0.6 4.1 %collective-permute-start.3 = (bf16[8,128,128]{2,1,0:T(8,128)(2,1)}, bf16[8,128,128]{2,1,0:T(8,128)(2,1)S(1)}, u32[]{:S(2)}, u32[]{:S(2)}) collective-permute-start(bf16[8,128,128]{2,1,0:T(8,128)(2,1)} %bitcast.3), channel_id=1, source_target_pairs={{0,16},{4,20},{8,24},{12,28},{16,0},{20,4},{24,8},{28,12},{1,17},{... | collective-permute-start | bytes 786440 | tf_op jit(solution)/shard_map/ppermute | solution.py:26
  4.8 1.6 %collective-permute-start.1 = (bf16[8,128,128]{2,1,0:T(8,128)(2,1)}, bf16[8,128,128]{2,1,0:T(8,128)(2,1)S(1)}, u32[]{:S(2)}, u32[]{:S(2)}) collective-permute-start(bf16[8,128,128]{2,1,0:T(8,128)(2,1)} %bitcast.4), channel_id=1, source_target_pairs={{0,8},{4,12},{8,0},{12,4},{16,24},{20,28},{24,16},{28,20},{1,9},{5... | collective-permute-start | bytes 786440 | tf_op jit(solution)/shard_map/ppermute | solution.py:26
  6.3 10.7 %collective-permute-done.3.refs_4_ = bf16[8,128,128]{2,1,0:T(8,128)(2,1)S(1)} collective-permute-done((bf16[8,128,128]{2,1,0:T(8,128)(2,1)}, bf16[8,128,128]{2,1,0:T(8,128)(2,1)S(1)}, u32[]{:S(2)}, u32[]{:S(2)}) %collective-permute-start.3) | collective-permute-done | bytes 262176 | tf_op jit(solution)/shard_map/ppermute | solution.py:26
  17.0 0.7 collective-permute-start.5
  17.7 0.5 collective-permute-start.4
  18.2 0.1 collective-permute-start.2
  18.3 6.1 %collective-permute-done.5.refs_6_ = bf16[8,128,128]{2,1,0:T(8,128)(2,1)S(1)} collective-permute-done((bf16[8,128,128]{2,1,0:T(8,128)(2,1)S(1)}, bf16[8,128,128]{2,1,0:T(8,128)(2,1)S(1)}, u32[]{:S(2)}, u32[]{:S(2)}) %collective-permute-start.5) | collective-permute-done | bytes 262176 | tf_op jit(solution)/shard_map/ppermute | solution.py:26
  25.1 0.0 copy-start.4
  25.1 0.8 collective-permute-done.6.refs_7_
  26.0 0.7 copy-done.8
  26.7 7.0 %shard_map.68 = (f32[8,128,128]{2,1,0:T(8,128)}, bf16[8,128,128]{2,1,0:T(8,128)(2,1)}, bf16[8,128,128]{2,1,0:T(8,128)(2,1)}, bf16[8,128,128]{2,1,0:T(8,128)(2,1)}) custom-call(s32[1,1]{1,0:T(1,128)S(6)} %copy.7.counts, s32[1,1,352]{2,1,0:T(1,128)} %rows.3, s32[1,1,352]{2,1,0:T(1,128)} %cols.3, bf16[1,1,352,128,128]{4,3,2,1,0:T(8,128)(2,1)} %values.3, ...), custom_call_target="tpu_custom_call" | custom-call | flops 1476395008 | bytes 11534336 | tf_op jit(solution)/shard_map/pallas_call | solution.py:115
  33.7 2.3 %collective-permute-start.7 = (bf16[8,128,128]{2,1,0:T(8,128)(2,1)}, bf16[8,128,128]{2,1,0:T(8,128)(2,1)S(1)}, u32[]{:S(2)}, u32[]{:S(2)}) collective-permute-start(bf16[8,128,128]{2,1,0:T(8,128)(2,1)} %get-tuple-element.21), channel_id=1, source_target_pairs={{0,1},{1,0},{2,3},{3,2},{4,5},{5,4},{6,7},{7,6},{8,9},{9,8},{10,11... | collective-permute-start | bytes 786440 | tf_op jit(solution)/shard_map/ppermute | solution.py:26
  36.0 0.6 collective-permute-start.8
  36.6 1.4 collective-permute-start.9
  38.0 5.1 %collective-permute-done.7.refs_0_ = bf16[8,128,128]{2,1,0:T(8,128)(2,1)S(1)} collective-permute-done((bf16[8,128,128]{2,1,0:T(8,128)(2,1)}, bf16[8,128,128]{2,1,0:T(8,128)(2,1)S(1)}, u32[]{:S(2)}, u32[]{:S(2)}) %collective-permute-start.7) | collective-permute-done | bytes 262176 | tf_op jit(solution)/shard_map/ppermute | solution.py:26
  43.0 7.2 %collective-permute-done.8.refs_1_ = bf16[8,128,128]{2,1,0:T(8,128)(2,1)S(1)} collective-permute-done((bf16[8,128,128]{2,1,0:T(8,128)(2,1)}, bf16[8,128,128]{2,1,0:T(8,128)(2,1)S(1)}, u32[]{:S(2)}, u32[]{:S(2)}) %collective-permute-start.8) | collective-permute-done | bytes 262176 | tf_op jit(solution)/shard_map/ppermute | solution.py:26
  50.3 0.7 copy-done.9
  50.9 0.1 copy-done.11
  51.0 2.2 %shard_map.69 = (bf16[8,128,128]{2,1,0:T(8,128)(2,1)}, bf16[8,128,128]{2,1,0:T(8,128)(2,1)}, f32[128,128]{1,0:T(8,128)}) custom-call(f32[8,128,128]{2,1,0:T(8,128)} %get-tuple-element.20.own, bf16[8,128,128]{2,1,0:T(8,128)(2,1)} %copy-done.7, bf16[8,128,128]{2,1,0:T(8,128)(2,1)} %copy-done.9, bf16[8,128,128]{2,1,0:T(8,128)(2,1)} %copy-done.11), custom_call_target="tpu_custom_call" | custom-call | tf_op jit(solution)/shard_map/pallas_call | solution.py:272
  53.3 1.4 collective-permute-start.16
  54.7 0.9 collective-permute-start.15
  55.6 1.2 collective-permute-start.14
  56.8 6.8 %collective-permute-done.16.refs_3_ = bf16[8,128,128]{2,1,0:T(8,128)(2,1)S(1)} collective-permute-done((bf16[8,128,128]{2,1,0:T(8,128)(2,1)}, bf16[8,128,128]{2,1,0:T(8,128)(2,1)S(1)}, u32[]{:S(2)}, u32[]{:S(2)}) %collective-permute-start.16) | collective-permute-done | bytes 262176 | tf_op jit(solution)/shard_map/ppermute | solution.py:26
  63.6 3.9 %collective-permute-done.15.refs_2_ = bf16[8,128,128]{2,1,0:T(8,128)(2,1)S(1)} collective-permute-done((bf16[8,128,128]{2,1,0:T(8,128)(2,1)}, bf16[8,128,128]{2,1,0:T(8,128)(2,1)S(1)}, u32[]{:S(2)}, u32[]{:S(2)}) %collective-permute-start.15) | collective-permute-done | bytes 262176 | tf_op jit(solution)/shard_map/ppermute | solution.py:26
  67.5 0.7 copy-done.12
  68.2 0.7 copy-done.13
  68.9 7.3 %shard_map.70 = (f32[4,8,128,128]{3,2,1,0:T(8,128)}, bf16[4,8,128,128]{3,2,1,0:T(8,128)(2,1)}) custom-call(s32[1,1]{1,0:T(1,128)S(6)} %copy.7.counts, s32[1,1,352]{2,1,0:T(1,128)} %rows.3, s32[1,1,352]{2,1,0:T(1,128)} %cols.3, bf16[1,1,352,128,128]{4,3,2,1,0:T(8,128)(2,1)} %values.3, bf16[8,128,128]{2,1,0:T(8,128)(2,1)} %get-tuple-element.25.refs_0_, ...), custom_call_target="tpu_custom_call" | custom-call | flops 1476395008 | bytes 11534336 | tf_op jit(solution)/shard_map/pallas_call | solution.py:115
  76.3 1.9 %collective-permute-start.17 = (bf16[4,8,128,128]{3,2,1,0:T(8,128)(2,1)}, bf16[4,8,128,128]{3,2,1,0:T(8,128)(2,1)S(1)}, u32[]{:S(2)}, u32[]{:S(2)}) collective-permute-start(bf16[4,8,128,128]{3,2,1,0:T(8,128)(2,1)} %get-tuple-element.27), channel_id=1, source_target_pairs={{0,4},{4,0},{8,12},{12,8},{16,20},{20,16},{24,28},{28,24},{1,5},{5... | collective-permute-start | bytes 3145736 | tf_op jit(solution)/shard_map/ppermute | solution.py:26
  78.2 0.1 collective-permute-start.10
  78.3 2.5 %collective-permute-done.10 = f32[128,128]{1,0:T(8,128)S(1)} collective-permute-done((f32[128,128]{1,0:T(8,128)S(1)}, f32[128,128]{1,0:T(8,128)S(1)}, u32[]{:S(2)}, u32[]{:S(2)}) %collective-permute-start.10) | collective-permute-done | bytes 65568 | tf_op jit(solution)/shard_map/ppermute | solution.py:26
  80.8 5.9 %collective-permute-start.13 = (f32[128,128]{1,0:T(8,128)S(1)}, f32[128,128]{1,0:T(8,128)S(1)}, u32[]{:S(2)}, u32[]{:S(2)}) collective-permute-start(f32[128,128]{1,0:T(8,128)S(1)} %add.24), channel_id=1, source_target_pairs={{0,24},{4,28},{8,16},{12,20},{16,8},{20,12},{24,0},{28,4},{1,25},{... | collective-permute-start | bytes 196616 | tf_op jit(solution)/shard_map/ppermute | solution.py:26
  86.6 0.6 collective-permute-start.11
  87.3 1.0 copy-done
  88.3 3.0 %shard_map.71 = (f32[8,128,128]{2,1,0:T(8,128)}, bf16[8,128,128]{2,1,0:T(8,128)(2,1)}, bf16[8,128,128]{2,1,0:T(8,128)(2,1)}, bf16[8,128,128]{2,1,0:T(8,128)(2,1)}) custom-call(f32[4,8,128,128]{3,2,1,0:T(8,128)} %get-tuple-element.26.keep, bf16[4,8,128,128]{3,2,1,0:T(8,128)(2,1)} %copy-done), custom_call_target="tpu_custom_call" | custom-call | tf_op jit(solution)/shard_map/pallas_call | solution.py:272
  91.2 1.4 collective-permute-start.21
  92.6 2.9 %collective-permute-start.22 = (bf16[8,128,128]{2,1,0:T(8,128)(2,1)}, bf16[8,128,128]{2,1,0:T(8,128)(2,1)S(1)}, u32[]{:S(2)}, u32[]{:S(2)}) collective-permute-start(bf16[8,128,128]{2,1,0:T(8,128)(2,1)} %get-tuple-element.35), channel_id=1, source_target_pairs={{0,16},{4,20},{8,24},{12,28},{16,0},{20,4},{24,8},{28,12},{1,17},{... | collective-permute-start | bytes 786440 | tf_op jit(solution)/shard_map/ppermute | solution.py:26
  95.5 0.1 collective-permute-start.23
  95.7 1.8 %collective-permute-start.20 = (f32[128,128]{1,0:T(8,128)S(1)}, f32[128,128]{1,0:T(8,128)S(1)}, u32[]{:S(2)}, u32[]{:S(2)}) collective-permute-start(f32[128,128]{1,0:T(8,128)S(1)} %add_add_fusion.1.refs_0_), channel_id=1, source_target_pairs={{0,3},{1,2},{2,1},{3,0},{4,7},{5,6},{6,5},{7,4},{8,11},{9,10},{10,... | collective-permute-start | bytes 196616 | tf_op jit(solution)/shard_map/ppermute | solution.py:26
  97.5 0.1 collective-permute-start.19
  97.6 3.3 %collective-permute-done.20.refs_3_ = f32[128,128]{1,0:T(8,128)S(1)} collective-permute-done((f32[128,128]{1,0:T(8,128)S(1)}, f32[128,128]{1,0:T(8,128)S(1)}, u32[]{:S(2)}, u32[]{:S(2)}) %collective-permute-start.20) | collective-permute-done | bytes 65568 | tf_op jit(solution)/shard_map/ppermute | solution.py:26
  100.9 0.5 collective-permute-start.18
  101.4 0.4 collective-permute-done.19.refs_2_
  101.7 3.4 %collective-permute-done.18.refs_1_ = f32[128,128]{1,0:T(8,128)S(1)} collective-permute-done((f32[128,128]{1,0:T(8,128)S(1)}, f32[128,128]{1,0:T(8,128)S(1)}, u32[]{:S(2)}, u32[]{:S(2)}) %collective-permute-start.18) | collective-permute-done | bytes 65568 | tf_op jit(solution)/shard_map/ppermute | solution.py:26
  105.2 0.6 copy-done.25
  105.8 6.5 %shard_map.72 = (f32[128,128]{1,0:T(8,128)}, bf16[8,128,128]{2,1,0:T(8,128)(2,1)}) custom-call(f32[128,128]{1,0:T(8,128)} %copy-done.18, f32[128,128]{1,0:T(8,128)} %copy-done.25, f32[128,128]{1,0:T(8,128)} %copy-done.24, f32[128,128]{1,0:T(8,128)} %copy-done.23, bf16[8,128,128]{2,1,0:T(8,128)(2,1)} %get-tuple-element.30.refs_4_), custom_call_target="tpu_custom_call" | custom-call | tf_op jit(solution)/shard_map/pallas_call | solution.py:272
  112.3 1.9 %collective-permute-done.22.refs_1_ = bf16[8,128,128]{2,1,0:T(8,128)(2,1)S(1)} collective-permute-done((bf16[8,128,128]{2,1,0:T(8,128)(2,1)}, bf16[8,128,128]{2,1,0:T(8,128)(2,1)S(1)}, u32[]{:S(2)}, u32[]{:S(2)}) %collective-permute-start.22) | collective-permute-done | bytes 262176 | tf_op jit(solution)/shard_map/ppermute | solution.py:26
  114.2 0.7 copy-done.16
  114.9 0.1 copy-done.17
  115.0 3.1 %shard_map.73 = (bf16[8,128,128]{2,1,0:T(8,128)(2,1)}, f32[128,128]{1,0:T(8,128)}) custom-call(f32[128,128]{1,0:T(8,128)} %get-tuple-element.32.inverse, f32[8,128,128]{2,1,0:T(8,128)} %get-tuple-element.33.own, bf16[8,128,128]{2,1,0:T(8,128)(2,1)} %copy-done.15, bf16[8,128,128]{2,1,0:T(8,128)(2,1)} %copy-done.16, bf16[8,128,128]{2,1,0:T(8,128)(2,1)} %copy-done.17), custom_call_target="tpu_custom_call" | custom-call | tf_op jit(solution)/shard_map/pallas_call | solution.py:272
  118.1 1.5 %collective-permute-done.24 = f32[128,128]{1,0:T(8,128)S(1)} collective-permute-done((f32[128,128]{1,0:T(8,128)}, f32[128,128]{1,0:T(8,128)S(1)}, u32[]{:S(2)}, u32[]{:S(2)}) %collective-permute-start.24) | collective-permute-done | bytes 65568 | tf_op jit(solution)/shard_map/ppermute | solution.py:26
  119.6 0.9 add.28
  120.4 1.8 %collective-permute-start.27 = (f32[128,128]{1,0:T(8,128)S(1)}, f32[128,128]{1,0:T(8,128)S(1)}, u32[]{:S(2)}, u32[]{:S(2)}) collective-permute-start(f32[128,128]{1,0:T(8,128)S(1)} %add.28), channel_id=1, source_target_pairs={{0,3},{1,2},{2,1},{3,0},{4,7},{5,6},{6,5},{7,4},{8,11},{9,10},{10,... | collective-permute-start | bytes 196616 | tf_op jit(solution)/shard_map/ppermute | solution.py:26
  122.2 0.2 collective-permute-start.26
  122.4 1.6 %collective-permute-start.25 = (f32[128,128]{1,0:T(8,128)S(1)}, f32[128,128]{1,0:T(8,128)S(1)}, u32[]{:S(2)}, u32[]{:S(2)}) collective-permute-start(f32[128,128]{1,0:T(8,128)S(1)} %add.28), channel_id=1, source_target_pairs={{0,1},{1,0},{2,3},{3,2},{4,5},{5,4},{6,7},{7,6},{8,9},{9,8},{10,11... | collective-permute-start | bytes 196616 | tf_op jit(solution)/shard_map/ppermute | solution.py:26
  124.0 1.7 %collective-permute-done.27 = f32[128,128]{1,0:T(8,128)S(1)} collective-permute-done((f32[128,128]{1,0:T(8,128)S(1)}, f32[128,128]{1,0:T(8,128)S(1)}, u32[]{:S(2)}, u32[]{:S(2)}) %collective-permute-start.27) | collective-permute-done | bytes 65568 | tf_op jit(solution)/shard_map/ppermute | solution.py:26
  125.7 1.3 collective-permute-done.26
  126.9 0.4 collective-permute-done.25
  127.3 2.4 %collective-permute-start.30 = (f32[128,128]{1,0:T(8,128)S(1)}, f32[128,128]{1,0:T(8,128)S(1)}, u32[]{:S(2)}, u32[]{:S(2)}) collective-permute-start(f32[128,128]{1,0:T(8,128)S(1)} %add_add_fusion.refs_0_), channel_id=1, source_target_pairs={{0,24},{4,28},{8,16},{12,20},{16,8},{20,12},{24,0},{28,4},{1,25},{... | collective-permute-start | bytes 196616 | tf_op jit(solution)/shard_map/ppermute | solution.py:26
  129.7 3.6 %collective-permute-start.29 = (f32[128,128]{1,0:T(8,128)S(1)}, f32[128,128]{1,0:T(8,128)S(1)}, u32[]{:S(2)}, u32[]{:S(2)}) collective-permute-start(f32[128,128]{1,0:T(8,128)S(1)} %add_add_fusion.refs_0_), channel_id=1, source_target_pairs={{0,16},{4,20},{8,24},{12,28},{16,0},{20,4},{24,8},{28,12},{1,17},{... | collective-permute-start | bytes 196616 | tf_op jit(solution)/shard_map/ppermute | solution.py:26
  133.3 0.2 collective-permute-done.30.refs_3_
  133.5 3.5 %collective-permute-done.29.refs_2_ = f32[128,128]{1,0:T(8,128)S(1)} collective-permute-done((f32[128,128]{1,0:T(8,128)S(1)}, f32[128,128]{1,0:T(8,128)S(1)}, u32[]{:S(2)}, u32[]{:S(2)}) %collective-permute-start.29) | collective-permute-done | bytes 65568 | tf_op jit(solution)/shard_map/ppermute | solution.py:26
  137.0 0.7 collective-permute-done.28.refs_1_
  137.7 0.6 copy-done.22
  138.3 6.2 %shard_map.74 = bf16[8,128,128]{2,1,0:T(8,128)(2,1)} custom-call(f32[128,128]{1,0:T(8,128)} %copy-done.14, f32[128,128]{1,0:T(8,128)} %copy-done.22, f32[128,128]{1,0:T(8,128)} %copy-done.21, f32[128,128]{1,0:T(8,128)} %copy-done.20, bf16[8,128,128]{2,1,0:T(8,128)(2,1)} %get-tuple-element.37.refs_4_), custom_call_target="tpu_custom_call" | custom-call | tf_op jit(solution)/shard_map/pallas_call | solution.py:272
  (61 shorter events, 0.2 us)
Async XLA Ops:
  0.6 16.4 %collective-permute-start.3 = (bf16[8,128,128]{2,1,0:T(8,128)(2,1)}, bf16[8,128,128]{2,1,0:T(8,128)(2,1)S(1)}, u32[]{:S(2)}, u32[]{:S(2)}) collective-permute-start(bf16[8,128,128]{2,1,0:T(8,128)(2,1)} %bitcast.3), channel_id=1, source_target_pairs={{0,16},{4,20},{8,24},{12,28},{16,0},{20,4},{24,8},{28,12},{1,17},{... | collective-permute-start | bytes 786440 | tf_op jit(solution)/shard_map/ppermute | solution.py:26
  4.8 13.5 %collective-permute-start.1 = (bf16[8,128,128]{2,1,0:T(8,128)(2,1)}, bf16[8,128,128]{2,1,0:T(8,128)(2,1)S(1)}, u32[]{:S(2)}, u32[]{:S(2)}) collective-permute-start(bf16[8,128,128]{2,1,0:T(8,128)(2,1)} %bitcast.4), channel_id=1, source_target_pairs={{0,8},{4,12},{8,0},{12,4},{16,24},{20,28},{24,16},{28,20},{1,9},{5... | collective-permute-start | bytes 786440 | tf_op jit(solution)/shard_map/ppermute | solution.py:26
  17.0 9.0 %copy-start.1 = (bf16[8,128,128]{2,1,0:T(8,128)(2,1)}, bf16[8,128,128]{2,1,0:T(8,128)(2,1)S(1)}, u32[]{:S(2)}) copy-start(bf16[8,128,128]{2,1,0:T(8,128)(2,1)S(1)} %collective-permute-done.3.refs_4_) | copy-start | bytes 786436
  17.0 7.4 %collective-permute-start.5 = (bf16[8,128,128]{2,1,0:T(8,128)(2,1)S(1)}, bf16[8,128,128]{2,1,0:T(8,128)(2,1)S(1)}, u32[]{:S(2)}, u32[]{:S(2)}) collective-permute-start(bf16[8,128,128]{2,1,0:T(8,128)(2,1)S(1)} %collective-permute-done.3.refs_4_), channel_id=1, source_target_pairs={{0,8},{4,12},{8,0},{12,4},{16,24},{20,28},{24,16},{28,20},{1,9},{5... | collective-permute-start | bytes 786440 | tf_op jit(solution)/shard_map/ppermute | solution.py:26
  17.7 7.3 %collective-permute-start = (bf16[8,128,128]{2,1,0:T(8,128)(2,1)}, bf16[8,128,128]{2,1,0:T(8,128)(2,1)S(1)}, u32[]{:S(2)}, u32[]{:S(2)}) collective-permute-start(bf16[8,128,128]{2,1,0:T(8,128)(2,1)} %bitcast.5), channel_id=1, source_target_pairs={{0,4},{4,0},{8,12},{12,8},{16,20},{20,16},{24,28},{28,24},{1,5},{5... | collective-permute-start | bytes 786440 | tf_op jit(solution)/shard_map/ppermute | solution.py:26
  17.7 7.4 %collective-permute-start.4 = (bf16[8,128,128]{2,1,0:T(8,128)(2,1)S(1)}, bf16[8,128,128]{2,1,0:T(8,128)(2,1)S(1)}, u32[]{:S(2)}, u32[]{:S(2)}) collective-permute-start(bf16[8,128,128]{2,1,0:T(8,128)(2,1)S(1)} %collective-permute-done.3.refs_4_), channel_id=1, source_target_pairs={{0,4},{4,0},{8,12},{12,8},{16,20},{20,16},{24,28},{28,24},{1,5},{5... | collective-permute-start | bytes 786440 | tf_op jit(solution)/shard_map/ppermute | solution.py:26
  18.2 7.7 %copy-start.2 = (bf16[8,128,128]{2,1,0:T(8,128)(2,1)}, bf16[8,128,128]{2,1,0:T(8,128)(2,1)S(1)}, u32[]{:S(2)}) copy-start(bf16[8,128,128]{2,1,0:T(8,128)(2,1)S(1)} %collective-permute-done.1.refs_2_) | copy-start | bytes 786436
  18.2 6.9 %collective-permute-start.2 = (bf16[8,128,128]{2,1,0:T(8,128)(2,1)S(1)}, bf16[8,128,128]{2,1,0:T(8,128)(2,1)S(1)}, u32[]{:S(2)}, u32[]{:S(2)}) collective-permute-start(bf16[8,128,128]{2,1,0:T(8,128)(2,1)S(1)} %collective-permute-done.1.refs_2_), channel_id=1, source_target_pairs={{0,4},{4,0},{8,12},{12,8},{16,20},{20,16},{24,28},{28,24},{1,5},{5... | collective-permute-start | bytes 786440 | tf_op jit(solution)/shard_map/ppermute | solution.py:26
  24.4 1.5 %copy-start.3 = (bf16[8,128,128]{2,1,0:T(8,128)(2,1)}, bf16[8,128,128]{2,1,0:T(8,128)(2,1)S(1)}, u32[]{:S(2)}) copy-start(bf16[8,128,128]{2,1,0:T(8,128)(2,1)S(1)} %collective-permute-done.5.refs_6_) | copy-start | bytes 786436
  24.4 1.5 %collective-permute-start.6 = (bf16[8,128,128]{2,1,0:T(8,128)(2,1)S(1)}, bf16[8,128,128]{2,1,0:T(8,128)(2,1)S(1)}, u32[]{:S(2)}, u32[]{:S(2)}) collective-permute-start(bf16[8,128,128]{2,1,0:T(8,128)(2,1)S(1)} %collective-permute-done.5.refs_6_), channel_id=1, source_target_pairs={{0,4},{4,0},{8,12},{12,8},{16,20},{20,16},{24,28},{28,24},{1,5},{5... | collective-permute-start | bytes 786440 | tf_op jit(solution)/shard_map/ppermute | solution.py:26
  25.1 0.9 copy-start.4
  25.1 0.9 copy-start.5
  25.1 0.9 copy-start.6
  26.0 0.7 copy-start.8
  33.7 9.3 %collective-permute-start.7 = (bf16[8,128,128]{2,1,0:T(8,128)(2,1)}, bf16[8,128,128]{2,1,0:T(8,128)(2,1)S(1)}, u32[]{:S(2)}, u32[]{:S(2)}) collective-permute-start(bf16[8,128,128]{2,1,0:T(8,128)(2,1)} %get-tuple-element.21), channel_id=1, source_target_pairs={{0,1},{1,0},{2,3},{3,2},{4,5},{5,4},{6,7},{7,6},{8,9},{9,8},{10,11... | collective-permute-start | bytes 786440 | tf_op jit(solution)/shard_map/ppermute | solution.py:26
  36.0 14.2 %collective-permute-start.8 = (bf16[8,128,128]{2,1,0:T(8,128)(2,1)}, bf16[8,128,128]{2,1,0:T(8,128)(2,1)S(1)}, u32[]{:S(2)}, u32[]{:S(2)}) collective-permute-start(bf16[8,128,128]{2,1,0:T(8,128)(2,1)} %get-tuple-element.22), channel_id=1, source_target_pairs={{0,2},{1,3},{2,0},{3,1},{4,6},{5,7},{6,4},{7,5},{8,10},{9,11},{10,... | collective-permute-start | bytes 786440 | tf_op jit(solution)/shard_map/ppermute | solution.py:26
  36.6 13.7 %collective-permute-start.9 = (bf16[8,128,128]{2,1,0:T(8,128)(2,1)}, bf16[8,128,128]{2,1,0:T(8,128)(2,1)S(1)}, u32[]{:S(2)}, u32[]{:S(2)}) collective-permute-start(bf16[8,128,128]{2,1,0:T(8,128)(2,1)} %get-tuple-element.23), channel_id=1, source_target_pairs={{0,3},{1,2},{2,1},{3,0},{4,7},{5,6},{6,5},{7,4},{8,11},{9,10},{10,... | collective-permute-start | bytes 786440 | tf_op jit(solution)/shard_map/ppermute | solution.py:26
  43.0 7.2 %copy-start.7 = (bf16[8,128,128]{2,1,0:T(8,128)(2,1)}, bf16[8,128,128]{2,1,0:T(8,128)(2,1)S(1)}, u32[]{:S(2)}) copy-start(bf16[8,128,128]{2,1,0:T(8,128)(2,1)S(1)} %collective-permute-done.7.refs_0_) | copy-start | bytes 786436
  50.2 0.7 copy-start.9
  50.2 0.8 copy-start.11
  53.3 24.9 %copy-start.19 = (f32[128,128]{1,0:T(8,128)S(1)}, f32[128,128]{1,0:T(8,128)}, u32[]{:S(2)}) copy-start(f32[128,128]{1,0:T(8,128)} %get-tuple-element.24) | copy-start | bytes 196612
  53.3 10.3 %collective-permute-start.16 = (bf16[8,128,128]{2,1,0:T(8,128)(2,1)}, bf16[8,128,128]{2,1,0:T(8,128)(2,1)S(1)}, u32[]{:S(2)}, u32[]{:S(2)}) collective-permute-start(bf16[8,128,128]{2,1,0:T(8,128)(2,1)} %get-tuple-element.25.refs_0_), channel_id=1, source_target_pairs={{0,3},{1,2},{2,1},{3,0},{4,7},{5,6},{6,5},{7,4},{8,11},{9,10},{10,... | collective-permute-start | bytes 786440 | tf_op jit(solution)/shard_map/ppermute | solution.py:26
  54.7 12.9 %collective-permute-start.15 = (bf16[8,128,128]{2,1,0:T(8,128)(2,1)}, bf16[8,128,128]{2,1,0:T(8,128)(2,1)S(1)}, u32[]{:S(2)}, u32[]{:S(2)}) collective-permute-start(bf16[8,128,128]{2,1,0:T(8,128)(2,1)} %get-tuple-element.25.refs_0_), channel_id=1, source_target_pairs={{0,2},{1,3},{2,0},{3,1},{4,6},{5,7},{6,4},{7,5},{8,10},{9,11},{10,... | collective-permute-start | bytes 786440 | tf_op jit(solution)/shard_map/ppermute | solution.py:26
  55.6 11.9 %collective-permute-start.14 = (bf16[8,128,128]{2,1,0:T(8,128)(2,1)}, bf16[8,128,128]{2,1,0:T(8,128)(2,1)S(1)}, u32[]{:S(2)}, u32[]{:S(2)}) collective-permute-start(bf16[8,128,128]{2,1,0:T(8,128)(2,1)} %get-tuple-element.25.refs_0_), channel_id=1, source_target_pairs={{0,1},{1,0},{2,3},{3,2},{4,5},{5,4},{6,7},{7,6},{8,9},{9,8},{10,11... | collective-permute-start | bytes 786440 | tf_op jit(solution)/shard_map/ppermute | solution.py:26
  63.6 3.9 %copy-start.10 = (bf16[8,128,128]{2,1,0:T(8,128)(2,1)}, bf16[8,128,128]{2,1,0:T(8,128)(2,1)S(1)}, u32[]{:S(2)}) copy-start(bf16[8,128,128]{2,1,0:T(8,128)(2,1)S(1)} %collective-permute-done.16.refs_3_) | copy-start | bytes 786436
  67.5 0.7 copy-start.12
  68.2 0.7 copy-start.13
  76.3 11.0 %collective-permute-start.17 = (bf16[4,8,128,128]{3,2,1,0:T(8,128)(2,1)}, bf16[4,8,128,128]{3,2,1,0:T(8,128)(2,1)S(1)}, u32[]{:S(2)}, u32[]{:S(2)}) collective-permute-start(bf16[4,8,128,128]{3,2,1,0:T(8,128)(2,1)} %get-tuple-element.27), channel_id=1, source_target_pairs={{0,4},{4,0},{8,12},{12,8},{16,20},{20,16},{24,28},{28,24},{1,5},{5... | collective-permute-start | bytes 3145736 | tf_op jit(solution)/shard_map/ppermute | solution.py:26
  78.2 2.6 %collective-permute-start.10 = (f32[128,128]{1,0:T(8,128)S(1)}, f32[128,128]{1,0:T(8,128)S(1)}, u32[]{:S(2)}, u32[]{:S(2)}) collective-permute-start(f32[128,128]{1,0:T(8,128)S(1)} %copy-done.19), channel_id=1, source_target_pairs={{0,4},{4,0},{8,12},{12,8},{16,20},{20,16},{24,28},{28,24},{1,5},{5... | collective-permute-start | bytes 196616 | tf_op jit(solution)/shard_map/ppermute | solution.py:26
  80.8 14.8 %collective-permute-start.13 = (f32[128,128]{1,0:T(8,128)S(1)}, f32[128,128]{1,0:T(8,128)S(1)}, u32[]{:S(2)}, u32[]{:S(2)}) collective-permute-start(f32[128,128]{1,0:T(8,128)S(1)} %add.24), channel_id=1, source_target_pairs={{0,24},{4,28},{8,16},{12,20},{16,8},{20,12},{24,0},{28,4},{1,25},{... | collective-permute-start | bytes 196616 | tf_op jit(solution)/shard_map/ppermute | solution.py:26
  86.6 9.0 %collective-permute-start.12 = (f32[128,128]{1,0:T(8,128)S(1)}, f32[128,128]{1,0:T(8,128)S(1)}, u32[]{:S(2)}, u32[]{:S(2)}) collective-permute-start(f32[128,128]{1,0:T(8,128)S(1)} %add.24), channel_id=1, source_target_pairs={{0,16},{4,20},{8,24},{12,28},{16,0},{20,4},{24,8},{28,12},{1,17},{... | collective-permute-start | bytes 196616 | tf_op jit(solution)/shard_map/ppermute | solution.py:26
  86.6 9.0 %collective-permute-start.11 = (f32[128,128]{1,0:T(8,128)S(1)}, f32[128,128]{1,0:T(8,128)S(1)}, u32[]{:S(2)}, u32[]{:S(2)}) collective-permute-start(f32[128,128]{1,0:T(8,128)S(1)} %add.24), channel_id=1, source_target_pairs={{0,8},{4,12},{8,0},{12,4},{16,24},{20,28},{24,16},{28,20},{1,9},{5... | collective-permute-start | bytes 196616 | tf_op jit(solution)/shard_map/ppermute | solution.py:26
  87.3 1.0 copy-start
  91.2 21.0 %collective-permute-start.21 = (bf16[8,128,128]{2,1,0:T(8,128)(2,1)}, bf16[8,128,128]{2,1,0:T(8,128)(2,1)S(1)}, u32[]{:S(2)}, u32[]{:S(2)}) collective-permute-start(bf16[8,128,128]{2,1,0:T(8,128)(2,1)} %get-tuple-element.34), channel_id=1, source_target_pairs={{0,8},{4,12},{8,0},{12,4},{16,24},{20,28},{24,16},{28,20},{1,9},{5... | collective-permute-start | bytes 786440 | tf_op jit(solution)/shard_map/ppermute | solution.py:26
  92.6 21.5 %collective-permute-start.22 = (bf16[8,128,128]{2,1,0:T(8,128)(2,1)}, bf16[8,128,128]{2,1,0:T(8,128)(2,1)S(1)}, u32[]{:S(2)}, u32[]{:S(2)}) collective-permute-start(bf16[8,128,128]{2,1,0:T(8,128)(2,1)} %get-tuple-element.35), channel_id=1, source_target_pairs={{0,16},{4,20},{8,24},{12,28},{16,0},{20,4},{24,8},{28,12},{1,17},{... | collective-permute-start | bytes 786440 | tf_op jit(solution)/shard_map/ppermute | solution.py:26
  95.5 18.6 %collective-permute-start.23 = (bf16[8,128,128]{2,1,0:T(8,128)(2,1)}, bf16[8,128,128]{2,1,0:T(8,128)(2,1)S(1)}, u32[]{:S(2)}, u32[]{:S(2)}) collective-permute-start(bf16[8,128,128]{2,1,0:T(8,128)(2,1)} %get-tuple-element.28), channel_id=1, source_target_pairs={{0,24},{4,28},{8,16},{12,20},{16,8},{20,12},{24,0},{28,4},{1,25},{... | collective-permute-start | bytes 786440 | tf_op jit(solution)/shard_map/ppermute | solution.py:26
  95.7 9.5 %copy-start.18 = (f32[128,128]{1,0:T(8,128)}, f32[128,128]{1,0:T(8,128)S(1)}, u32[]{:S(2)}) copy-start(f32[128,128]{1,0:T(8,128)S(1)} %add_add_fusion.1.refs_0_) | copy-start | bytes 196612
  95.7 5.2 %collective-permute-start.20 = (f32[128,128]{1,0:T(8,128)S(1)}, f32[128,128]{1,0:T(8,128)S(1)}, u32[]{:S(2)}, u32[]{:S(2)}) collective-permute-start(f32[128,128]{1,0:T(8,128)S(1)} %add_add_fusion.1.refs_0_), channel_id=1, source_target_pairs={{0,3},{1,2},{2,1},{3,0},{4,7},{5,6},{6,5},{7,4},{8,11},{9,10},{10,... | collective-permute-start | bytes 196616 | tf_op jit(solution)/shard_map/ppermute | solution.py:26
  97.5 4.3 %collective-permute-start.19 = (f32[128,128]{1,0:T(8,128)S(1)}, f32[128,128]{1,0:T(8,128)S(1)}, u32[]{:S(2)}, u32[]{:S(2)}) collective-permute-start(f32[128,128]{1,0:T(8,128)S(1)} %add_add_fusion.1.refs_0_), channel_id=1, source_target_pairs={{0,2},{1,3},{2,0},{3,1},{4,6},{5,7},{6,4},{7,5},{8,10},{9,11},{10,... | collective-permute-start | bytes 196616 | tf_op jit(solution)/shard_map/ppermute | solution.py:26
  100.9 4.3 %copy-start.23 = (f32[128,128]{1,0:T(8,128)}, f32[128,128]{1,0:T(8,128)S(1)}, u32[]{:S(2)}) copy-start(f32[128,128]{1,0:T(8,128)S(1)} %collective-permute-done.20.refs_3_) | copy-start | bytes 196612
  100.9 4.3 %collective-permute-start.18 = (f32[128,128]{1,0:T(8,128)S(1)}, f32[128,128]{1,0:T(8,128)S(1)}, u32[]{:S(2)}, u32[]{:S(2)}) collective-permute-start(f32[128,128]{1,0:T(8,128)S(1)} %add_add_fusion.1.refs_0_), channel_id=1, source_target_pairs={{0,1},{1,0},{2,3},{3,2},{4,5},{5,4},{6,7},{7,6},{8,9},{9,8},{10,11... | collective-permute-start | bytes 196616 | tf_op jit(solution)/shard_map/ppermute | solution.py:26
  101.7 3.4 %copy-start.24 = (f32[128,128]{1,0:T(8,128)}, f32[128,128]{1,0:T(8,128)S(1)}, u32[]{:S(2)}) copy-start(f32[128,128]{1,0:T(8,128)S(1)} %collective-permute-done.19.refs_2_) | copy-start | bytes 196612
  105.2 0.6 copy-start.25
  112.3 1.9 %copy-start.15 = (bf16[8,128,128]{2,1,0:T(8,128)(2,1)}, bf16[8,128,128]{2,1,0:T(8,128)(2,1)S(1)}, u32[]{:S(2)}) copy-start(bf16[8,128,128]{2,1,0:T(8,128)(2,1)S(1)} %collective-permute-done.21.refs_0_) | copy-start | bytes 786436
  114.1 0.7 copy-start.16
  114.2 0.8 copy-start.17
  118.1 1.5 %collective-permute-start.24 = (f32[128,128]{1,0:T(8,128)}, f32[128,128]{1,0:T(8,128)S(1)}, u32[]{:S(2)}, u32[]{:S(2)}) collective-permute-start(f32[128,128]{1,0:T(8,128)} %get-tuple-element.36), channel_id=1, source_target_pairs={{0,4},{4,0},{8,12},{12,8},{16,20},{20,16},{24,28},{28,24},{1,5},{5... | collective-permute-start | bytes 196616 | tf_op jit(solution)/shard_map/ppermute | solution.py:26
  120.4 5.2 %collective-permute-start.27 = (f32[128,128]{1,0:T(8,128)S(1)}, f32[128,128]{1,0:T(8,128)S(1)}, u32[]{:S(2)}, u32[]{:S(2)}) collective-permute-start(f32[128,128]{1,0:T(8,128)S(1)} %add.28), channel_id=1, source_target_pairs={{0,3},{1,2},{2,1},{3,0},{4,7},{5,6},{6,5},{7,4},{8,11},{9,10},{10,... | collective-permute-start | bytes 196616 | tf_op jit(solution)/shard_map/ppermute | solution.py:26
  122.2 4.7 %collective-permute-start.26 = (f32[128,128]{1,0:T(8,128)S(1)}, f32[128,128]{1,0:T(8,128)S(1)}, u32[]{:S(2)}, u32[]{:S(2)}) collective-permute-start(f32[128,128]{1,0:T(8,128)S(1)} %add.28), channel_id=1, source_target_pairs={{0,2},{1,3},{2,0},{3,1},{4,6},{5,7},{6,4},{7,5},{8,10},{9,11},{10,... | collective-permute-start | bytes 196616 | tf_op jit(solution)/shard_map/ppermute | solution.py:26
  122.4 4.9 %collective-permute-start.25 = (f32[128,128]{1,0:T(8,128)S(1)}, f32[128,128]{1,0:T(8,128)S(1)}, u32[]{:S(2)}, u32[]{:S(2)}) collective-permute-start(f32[128,128]{1,0:T(8,128)S(1)} %add.28), channel_id=1, source_target_pairs={{0,1},{1,0},{2,3},{3,2},{4,5},{5,4},{6,7},{7,6},{8,9},{9,8},{10,11... | collective-permute-start | bytes 196616 | tf_op jit(solution)/shard_map/ppermute | solution.py:26
  127.3 10.4 %copy-start.14 = (f32[128,128]{1,0:T(8,128)}, f32[128,128]{1,0:T(8,128)S(1)}, u32[]{:S(2)}) copy-start(f32[128,128]{1,0:T(8,128)S(1)} %add_add_fusion.refs_0_) | copy-start | bytes 196612
  127.3 6.1 %collective-permute-start.30 = (f32[128,128]{1,0:T(8,128)S(1)}, f32[128,128]{1,0:T(8,128)S(1)}, u32[]{:S(2)}, u32[]{:S(2)}) collective-permute-start(f32[128,128]{1,0:T(8,128)S(1)} %add_add_fusion.refs_0_), channel_id=1, source_target_pairs={{0,24},{4,28},{8,16},{12,20},{16,8},{20,12},{24,0},{28,4},{1,25},{... | collective-permute-start | bytes 196616 | tf_op jit(solution)/shard_map/ppermute | solution.py:26
  129.7 7.2 %collective-permute-start.29 = (f32[128,128]{1,0:T(8,128)S(1)}, f32[128,128]{1,0:T(8,128)S(1)}, u32[]{:S(2)}, u32[]{:S(2)}) collective-permute-start(f32[128,128]{1,0:T(8,128)S(1)} %add_add_fusion.refs_0_), channel_id=1, source_target_pairs={{0,16},{4,20},{8,24},{12,28},{16,0},{20,4},{24,8},{28,12},{1,17},{... | collective-permute-start | bytes 196616 | tf_op jit(solution)/shard_map/ppermute | solution.py:26
  133.3 4.4 %collective-permute-start.28 = (f32[128,128]{1,0:T(8,128)S(1)}, f32[128,128]{1,0:T(8,128)S(1)}, u32[]{:S(2)}, u32[]{:S(2)}) collective-permute-start(f32[128,128]{1,0:T(8,128)S(1)} %add_add_fusion.refs_0_), channel_id=1, source_target_pairs={{0,8},{4,12},{8,0},{12,4},{16,24},{20,28},{24,16},{28,20},{1,9},{5... | collective-permute-start | bytes 196616 | tf_op jit(solution)/shard_map/ppermute | solution.py:26
  133.5 4.2 %copy-start.20 = (f32[128,128]{1,0:T(8,128)}, f32[128,128]{1,0:T(8,128)S(1)}, u32[]{:S(2)}) copy-start(f32[128,128]{1,0:T(8,128)S(1)} %collective-permute-done.30.refs_3_) | copy-start | bytes 196612
  137.0 0.7 copy-start.21
  137.7 0.6 copy-start.22

commit v3 on v2

--- a/solution.py
+++ b/solution.py
@@ -7,18 +7,27 @@
 from jax.experimental.pallas import tpu as pltpu
 from jax.sharding import PartitionSpec as P
 
+
 F32 = jnp.float32
 BF16 = jnp.bfloat16
 UNROLL = 32
 STEP = 8
+MARGIN = 4 * 1024 * 1024
 VMEM = pl.BlockSpec(memory_space=pltpu.VMEM)
 SMEM = pl.BlockSpec(memory_space=pltpu.SMEM)
 ANY = pl.BlockSpec(memory_space=pl.ANY)
-HIGH = lax.Precision.HIGHEST
-
-
-def params():
-    return pltpu.CompilerParams(vmem_limit_bytes=60 * 1024 * 1024)
+HBM = pl.BlockSpec(memory_space=pltpu.HBM)
+
+
+def nbytes(item):
+    total = jnp.dtype(item.dtype).itemsize
+    for extent in item.shape:
+        total *= extent
+    return total
+
+
+def params(items):
+    return pltpu.CompilerParams(vmem_limit_bytes=sum(map(nbytes, items)) + MARGIN)
 
 
 def swap(value, axis, mask):
@@ -26,38 +35,26 @@
     return lax.ppermute(value, axis, [(i, i ^ mask) for i in range(size)])
 
 
-def chunk_of(slots):
-    for size in (32, 16, 8):
-        if slots % size == 0:
-            return size
-    return slots
-
-
-def product_body(in_axis, forward, counts, out_index, in_index, values, shards, panel, vbuf, acc, sems):
-    axis_size = len(shards)
+def group_of(slots):
+    return max(size for size in range(1, UNROLL + 1) if slots % size == 0)
+
+
+def product_body(in_axis, forward, counts, lists, values, shards, scratch):
     in_me, count = lax.axis_index(in_axis), counts[0, 0]
-    slots = values.shape[2]
-    chunk = chunk_of(slots)
-    group = min(UNROLL, chunk)
-    chunks = slots // chunk
-    per_shard = panel.shape[0] // axis_size
+    panel, acc, index, sems = scratch
+    per_shard = panel.shape[0] // len(shards)
     out_blocks = acc.shape[0] - 1
-
-    def panel_copy(k):
-        slot = (in_me ^ k) * per_shard
-        return pltpu.make_async_copy(shards[k], panel.at[pl.ds(slot, per_shard)], sems.at[chunks + k])
-
-    def value_copy(c):
-        span = pl.ds(c * chunk, chunk)
-        return pltpu.make_async_copy(values.at[0, 0, span], vbuf.at[span], sems.at[c])
-
-    for k in range(axis_size):
-        panel_copy(k).start()
-    for c in range(chunks):
-        value_copy(c).start()
+    group = group_of(values.shape[0])
+    out_row, in_row = (0, 1) if forward else (1, 0)
+    copies = [pltpu.make_async_copy(lists, index, sems.at[0])]
+    for k, shard in enumerate(shards):
+        place = panel.at[pl.ds((in_me ^ k) * per_shard, per_shard)]
+        copies.append(pltpu.make_async_copy(shard, place, sems.at[k + 1]))
+    for copy in copies:
+        copy.start()
     acc[...] = jnp.zeros_like(acc)
-    for k in range(axis_size):
-        panel_copy(k).wait()
+    for copy in copies:
+        copy.wait()
 
     def one_group(g, carry):
         first = g * group
@@ -65,31 +62,24 @@
         targets = []
         for u in range(group):
             k = first + u
-            block = vbuf[k]
-            piece = panel[in_index[0, 0, k]]
+            block = values[k]
+            piece = panel[index[in_row, k]]
             if forward:
                 products.append(jnp.dot(block, piece, preferred_element_type=F32))
             else:
                 products.append(jnp.dot(piece, block, preferred_element_type=F32))
-            targets.append(jnp.where(k < count, out_index[0, 0, k], out_blocks))
+            targets.append(jnp.where(k < count, index[out_row, k], out_blocks))
         for target, product in zip(targets, products):
             acc[target] += product
         return carry
 
-    def one_chunk(c, carry):
-        value_copy(c).wait()
-        low = c * (chunk // group)
-        live = (count + group - 1) // group
-        high = jnp.clip(live, low, low + chunk // group)
-        return lax.fori_loop(low, high, one_group, carry)
-
-    lax.fori_loop(0, chunks, one_chunk, 0)
-
-
-def left_kernel(row_size, col_size, counts, rows, cols, values, *refs):
+    lax.fori_loop(0, (count + group - 1) // group, one_group, 0)
+
+
+def left_kernel(row_size, col_size, counts, lists, values, *refs):
     shards, outs, scratch = refs[:row_size], refs[row_size:-4], refs[-4:]
-    panel, vbuf, acc, sems = scratch
-    product_body("row", True, counts, rows, cols, values, shards, panel, vbuf, acc, sems)
+    acc = scratch[1]
+    product_body("row", True, counts, lists, values, shards, scratch)
     per = (acc.shape[0] - 1) // col_size
     me = lax.axis_index("col")
     for k in range(col_size):
@@ -97,10 +87,10 @@
         outs[k][...] = part.astype(outs[k].dtype)
 
 
-def right_kernel(row_size, col_size, counts, rows, cols, values, *refs):
+def right_kernel(row_size, col_size, counts, lists, values, *refs):
     shards, (keep, send), scratch = refs[:col_size], refs[col_size:-4], refs[-4:]
-    panel, vbuf, acc, sems = scratch
-    product_body("col", False, counts, cols, rows, values, shards, panel, vbuf, acc, sems)
+    acc = scratch[1]
+    product_body("col", False, counts, lists, values, shards, scratch)
     per = (acc.shape[0] - 1) // row_size
     me = lax.axis_index("row")
     for k in range(0, row_size, 2):
@@ -108,26 +98,32 @@
         send[k // 2] = acc[pl.ds((me ^ (k + 1)) * per, per)].astype(BF16)
 
 
-def run_product(kernel, counts, rows, cols, values, shards, panel_blocks, out_blocks, out_shape):
-    slots, size = values.shape[2], values.shape[-1]
+def run_product(kernel, first, counts, lists, values, shards, panel_blocks, out_blocks, out_shape):
+    slots, size = values.shape[0], values.shape[-1]
     width = shards[0].shape[-1]
-    chunks = slots // chunk_of(slots)
+    held = [
+        pltpu.VMEM((panel_blocks, size, width), BF16),
+        pltpu.VMEM((out_blocks + 1, size, width), F32),
+    ]
     return pl.pallas_call(
         kernel,
         out_shape=out_shape,
-        in_specs=[SMEM, SMEM, SMEM, ANY] + [ANY] * len(shards),
+        in_specs=[SMEM, ANY, VMEM, first] + [ANY] * (len(shards) - 1),
         out_specs=jax.tree.map(lambda _: VMEM, out_shape),
-        scratch_shapes=[
-            pltpu.VMEM((panel_blocks, size, width), BF16),
-            pltpu.VMEM(values.shape[2:], BF16),
-            pltpu.VMEM((out_blocks + 1, size, width), F32),
-            pltpu.SemaphoreType.DMA((chunks + len(shards),)),
-        ],
-        compiler_params=params(),
+        scratch_shapes=held
+        + [pltpu.SMEM(lists.shape, jnp.int32), pltpu.SemaphoreType.DMA((len(shards) + 1,))],
+        compiler_params=params(held + list(out_shape) + [values]),
         cost_estimate=pl.CostEstimate(
             flops=2 * slots * size * size * width, bytes_accessed=2 * values.size, transcendentals=0
         ),
-    )(counts, rows, cols, values, *shards)
+    )(counts, lists, values, *shards)
+
+
+def stage_kernel(rows, cols, values, lists, staged, sem):
+    copy = pltpu.make_async_copy(values.at[0, 0], staged, sem)
+    copy.start()
+    lists[0], lists[1] = rows[0, 0], cols[0, 0]
+    copy.wait()
 
 
 def left_sum_kernel(nodes_total, own, *refs):
@@ -220,7 +216,7 @@
 def factor_of(parts, scratch):
     total = parts[0][...]
     for part in parts[1:]:
-        total = total + part[...]
+        total = total + part[...].astype(F32)
     for t, strip in enumerate(inverse_lower(total)):
         scratch[t * STEP:(t + 1) * STEP, :] = strip
     return scratch[...]
@@ -248,7 +244,6 @@
 def left_factor_kernel(*refs):
     parts, natural, inverse, out = refs[:-3], refs[-3], refs[-2], refs[-1]
     factor = factor_of(parts, inverse)
-    order = factor.shape[0]
     terms = limbs(factor, 3)
     for b in range(natural.shape[0]):
         solved = jnp.zeros(out.shape[1:], F32)
@@ -275,7 +270,7 @@
         in_specs=[VMEM] * len(args),
         out_specs=jax.tree.map(lambda _: VMEM, out_shape),
         scratch_shapes=scratch,
-        compiler_params=params(),
+        compiler_params=params(list(args) + jax.tree.leaves(out_shape) + list(scratch)),
     )(*args)
 
 
@@ -284,7 +279,12 @@
 
 
 def exchange(value, axis, first, step=1):
-    return [value] + [swap(value, axis, k) for k in range(first, lax.axis_size(axis), step)]
+    sent = value.astype(BF16)
+    return [value] + [swap(sent, axis, k) for k in range(first, lax.axis_size(axis), step)]
+
+
+def add_parts(parts):
+    return functools.reduce(lambda total, part: total + part.astype(total.dtype), parts)
 
 
 def gather_row(shard):
@@ -304,7 +304,17 @@
     col_size = lax.axis_size("col")
     nodes_total = group_rows * row_size * col_size
     size = block_values.shape[-1]
-    lists = (block_counts, block_rows, block_cols, block_values)
+    slots = block_values.shape[2]
+    staged = (shape((2, slots), jnp.int32), shape((slots, size, size), BF16))
+    lists, values = pl.pallas_call(
+        stage_kernel,
+        out_shape=staged,
+        in_specs=[VMEM, VMEM, HBM],
+        out_specs=(VMEM, VMEM),
+        scratch_shapes=[pltpu.SemaphoreType.DMA(())],
+        compiler_params=params(staged),
+    )(block_rows, block_cols, block_values)
+    tile = (block_counts, lists, values)
     per = group_rows // size
     row_blocks, col_blocks = per * col_size, per * row_size
     block = (per, size, width)
@@ -312,8 +322,8 @@
 
     shards = gather_row(start_panel.reshape(block))
     parts = run_product(
-        functools.partial(left_kernel, row_size, col_size),
-        *lists, shards, col_blocks, row_blocks,
+        functools.partial(left_kernel, row_size, col_size), HBM,
+        *tile, shards, col_blocks, row_blocks,
         [shape(block, F32)] + [shape(block, BF16)] * (col_size - 1),
     )
     came = [swap(parts[k], "col", k) for k in range(1, col_size)]
@@ -322,13 +332,13 @@
         (shape(block, BF16), shape(block, BF16), square), parts[0], *came,
     )
     turned = exchange(flipped, "col", 1)
-    gram = gram + swap(gram, "row", 1)
-    gram = functools.reduce(jnp.add, exchange(gram, "row", 2, 2))
+    gram = add_parts(exchange(gram + swap(gram, "row", 1), "row", 2, 2))
+    gram, turned = lax.optimization_barrier((gram, turned))
 
     half = (row_size // 2,) + block
     keep, send = run_product(
-        functools.partial(right_kernel, row_size, col_size),
-        *lists, turned, row_blocks, col_blocks,
+        functools.partial(right_kernel, row_size, col_size), ANY,
+        *tile, turned, row_blocks, col_blocks,
         [shape(half, F32), shape(half, BF16)],
     )
     sums = call(
@@ -337,14 +347,13 @@
     )
     came = [swap(sums[k // 2], "row", k) for k in range(2, row_size, 2)]
     gram, _ = lax.optimization_barrier((gram, sums[-1]))
-    inverse, left_panel = call(
-        left_factor_kernel, (square, shape(block, BF16)), *exchange(gram, "col", 1), natural
-    )
+    grams = exchange(gram, "col", 1)
+    inverse, left_panel = call(left_factor_kernel, (square, shape(block, BF16)), *grams, natural)
     right_flipped, gram = call(
         functools.partial(right_sum_kernel, nodes_total), (shape(block, BF16), square), inverse, sums[0], *came
     )
     gram = gram + swap(gram, "row", 1)
-    gram = functools.reduce(jnp.add, exchange(gram, "col", 1))
+    gram = add_parts(exchange(gram, "col", 1))
     right_panel = call(
         right_factor_kernel, shape(block, BF16), *exchange(gram, "row", 2, 2), right_flipped,
         scratch=[pltpu.VMEM((width, width), F32)],

time: 145 us -> 130 us (0.90)
  Pallas kernels: 35.4 us -> 19.9 us
  starting transfers between devices: 39.6 us -> 41.4 us
    pallas_call x5, Pallas kernels: 21.1 us -> 12.3 us  [call(): pl.pallas_call(kernel, out_shape=out_shape, in_specs=[VMEM] * len(args),...]
    pallas_call x2 -> x3, Pallas kernels: 14.3 us -> 7.55 us  [the longest x2 6.77 us: run_product(): pl.pallas_call(kernel, out_shape=out_shape, in_specs=[SMEM, ANY, VMEM, fi...]
    ppermute x31, starting transfers between devices: 39.6 us -> 41.4 us  [swap(): return lax.ppermute(value, axis, [(i, i ^ mask) for i in range(size)])]
    unnamed x52 -> x8, local copies, waits for them, and re-layouts: 5.98 us -> 5.75 us
  transfers between devices with their start and end apart: 31 -> 31, of which waited for: 19 -> 19; matrix products, arithmetic and copies ran while one was open for 0% -> 0% of each run, Pallas kernels for 7% -> 5%
where the time goes in v3:
time: 130 us
  waiting for transfers between devices  61.2 us (47%)
  starting transfers between devices  41.4 us (32%)
  Pallas kernels  19.9 us (15%)
  local copies, waits for them, and re-layouts  5.75 us (4%)
  between operations  1.43 us (1%)
    ppermute x31, waiting for transfers between devices, swap(): return lax.ppermute(value, axis, [(i, i ^ mask) for i in range(size)])  61.2 us
    ppermute x31, starting transfers between devices, swap(): return lax.ppermute(value, axis, [(i, i ^ mask) for i in range(size)])  41.4 us
    pallas_call x5, Pallas kernels, call(): pl.pallas_call(kernel, out_shape=out_shape, in_specs=[VMEM] * len(args),...  12.3 us
    pallas_call x2, Pallas kernels, run_product(): pl.pallas_call(kernel, out_shape=out_shape, in_specs=[SMEM, ANY, VMEM, fi...  6.77 us
    unnamed x8, local copies, waits for them, and re-layouts  5.75 us
  transfers between devices with their start and end apart: 31, of which 19 were waited for; matrix products, arithmetic and copies ran while one was open for 0% of the time, Pallas kernels for 5%

profile of v3, /device:TPU:0, one launch (start us, length us, event | category | flops | bytes accessed | tf_op | source)
XLA Modules:
  0.0 129.7 jit_solution(8130306107265263713)
XLA Ops:
  0.6 4.1 %collective-permute-start.3 = (bf16[8,128,128]{2,1,0:T(8,128)(2,1)}, bf16[8,128,128]{2,1,0:T(8,128)(2,1)S(1)}, u32[]{:S(2)}, u32[]{:S(2)}) collective-permute-start(bf16[8,128,128]{2,1,0:T(8,128)(2,1)} %bitcast.3), channel_id=1, source_target_pairs={{0,16},{4,20},{8,24},{12,28},{16,0},{20,4},{24,8},{28,12},{1,17},{... | collective-permute-start | bytes 786440 | tf_op jit(solution)/shard_map/ppermute | solution.py:35
  4.8 1.6 %collective-permute-start.1 = (bf16[8,128,128]{2,1,0:T(8,128)(2,1)}, bf16[8,128,128]{2,1,0:T(8,128)(2,1)S(1)}, u32[]{:S(2)}, u32[]{:S(2)}) collective-permute-start(bf16[8,128,128]{2,1,0:T(8,128)(2,1)} %bitcast.4), channel_id=1, source_target_pairs={{0,8},{4,12},{8,0},{12,4},{16,24},{20,28},{24,16},{28,20},{1,9},{5... | collective-permute-start | bytes 786440 | tf_op jit(solution)/shard_map/ppermute | solution.py:35
  6.3 10.7 %collective-permute-done.3.refs_4_ = bf16[8,128,128]{2,1,0:T(8,128)(2,1)S(1)} collective-permute-done((bf16[8,128,128]{2,1,0:T(8,128)(2,1)}, bf16[8,128,128]{2,1,0:T(8,128)(2,1)S(1)}, u32[]{:S(2)}, u32[]{:S(2)}) %collective-permute-start.3) | collective-permute-done | bytes 262176 | tf_op jit(solution)/shard_map/ppermute | solution.py:35
  17.0 0.7 collective-permute-start.5
  17.7 0.5 collective-permute-start.4
  18.2 0.0 collective-permute-done.1.refs_2_
  18.2 0.0 collective-permute-start.2
  18.2 6.2 %collective-permute-done.5.refs_6_ = bf16[8,128,128]{2,1,0:T(8,128)(2,1)S(1)} collective-permute-done((bf16[8,128,128]{2,1,0:T(8,128)(2,1)S(1)}, bf16[8,128,128]{2,1,0:T(8,128)(2,1)S(1)}, u32[]{:S(2)}, u32[]{:S(2)}) %collective-permute-start.5) | collective-permute-done | bytes 262176 | tf_op jit(solution)/shard_map/ppermute | solution.py:35
  24.4 0.0 collective-permute-start.6
  25.1 4.3 %copy-done = bf16[1,1,352,128,128]{4,3,2,1,0:T(8,128)(2,1)S(1)} copy-done((bf16[1,1,352,128,128]{4,3,2,1,0:T(8,128)(2,1)S(1)}, bf16[1,1,352,128,128]{4,3,2,1,0:T(8,128)(2,1)}, u32[]{:S(2)}) %copy-start) | copy-done | bytes 11534360
  29.3 0.7 copy-done.2
  30.0 0.7 copy-done.3
  30.7 0.8 shard_map.68
  31.5 0.0 collective-permute-done.refs_1_
  31.5 0.0 collective-permute-done.6.refs_7_
  31.5 0.1 copy-done.1
  31.7 3.2 %shard_map.69 = (f32[8,128,128]{2,1,0:T(8,128)S(1)}, bf16[8,128,128]{2,1,0:T(8,128)(2,1)S(1)}, bf16[8,128,128]{2,1,0:T(8,128)(2,1)S(1)}, bf16[8,128,128]{2,1,0:T(8,128)(2,1)S(1)}) custom-call(s32[1,1]{1,0:T(1,128)S(6)} %copy.7.counts, s32[2,352]{1,0:T(2,128)S(1)} %get-tuple-element.27.lists, bf16[352,128,128]{2,1,0:T(8,128)(2,1)S(1)} %get-tuple-element.28.values, ...), custom_call_target="tpu_custom_call" | custom-call | flops 1476395008 | bytes 11534336 | tf_op jit(solution)/shard_map/pallas_call | solution.py:108
  34.9 1.4 %collective-permute-start.7 = (bf16[8,128,128]{2,1,0:T(8,128)(2,1)S(1)}, bf16[8,128,128]{2,1,0:T(8,128)(2,1)S(1)}, u32[]{:S(2)}, u32[]{:S(2)}) collective-permute-start(bf16[8,128,128]{2,1,0:T(8,128)(2,1)S(1)} %get-tuple-element.30), channel_id=1, source_target_pairs={{0,1},{1,0},{2,3},{3,2},{4,5},{5,4},{6,7},{7,6},{8,9},{9,8},{10,11... | collective-permute-start | bytes 786440 | tf_op jit(solution)/shard_map/ppermute | solution.py:35
  36.2 2.5 %collective-permute-start.8 = (bf16[8,128,128]{2,1,0:T(8,128)(2,1)S(1)}, bf16[8,128,128]{2,1,0:T(8,128)(2,1)S(1)}, u32[]{:S(2)}, u32[]{:S(2)}) collective-permute-start(bf16[8,128,128]{2,1,0:T(8,128)(2,1)S(1)} %get-tuple-element.31), channel_id=1, source_target_pairs={{0,2},{1,3},{2,0},{3,1},{4,6},{5,7},{6,4},{7,5},{8,10},{9,11},{10,... | collective-permute-start | bytes 786440 | tf_op jit(solution)/shard_map/ppermute | solution.py:35
  38.7 0.9 collective-permute-start.9
  39.7 2.0 %collective-permute-done.7.refs_0_ = bf16[8,128,128]{2,1,0:T(8,128)(2,1)S(1)} collective-permute-done((bf16[8,128,128]{2,1,0:T(8,128)(2,1)S(1)}, bf16[8,128,128]{2,1,0:T(8,128)(2,1)S(1)}, u32[]{:S(2)}, u32[]{:S(2)}) %collective-permute-start.7) | collective-permute-done | bytes 262176 | tf_op jit(solution)/shard_map/ppermute | solution.py:35
  41.7 8.7 %collective-permute-done.8.refs_1_ = bf16[8,128,128]{2,1,0:T(8,128)(2,1)S(1)} collective-permute-done((bf16[8,128,128]{2,1,0:T(8,128)(2,1)S(1)}, bf16[8,128,128]{2,1,0:T(8,128)(2,1)S(1)}, u32[]{:S(2)}, u32[]{:S(2)}) %collective-permute-start.8) | collective-permute-done | bytes 262176 | tf_op jit(solution)/shard_map/ppermute | solution.py:35
  50.3 1.9 %collective-permute-done.9.refs_2_ = bf16[8,128,128]{2,1,0:T(8,128)(2,1)S(1)} collective-permute-done((bf16[8,128,128]{2,1,0:T(8,128)(2,1)S(1)}, bf16[8,128,128]{2,1,0:T(8,128)(2,1)S(1)}, u32[]{:S(2)}, u32[]{:S(2)}) %collective-permute-start.9) | collective-permute-done | bytes 262176 | tf_op jit(solution)/shard_map/ppermute | solution.py:35
  52.2 0.3 shard_map.70
  52.6 0.1 collective-permute-start.10
  52.6 1.2 collective-permute-done.10
  53.9 5.0 %collective-permute-start.13 = (bf16[128,128]{1,0:T(8,128)(2,1)S(1)}, bf16[128,128]{1,0:T(8,128)(2,1)S(1)}, u32[]{:S(2)}, u32[]{:S(2)}) collective-permute-start(bf16[128,128]{1,0:T(8,128)(2,1)S(1)} %get-tuple-element.56), channel_id=1, source_target_pairs={{0,24},{4,28},{8,16},{12,20},{16,8},{20,12},{24,0},{28,4},{1,25},{... | collective-permute-start | bytes 98312 | tf_op jit(solution)/shard_map/ppermute | solution.py:35
  58.9 0.6 collective-permute-start.11
  59.6 1.1 collective-permute-start.16
  60.7 0.6 collective-permute-start.15
  61.4 1.7 %collective-permute-start.14 = (bf16[8,128,128]{2,1,0:T(8,128)(2,1)S(1)}, bf16[8,128,128]{2,1,0:T(8,128)(2,1)S(1)}, u32[]{:S(2)}, u32[]{:S(2)}) collective-permute-start(bf16[8,128,128]{2,1,0:T(8,128)(2,1)S(1)} %get-tuple-element.36.refs_0_), channel_id=1, source_target_pairs={{0,1},{1,0},{2,3},{3,2},{4,5},{5,4},{6,7},{7,6},{8,9},{9,8},{10,11... | collective-permute-start | bytes 786440 | tf_op jit(solution)/shard_map/ppermute | solution.py:35
  63.1 0.7 collective-permute-done.12
  63.8 5.9 %collective-permute-done.16.refs_3_ = bf16[8,128,128]{2,1,0:T(8,128)(2,1)S(1)} collective-permute-done((bf16[8,128,128]{2,1,0:T(8,128)(2,1)S(1)}, bf16[8,128,128]{2,1,0:T(8,128)(2,1)S(1)}, u32[]{:S(2)}, u32[]{:S(2)}) %collective-permute-start.16) | collective-permute-done | bytes 262176 | tf_op jit(solution)/shard_map/ppermute | solution.py:35
  69.7 4.2 %collective-permute-done.15.refs_2_ = bf16[8,128,128]{2,1,0:T(8,128)(2,1)S(1)} collective-permute-done((bf16[8,128,128]{2,1,0:T(8,128)(2,1)S(1)}, bf16[8,128,128]{2,1,0:T(8,128)(2,1)S(1)}, u32[]{:S(2)}, u32[]{:S(2)}) %collective-permute-start.15) | collective-permute-done | bytes 262176 | tf_op jit(solution)/shard_map/ppermute | solution.py:35
  73.9 3.6 %shard_map.71 = (f32[4,8,128,128]{3,2,1,0:T(8,128)S(1)}, bf16[4,8,128,128]{3,2,1,0:T(8,128)(2,1)S(1)}) custom-call(s32[1,1]{1,0:T(1,128)S(6)} %copy.7.counts, s32[2,352]{1,0:T(2,128)S(1)} %get-tuple-element.27.lists, bf16[352,128,128]{2,1,0:T(8,128)(2,1)S(1)} %get-tuple-element.28.values, bf16[8,128,128]{2,1,0:T(8,128)(2,1)S(1)} %get-tuple-element.36.refs_0_, ...), custom_call_target="tpu_custom_call" | custom-call | flops 1476395008 | bytes 11534336 | tf_op jit(solution)/shard_map/pallas_call | solution.py:108
  77.4 3.0 %collective-permute-start.17 = (bf16[4,8,128,128]{3,2,1,0:T(8,128)(2,1)S(1)}, bf16[4,8,128,128]{3,2,1,0:T(8,128)(2,1)S(1)}, u32[]{:S(2)}, u32[]{:S(2)}) collective-permute-start(bf16[4,8,128,128]{3,2,1,0:T(8,128)(2,1)S(1)} %get-tuple-element.41), channel_id=1, source_target_pairs={{0,4},{4,0},{8,12},{12,8},{16,20},{20,16},{24,28},{28,24},{1,5},{5... | collective-permute-start | bytes 3145736 | tf_op jit(solution)/shard_map/ppermute | solution.py:35
  80.4 2.3 %collective-permute-done.17.came = bf16[4,8,128,128]{3,2,1,0:T(8,128)(2,1)S(1)} collective-permute-done((bf16[4,8,128,128]{3,2,1,0:T(8,128)(2,1)S(1)}, bf16[4,8,128,128]{3,2,1,0:T(8,128)(2,1)S(1)}, u32[]{:S(2)}, u32[]{:S(2)}) %collective-permute-start.17) | collective-permute-done | bytes 1048608 | tf_op jit(solution)/shard_map/ppermute | solution.py:35
  82.7 0.2 shard_map.72
  82.9 0.9 collective-permute-start.21
  83.8 1.2 collective-permute-start.22
  85.0 2.4 %collective-permute-start.23 = (bf16[8,128,128]{2,1,0:T(8,128)(2,1)S(1)}, bf16[8,128,128]{2,1,0:T(8,128)(2,1)S(1)}, u32[]{:S(2)}, u32[]{:S(2)}) collective-permute-start(bf16[8,128,128]{2,1,0:T(8,128)(2,1)S(1)} %get-tuple-element.42), channel_id=1, source_target_pairs={{0,24},{4,28},{8,16},{12,20},{16,8},{20,12},{24,0},{28,4},{1,25},{... | collective-permute-start | bytes 786440 | tf_op jit(solution)/shard_map/ppermute | solution.py:35
  87.4 0.7 collective-permute-start.20
  88.1 0.9 collective-permute-start.19
  89.0 3.3 %collective-permute-done.20.refs_3_ = bf16[128,128]{1,0:T(8,128)(2,1)S(1)} collective-permute-done((bf16[128,128]{1,0:T(8,128)(2,1)S(1)}, bf16[128,128]{1,0:T(8,128)(2,1)S(1)}, u32[]{:S(2)}, u32[]{:S(2)}) %collective-permute-start.20) | collective-permute-done | bytes 32800 | tf_op jit(solution)/shard_map/ppermute | solution.py:35
  92.3 0.0 collective-permute-start.18
  92.3 0.0 collective-permute-done.19.refs_2_
  92.4 3.8 %collective-permute-done.18.refs_1_ = bf16[128,128]{1,0:T(8,128)(2,1)S(1)} collective-permute-done((bf16[128,128]{1,0:T(8,128)(2,1)S(1)}, bf16[128,128]{1,0:T(8,128)(2,1)S(1)}, u32[]{:S(2)}, u32[]{:S(2)}) %collective-permute-start.18) | collective-permute-done | bytes 32800 | tf_op jit(solution)/shard_map/ppermute | solution.py:35
  96.2 5.4 %shard_map.73 = (f32[128,128]{1,0:T(8,128)S(1)}, bf16[8,128,128]{2,1,0:T(8,128)(2,1)}) custom-call(f32[128,128]{1,0:T(8,128)S(1)} %convert_add_fusion.1.refs_0_, bf16[128,128]{1,0:T(8,128)(2,1)S(1)} %collective-permute-done.18.refs_1_, bf16[128,128]{1,0:T(8,128)(2,1)S(1)} %collective-permute-done.19.refs_2_, ...), custom_call_target="tpu_custom_call" | custom-call | tf_op jit(solution)/shard_map/pallas_call | solution.py:267
  101.6 3.5 %collective-permute-done.22.refs_1_ = bf16[8,128,128]{2,1,0:T(8,128)(2,1)S(1)} collective-permute-done((bf16[8,128,128]{2,1,0:T(8,128)(2,1)S(1)}, bf16[8,128,128]{2,1,0:T(8,128)(2,1)S(1)}, u32[]{:S(2)}, u32[]{:S(2)}) %collective-permute-start.22) | collective-permute-done | bytes 262176 | tf_op jit(solution)/shard_map/ppermute | solution.py:35
  105.1 1.2 shard_map.74
  106.3 0.1 collective-permute-start.24
  106.4 1.2 collective-permute-done.24
  107.7 1.2 collective-permute-start.27
  108.9 0.5 collective-permute-start.26
  109.5 1.8 %collective-permute-start.25 = (bf16[128,128]{1,0:T(8,128)(2,1)S(1)}, bf16[128,128]{1,0:T(8,128)(2,1)S(1)}, u32[]{:S(2)}, u32[]{:S(2)}) collective-permute-start(bf16[128,128]{1,0:T(8,128)(2,1)S(1)} %get-tuple-element.54), channel_id=1, source_target_pairs={{0,1},{1,0},{2,3},{3,2},{4,5},{5,4},{6,7},{7,6},{8,9},{9,8},{10,11... | collective-permute-start | bytes 98312 | tf_op jit(solution)/shard_map/ppermute | solution.py:35
  111.2 1.3 %collective-permute-done.27 = bf16[128,128]{1,0:T(8,128)(2,1)S(1)} collective-permute-done((bf16[128,128]{1,0:T(8,128)(2,1)S(1)}, bf16[128,128]{1,0:T(8,128)(2,1)S(1)}, u32[]{:S(2)}, u32[]{:S(2)}) %collective-permute-start.27) | collective-permute-done | bytes 32800 | tf_op jit(solution)/shard_map/ppermute | solution.py:35
  112.6 0.4 collective-permute-done.26
  112.9 0.5 collective-permute-done.25
  113.4 3.5 %collective-permute-start.30 = (bf16[128,128]{1,0:T(8,128)(2,1)S(1)}, bf16[128,128]{1,0:T(8,128)(2,1)S(1)}, u32[]{:S(2)}, u32[]{:S(2)}) collective-permute-start(bf16[128,128]{1,0:T(8,128)(2,1)S(1)} %get-tuple-element.52), channel_id=1, source_target_pairs={{0,24},{4,28},{8,16},{12,20},{16,8},{20,12},{24,0},{28,4},{1,25},{... | collective-permute-start | bytes 98312 | tf_op jit(solution)/shard_map/ppermute | solution.py:35
  116.9 3.7 %collective-permute-start.29 = (bf16[128,128]{1,0:T(8,128)(2,1)S(1)}, bf16[128,128]{1,0:T(8,128)(2,1)S(1)}, u32[]{:S(2)}, u32[]{:S(2)}) collective-permute-start(bf16[128,128]{1,0:T(8,128)(2,1)S(1)} %get-tuple-element.52), channel_id=1, source_target_pairs={{0,16},{4,20},{8,24},{12,28},{16,0},{20,4},{24,8},{28,12},{1,17},{... | collective-permute-start | bytes 98312 | tf_op jit(solution)/shard_map/ppermute | solution.py:35
  120.7 0.5 collective-permute-start.28
  121.1 2.0 %collective-permute-done.29.refs_2_ = bf16[128,128]{1,0:T(8,128)(2,1)S(1)} collective-permute-done((bf16[128,128]{1,0:T(8,128)(2,1)S(1)}, bf16[128,128]{1,0:T(8,128)(2,1)S(1)}, u32[]{:S(2)}, u32[]{:S(2)}) %collective-permute-start.29) | collective-permute-done | bytes 32800 | tf_op jit(solution)/shard_map/ppermute | solution.py:35
  123.2 1.4 %collective-permute-done.28.refs_1_ = bf16[128,128]{1,0:T(8,128)(2,1)S(1)} collective-permute-done((bf16[128,128]{1,0:T(8,128)(2,1)S(1)}, bf16[128,128]{1,0:T(8,128)(2,1)S(1)}, u32[]{:S(2)}, u32[]{:S(2)}) %collective-permute-start.28) | collective-permute-done | bytes 32800 | tf_op jit(solution)/shard_map/ppermute | solution.py:35
  124.6 5.1 %shard_map.75 = bf16[8,128,128]{2,1,0:T(8,128)(2,1)} custom-call(f32[128,128]{1,0:T(8,128)S(1)} %get-tuple-element.53.refs_0_, bf16[128,128]{1,0:T(8,128)(2,1)S(1)} %collective-permute-done.28.refs_1_, bf16[128,128]{1,0:T(8,128)(2,1)S(1)} %collective-permute-done.29.refs_2_, bf16[128,128]{1,0:T(8,128)(2,1)S(1)} %collective-permute-done.30.refs_3_, ...), custom_call_target="tpu_custom_call" | custom-call | tf_op jit(solution)/shard_map/pallas_call | solution.py:267
  (19 shorter events, 0.1 us)
Async XLA Ops:
  0.6 16.4 %collective-permute-start.3 = (bf16[8,128,128]{2,1,0:T(8,128)(2,1)}, bf16[8,128,128]{2,1,0:T(8,128)(2,1)S(1)}, u32[]{:S(2)}, u32[]{:S(2)}) collective-permute-start(bf16[8,128,128]{2,1,0:T(8,128)(2,1)} %bitcast.3), channel_id=1, source_target_pairs={{0,16},{4,20},{8,24},{12,28},{16,0},{20,4},{24,8},{28,12},{1,17},{... | collective-permute-start | bytes 786440 | tf_op jit(solution)/shard_map/ppermute | solution.py:35
  4.8 13.5 %collective-permute-start.1 = (bf16[8,128,128]{2,1,0:T(8,128)(2,1)}, bf16[8,128,128]{2,1,0:T(8,128)(2,1)S(1)}, u32[]{:S(2)}, u32[]{:S(2)}) collective-permute-start(bf16[8,128,128]{2,1,0:T(8,128)(2,1)} %bitcast.4), channel_id=1, source_target_pairs={{0,8},{4,12},{8,0},{12,4},{16,24},{20,28},{24,16},{28,20},{1,9},{5... | collective-permute-start | bytes 786440 | tf_op jit(solution)/shard_map/ppermute | solution.py:35
  17.0 7.4 %collective-permute-start.5 = (bf16[8,128,128]{2,1,0:T(8,128)(2,1)S(1)}, bf16[8,128,128]{2,1,0:T(8,128)(2,1)S(1)}, u32[]{:S(2)}, u32[]{:S(2)}) collective-permute-start(bf16[8,128,128]{2,1,0:T(8,128)(2,1)S(1)} %collective-permute-done.3.refs_4_), channel_id=1, source_target_pairs={{0,8},{4,12},{8,0},{12,4},{16,24},{20,28},{24,16},{28,20},{1,9},{5... | collective-permute-start | bytes 786440 | tf_op jit(solution)/shard_map/ppermute | solution.py:35
  17.7 13.8 %collective-permute-start = (bf16[8,128,128]{2,1,0:T(8,128)(2,1)}, bf16[8,128,128]{2,1,0:T(8,128)(2,1)S(1)}, u32[]{:S(2)}, u32[]{:S(2)}) collective-permute-start(bf16[8,128,128]{2,1,0:T(8,128)(2,1)} %bitcast.5), channel_id=1, source_target_pairs={{0,4},{4,0},{8,12},{12,8},{16,20},{20,16},{24,28},{28,24},{1,5},{5... | collective-permute-start | bytes 786440 | tf_op jit(solution)/shard_map/ppermute | solution.py:35
  17.7 13.8 %collective-permute-start.4 = (bf16[8,128,128]{2,1,0:T(8,128)(2,1)S(1)}, bf16[8,128,128]{2,1,0:T(8,128)(2,1)S(1)}, u32[]{:S(2)}, u32[]{:S(2)}) collective-permute-start(bf16[8,128,128]{2,1,0:T(8,128)(2,1)S(1)} %collective-permute-done.3.refs_4_), channel_id=1, source_target_pairs={{0,4},{4,0},{8,12},{12,8},{16,20},{20,16},{24,28},{28,24},{1,5},{5... | collective-permute-start | bytes 786440 | tf_op jit(solution)/shard_map/ppermute | solution.py:35
  18.2 13.3 %collective-permute-start.2 = (bf16[8,128,128]{2,1,0:T(8,128)(2,1)S(1)}, bf16[8,128,128]{2,1,0:T(8,128)(2,1)S(1)}, u32[]{:S(2)}, u32[]{:S(2)}) collective-permute-start(bf16[8,128,128]{2,1,0:T(8,128)(2,1)S(1)} %collective-permute-done.1.refs_2_), channel_id=1, source_target_pairs={{0,4},{4,0},{8,12},{12,8},{16,20},{20,16},{24,28},{28,24},{1,5},{5... | collective-permute-start | bytes 786440 | tf_op jit(solution)/shard_map/ppermute | solution.py:35
  24.4 7.1 %collective-permute-start.6 = (bf16[8,128,128]{2,1,0:T(8,128)(2,1)S(1)}, bf16[8,128,128]{2,1,0:T(8,128)(2,1)S(1)}, u32[]{:S(2)}, u32[]{:S(2)}) collective-permute-start(bf16[8,128,128]{2,1,0:T(8,128)(2,1)S(1)} %collective-permute-done.5.refs_6_), channel_id=1, source_target_pairs={{0,4},{4,0},{8,12},{12,8},{16,20},{20,16},{24,28},{28,24},{1,5},{5... | collective-permute-start | bytes 786440 | tf_op jit(solution)/shard_map/ppermute | solution.py:35
  25.1 4.3 %copy-start = (bf16[1,1,352,128,128]{4,3,2,1,0:T(8,128)(2,1)S(1)}, bf16[1,1,352,128,128]{4,3,2,1,0:T(8,128)(2,1)}, u32[]{:S(2)}) copy-start(bf16[1,1,352,128,128]{4,3,2,1,0:T(8,128)(2,1)} %values.1) | copy-start | bytes 34603012
  29.3 0.7 copy-start.2
  30.0 0.7 copy-start.3
  30.7 0.9 copy-start.1
  34.9 6.8 %collective-permute-start.7 = (bf16[8,128,128]{2,1,0:T(8,128)(2,1)S(1)}, bf16[8,128,128]{2,1,0:T(8,128)(2,1)S(1)}, u32[]{:S(2)}, u32[]{:S(2)}) collective-permute-start(bf16[8,128,128]{2,1,0:T(8,128)(2,1)S(1)} %get-tuple-element.30), channel_id=1, source_target_pairs={{0,1},{1,0},{2,3},{3,2},{4,5},{5,4},{6,7},{7,6},{8,9},{9,8},{10,11... | collective-permute-start | bytes 786440 | tf_op jit(solution)/shard_map/ppermute | solution.py:35
  36.2 14.1 %collective-permute-start.8 = (bf16[8,128,128]{2,1,0:T(8,128)(2,1)S(1)}, bf16[8,128,128]{2,1,0:T(8,128)(2,1)S(1)}, u32[]{:S(2)}, u32[]{:S(2)}) collective-permute-start(bf16[8,128,128]{2,1,0:T(8,128)(2,1)S(1)} %get-tuple-element.31), channel_id=1, source_target_pairs={{0,2},{1,3},{2,0},{3,1},{4,6},{5,7},{6,4},{7,5},{8,10},{9,11},{10,... | collective-permute-start | bytes 786440 | tf_op jit(solution)/shard_map/ppermute | solution.py:35
  38.7 13.5 %collective-permute-start.9 = (bf16[8,128,128]{2,1,0:T(8,128)(2,1)S(1)}, bf16[8,128,128]{2,1,0:T(8,128)(2,1)S(1)}, u32[]{:S(2)}, u32[]{:S(2)}) collective-permute-start(bf16[8,128,128]{2,1,0:T(8,128)(2,1)S(1)} %get-tuple-element.32), channel_id=1, source_target_pairs={{0,3},{1,2},{2,1},{3,0},{4,7},{5,6},{6,5},{7,4},{8,11},{9,10},{10,... | collective-permute-start | bytes 786440 | tf_op jit(solution)/shard_map/ppermute | solution.py:35
  52.6 1.3 %collective-permute-start.10 = (f32[128,128]{1,0:T(8,128)S(1)}, f32[128,128]{1,0:T(8,128)S(1)}, u32[]{:S(2)}, u32[]{:S(2)}) collective-permute-start(f32[128,128]{1,0:T(8,128)S(1)} %get-tuple-element.33), channel_id=1, source_target_pairs={{0,4},{4,0},{8,12},{12,8},{16,20},{20,16},{24,28},{28,24},{1,5},{5... | collective-permute-start | bytes 196616 | tf_op jit(solution)/shard_map/ppermute | solution.py:35
  53.9 7.5 %collective-permute-start.13 = (bf16[128,128]{1,0:T(8,128)(2,1)S(1)}, bf16[128,128]{1,0:T(8,128)(2,1)S(1)}, u32[]{:S(2)}, u32[]{:S(2)}) collective-permute-start(bf16[128,128]{1,0:T(8,128)(2,1)S(1)} %get-tuple-element.56), channel_id=1, source_target_pairs={{0,24},{4,28},{8,16},{12,20},{16,8},{20,12},{24,0},{28,4},{1,25},{... | collective-permute-start | bytes 98312 | tf_op jit(solution)/shard_map/ppermute | solution.py:35
  58.9 4.8 %collective-permute-start.12 = (bf16[128,128]{1,0:T(8,128)(2,1)S(1)}, bf16[128,128]{1,0:T(8,128)(2,1)S(1)}, u32[]{:S(2)}, u32[]{:S(2)}) collective-permute-start(bf16[128,128]{1,0:T(8,128)(2,1)S(1)} %get-tuple-element.56), channel_id=1, source_target_pairs={{0,16},{4,20},{8,24},{12,28},{16,0},{20,4},{24,8},{28,12},{1,17},{... | collective-permute-start | bytes 98312 | tf_op jit(solution)/shard_map/ppermute | solution.py:35
  58.9 4.8 %collective-permute-start.11 = (bf16[128,128]{1,0:T(8,128)(2,1)S(1)}, bf16[128,128]{1,0:T(8,128)(2,1)S(1)}, u32[]{:S(2)}, u32[]{:S(2)}) collective-permute-start(bf16[128,128]{1,0:T(8,128)(2,1)S(1)} %get-tuple-element.56), channel_id=1, source_target_pairs={{0,8},{4,12},{8,0},{12,4},{16,24},{20,28},{24,16},{28,20},{1,9},{5... | collective-permute-start | bytes 98312 | tf_op jit(solution)/shard_map/ppermute | solution.py:35
  59.6 10.1 %collective-permute-start.16 = (bf16[8,128,128]{2,1,0:T(8,128)(2,1)S(1)}, bf16[8,128,128]{2,1,0:T(8,128)(2,1)S(1)}, u32[]{:S(2)}, u32[]{:S(2)}) collective-permute-start(bf16[8,128,128]{2,1,0:T(8,128)(2,1)S(1)} %get-tuple-element.36.refs_0_), channel_id=1, source_target_pairs={{0,3},{1,2},{2,1},{3,0},{4,7},{5,6},{6,5},{7,4},{8,11},{9,10},{10,... | collective-permute-start | bytes 786440 | tf_op jit(solution)/shard_map/ppermute | solution.py:35
  60.7 13.1 %collective-permute-start.15 = (bf16[8,128,128]{2,1,0:T(8,128)(2,1)S(1)}, bf16[8,128,128]{2,1,0:T(8,128)(2,1)S(1)}, u32[]{:S(2)}, u32[]{:S(2)}) collective-permute-start(bf16[8,128,128]{2,1,0:T(8,128)(2,1)S(1)} %get-tuple-element.36.refs_0_), channel_id=1, source_target_pairs={{0,2},{1,3},{2,0},{3,1},{4,6},{5,7},{6,4},{7,5},{8,10},{9,11},{10,... | collective-permute-start | bytes 786440 | tf_op jit(solution)/shard_map/ppermute | solution.py:35
  61.4 12.5 %collective-permute-start.14 = (bf16[8,128,128]{2,1,0:T(8,128)(2,1)S(1)}, bf16[8,128,128]{2,1,0:T(8,128)(2,1)S(1)}, u32[]{:S(2)}, u32[]{:S(2)}) collective-permute-start(bf16[8,128,128]{2,1,0:T(8,128)(2,1)S(1)} %get-tuple-element.36.refs_0_), channel_id=1, source_target_pairs={{0,1},{1,0},{2,3},{3,2},{4,5},{5,4},{6,7},{7,6},{8,9},{9,8},{10,11... | collective-permute-start | bytes 786440 | tf_op jit(solution)/shard_map/ppermute | solution.py:35
  77.4 5.3 %collective-permute-start.17 = (bf16[4,8,128,128]{3,2,1,0:T(8,128)(2,1)S(1)}, bf16[4,8,128,128]{3,2,1,0:T(8,128)(2,1)S(1)}, u32[]{:S(2)}, u32[]{:S(2)}) collective-permute-start(bf16[4,8,128,128]{3,2,1,0:T(8,128)(2,1)S(1)} %get-tuple-element.41), channel_id=1, source_target_pairs={{0,4},{4,0},{8,12},{12,8},{16,20},{20,16},{24,28},{28,24},{1,5},{5... | collective-permute-start | bytes 3145736 | tf_op jit(solution)/shard_map/ppermute | solution.py:35
  82.9 18.7 %collective-permute-start.21 = (bf16[8,128,128]{2,1,0:T(8,128)(2,1)S(1)}, bf16[8,128,128]{2,1,0:T(8,128)(2,1)S(1)}, u32[]{:S(2)}, u32[]{:S(2)}) collective-permute-start(bf16[8,128,128]{2,1,0:T(8,128)(2,1)S(1)} %get-tuple-element.48), channel_id=1, source_target_pairs={{0,8},{4,12},{8,0},{12,4},{16,24},{20,28},{24,16},{28,20},{1,9},{5... | collective-permute-start | bytes 786440 | tf_op jit(solution)/shard_map/ppermute | solution.py:35
  83.8 21.3 %collective-permute-start.22 = (bf16[8,128,128]{2,1,0:T(8,128)(2,1)S(1)}, bf16[8,128,128]{2,1,0:T(8,128)(2,1)S(1)}, u32[]{:S(2)}, u32[]{:S(2)}) collective-permute-start(bf16[8,128,128]{2,1,0:T(8,128)(2,1)S(1)} %get-tuple-element.49), channel_id=1, source_target_pairs={{0,16},{4,20},{8,24},{12,28},{16,0},{20,4},{24,8},{28,12},{1,17},{... | collective-permute-start | bytes 786440 | tf_op jit(solution)/shard_map/ppermute | solution.py:35
  85.0 20.2 %collective-permute-start.23 = (bf16[8,128,128]{2,1,0:T(8,128)(2,1)S(1)}, bf16[8,128,128]{2,1,0:T(8,128)(2,1)S(1)}, u32[]{:S(2)}, u32[]{:S(2)}) collective-permute-start(bf16[8,128,128]{2,1,0:T(8,128)(2,1)S(1)} %get-tuple-element.42), channel_id=1, source_target_pairs={{0,24},{4,28},{8,16},{12,20},{16,8},{20,12},{24,0},{28,4},{1,25},{... | collective-permute-start | bytes 786440 | tf_op jit(solution)/shard_map/ppermute | solution.py:35
  87.4 4.9 %collective-permute-start.20 = (bf16[128,128]{1,0:T(8,128)(2,1)S(1)}, bf16[128,128]{1,0:T(8,128)(2,1)S(1)}, u32[]{:S(2)}, u32[]{:S(2)}) collective-permute-start(bf16[128,128]{1,0:T(8,128)(2,1)S(1)} %convert_element_type.34), channel_id=1, source_target_pairs={{0,3},{1,2},{2,1},{3,0},{4,7},{5,6},{6,5},{7,4},{8,11},{9,10},{10,... | collective-permute-start | bytes 98312 | tf_op jit(solution)/shard_map/ppermute | solution.py:35
  88.1 4.3 %collective-permute-start.19 = (bf16[128,128]{1,0:T(8,128)(2,1)S(1)}, bf16[128,128]{1,0:T(8,128)(2,1)S(1)}, u32[]{:S(2)}, u32[]{:S(2)}) collective-permute-start(bf16[128,128]{1,0:T(8,128)(2,1)S(1)} %convert_element_type.34), channel_id=1, source_target_pairs={{0,2},{1,3},{2,0},{3,1},{4,6},{5,7},{6,4},{7,5},{8,10},{9,11},{10,... | collective-permute-start | bytes 98312 | tf_op jit(solution)/shard_map/ppermute | solution.py:35
  92.3 3.9 %collective-permute-start.18 = (bf16[128,128]{1,0:T(8,128)(2,1)S(1)}, bf16[128,128]{1,0:T(8,128)(2,1)S(1)}, u32[]{:S(2)}, u32[]{:S(2)}) collective-permute-start(bf16[128,128]{1,0:T(8,128)(2,1)S(1)} %convert_element_type.34), channel_id=1, source_target_pairs={{0,1},{1,0},{2,3},{3,2},{4,5},{5,4},{6,7},{7,6},{8,9},{9,8},{10,11... | collective-permute-start | bytes 98312 | tf_op jit(solution)/shard_map/ppermute | solution.py:35
  106.3 1.3 %collective-permute-start.24 = (f32[128,128]{1,0:T(8,128)S(1)}, f32[128,128]{1,0:T(8,128)S(1)}, u32[]{:S(2)}, u32[]{:S(2)}) collective-permute-start(f32[128,128]{1,0:T(8,128)S(1)} %get-tuple-element.50), channel_id=1, source_target_pairs={{0,4},{4,0},{8,12},{12,8},{16,20},{20,16},{24,28},{28,24},{1,5},{5... | collective-permute-start | bytes 196616 | tf_op jit(solution)/shard_map/ppermute | solution.py:35
  107.7 4.9 %collective-permute-start.27 = (bf16[128,128]{1,0:T(8,128)(2,1)S(1)}, bf16[128,128]{1,0:T(8,128)(2,1)S(1)}, u32[]{:S(2)}, u32[]{:S(2)}) collective-permute-start(bf16[128,128]{1,0:T(8,128)(2,1)S(1)} %get-tuple-element.54), channel_id=1, source_target_pairs={{0,3},{1,2},{2,1},{3,0},{4,7},{5,6},{6,5},{7,4},{8,11},{9,10},{10,... | collective-permute-start | bytes 98312 | tf_op jit(solution)/shard_map/ppermute | solution.py:35
  108.9 4.0 %collective-permute-start.26 = (bf16[128,128]{1,0:T(8,128)(2,1)S(1)}, bf16[128,128]{1,0:T(8,128)(2,1)S(1)}, u32[]{:S(2)}, u32[]{:S(2)}) collective-permute-start(bf16[128,128]{1,0:T(8,128)(2,1)S(1)} %get-tuple-element.54), channel_id=1, source_target_pairs={{0,2},{1,3},{2,0},{3,1},{4,6},{5,7},{6,4},{7,5},{8,10},{9,11},{10,... | collective-permute-start | bytes 98312 | tf_op jit(solution)/shard_map/ppermute | solution.py:35
  109.5 3.9 %collective-permute-start.25 = (bf16[128,128]{1,0:T(8,128)(2,1)S(1)}, bf16[128,128]{1,0:T(8,128)(2,1)S(1)}, u32[]{:S(2)}, u32[]{:S(2)}) collective-permute-start(bf16[128,128]{1,0:T(8,128)(2,1)S(1)} %get-tuple-element.54), channel_id=1, source_target_pairs={{0,1},{1,0},{2,3},{3,2},{4,5},{5,4},{6,7},{7,6},{8,9},{9,8},{10,11... | collective-permute-start | bytes 98312 | tf_op jit(solution)/shard_map/ppermute | solution.py:35
  113.4 7.7 %collective-permute-start.30 = (bf16[128,128]{1,0:T(8,128)(2,1)S(1)}, bf16[128,128]{1,0:T(8,128)(2,1)S(1)}, u32[]{:S(2)}, u32[]{:S(2)}) collective-permute-start(bf16[128,128]{1,0:T(8,128)(2,1)S(1)} %get-tuple-element.52), channel_id=1, source_target_pairs={{0,24},{4,28},{8,16},{12,20},{16,8},{20,12},{24,0},{28,4},{1,25},{... | collective-permute-start | bytes 98312 | tf_op jit(solution)/shard_map/ppermute | solution.py:35
  116.9 6.2 %collective-permute-start.29 = (bf16[128,128]{1,0:T(8,128)(2,1)S(1)}, bf16[128,128]{1,0:T(8,128)(2,1)S(1)}, u32[]{:S(2)}, u32[]{:S(2)}) collective-permute-start(bf16[128,128]{1,0:T(8,128)(2,1)S(1)} %get-tuple-element.52), channel_id=1, source_target_pairs={{0,16},{4,20},{8,24},{12,28},{16,0},{20,4},{24,8},{28,12},{1,17},{... | collective-permute-start | bytes 98312 | tf_op jit(solution)/shard_map/ppermute | solution.py:35
  120.7 3.9 %collective-permute-start.28 = (bf16[128,128]{1,0:T(8,128)(2,1)S(1)}, bf16[128,128]{1,0:T(8,128)(2,1)S(1)}, u32[]{:S(2)}, u32[]{:S(2)}) collective-permute-start(bf16[128,128]{1,0:T(8,128)(2,1)S(1)} %get-tuple-element.52), channel_id=1, source_target_pairs={{0,8},{4,12},{8,0},{12,4},{16,24},{20,28},{24,16},{28,20},{1,9},{5... | collective-permute-start | bytes 98312 | tf_op jit(solution)/shard_map/ppermute | solution.py:35

commit v4 on v3

--- a/solution.py
+++ b/solution.py
@@ -42,14 +42,17 @@
 def product_body(in_axis, forward, counts, lists, values, shards, scratch):
     in_me, count = lax.axis_index(in_axis), counts[0, 0]
     panel, acc, index, sems = scratch
-    per_shard = panel.shape[0] // len(shards)
     out_blocks = acc.shape[0] - 1
     group = group_of(values.shape[0])
     out_row, in_row = (0, 1) if forward else (1, 0)
     copies = [pltpu.make_async_copy(lists, index, sems.at[0])]
-    for k, shard in enumerate(shards):
-        place = panel.at[pl.ds((in_me ^ k) * per_shard, per_shard)]
-        copies.append(pltpu.make_async_copy(shard, place, sems.at[k + 1]))
+    for k, pieces in enumerate(shards):
+        length = sum(piece.shape[0] for piece in pieces)
+        first = (in_me ^ k) * length
+        for piece in pieces:
+            place = panel.at[pl.ds(first, piece.shape[0])]
+            copies.append(pltpu.make_async_copy(piece, place, sems.at[len(copies)]))
+            first = first + piece.shape[0]
     for copy in copies:
         copy.start()
     acc[...] = jnp.zeros_like(acc)
@@ -76,8 +79,25 @@
     lax.fori_loop(0, (count + group - 1) // group, one_group, 0)
 
 
-def left_kernel(row_size, col_size, counts, lists, values, *refs):
-    shards, outs, scratch = refs[:row_size], refs[row_size:-4], refs[-4:]
+def nested(form, refs):
+    refs = iter(refs)
+    return [[next(refs) for _ in range(pieces)] for pieces in form]
+
+
+def halves(value):
+    middle = value.shape[0] // 2
+    return [value[:middle], value[middle:]] if middle else [value]
+
+
+def block_of(pieces, b):
+    for piece in pieces:
+        if b < piece.shape[0]:
+            return piece[b].astype(F32)
+        b -= piece.shape[0]
+
+
+def left_kernel(form, col_size, counts, lists, values, *refs):
+    shards, outs, scratch = nested(form, refs), refs[sum(form):-4], refs[-4:]
     acc = scratch[1]
     product_body("row", True, counts, lists, values, shards, scratch)
     per = (acc.shape[0] - 1) // col_size
@@ -87,8 +107,8 @@
         outs[k][...] = part.astype(outs[k].dtype)
 
 
-def right_kernel(row_size, col_size, counts, lists, values, *refs):
-    shards, (keep, send), scratch = refs[:col_size], refs[col_size:-4], refs[-4:]
+def right_kernel(form, row_size, counts, lists, values, *refs):
+    shards, (keep, send), scratch = nested(form, refs), refs[sum(form):-4], refs[-4:]
     acc = scratch[1]
     product_body("col", False, counts, lists, values, shards, scratch)
     per = (acc.shape[0] - 1) // row_size
@@ -98,15 +118,17 @@
         send[k // 2] = acc[pl.ds((me ^ (k + 1)) * per, per)].astype(BF16)
 
 
-def run_product(kernel, first, counts, lists, values, shards, panel_blocks, out_blocks, out_shape):
+def run_product(kernel, other, first, counts, lists, values, shards, panel_blocks, out_blocks, out_shape):
     slots, size = values.shape[0], values.shape[-1]
-    width = shards[0].shape[-1]
+    width = shards[0][0].shape[-1]
+    form = tuple(map(len, shards))
+    shards = jax.tree.leaves(shards)
     held = [
         pltpu.VMEM((panel_blocks, size, width), BF16),
         pltpu.VMEM((out_blocks + 1, size, width), F32),
     ]
     return pl.pallas_call(
-        kernel,
+        functools.partial(kernel, form, other),
         out_shape=out_shape,
         in_specs=[SMEM, ANY, VMEM, first] + [ANY] * (len(shards) - 1),
         out_specs=jax.tree.map(lambda _: VMEM, out_shape),
@@ -141,9 +163,13 @@
     gram[...] = total / nodes_total
 
 
-def core_sum_kernel(keep, came, *outs):
-    for k, out in enumerate(outs):
-        out[...] = (keep[k] + came[k].astype(F32)).astype(out.dtype)
+def core_sum_kernel(form, keep, came, *outs):
+    for k, pieces in enumerate(nested(form, outs)):
+        first = 0
+        for out in pieces:
+            span = pl.ds(first, out.shape[0])
+            out[...] = (keep[k, span] + came[k, span].astype(F32)).astype(out.dtype)
+            first += out.shape[0]
 
 
 def inverse_lower(gram):
@@ -222,8 +248,8 @@
     return scratch[...]
 
 
-def right_sum_kernel(nodes_total, inverse, own, *refs):
-    parts, (flipped, gram) = refs[:-2], refs[-2:]
+def right_sum_kernel(form, nodes_total, inverse, own, *refs):
+    parts, (flipped, gram) = nested(form, refs), refs[-2:]
     order = inverse.shape[0]
     factor = limbs(inverse[...], 3)
     full, head = jnp.concatenate(factor, 0), jnp.concatenate(factor[:2], 0)
@@ -231,7 +257,7 @@
     for b in range(own.shape[0]):
         summed = own[b]
         for part in parts:
-            summed = summed + part[b].astype(F32)
+            summed = summed + block_of(part, b)
         first, second = limbs(summed, 2)
         scaled = fold(jnp.dot(head, second, preferred_element_type=F32), order)
         scaled = scaled + fold(jnp.dot(full, first, preferred_element_type=F32), order)
@@ -289,13 +315,31 @@
 
 def gather_row(shard):
     row_size = lax.axis_size("row")
-    have = {0: shard}
-    bit = row_size // 2
+    top = row_size // 2
+    have = {0: [shard], top: [swap(piece, "row", top) for piece in halves(shard)]}
+    bit = top // 2
     while bit:
-        for k in sorted(have):
-            have[k | bit] = swap(have[k], "row", bit)
+        for k in sorted(have, reverse=True):
+            have[k | bit] = [swap(piece, "row", bit) for piece in have[k]]
         bit //= 2
     return [have[k] for k in range(row_size)]
+
+
+def collect_row(terms):
+    row_size = lax.axis_size("row")
+    came = []
+    bit = 2
+    while bit < row_size:
+        for k in sorted(terms, reverse=True):
+            if not k & bit:
+                continue
+            moved = [swap(piece.astype(BF16), "row", bit) for piece in terms.pop(k)]
+            if k ^ bit:
+                terms[k ^ bit] = [(a + b.astype(F32)) for a, b in zip(terms[k ^ bit], moved)]
+            else:
+                came.append(moved)
+        bit *= 2
+    return came
 
 
 def local(start_panel, block_values, block_rows, block_cols, block_counts):
@@ -322,7 +366,7 @@
 
     shards = gather_row(start_panel.reshape(block))
     parts = run_product(
-        functools.partial(left_kernel, row_size, col_size), HBM,
+        left_kernel, col_size, HBM,
         *tile, shards, col_blocks, row_blocks,
         [shape(block, F32)] + [shape(block, BF16)] * (col_size - 1),
     )
@@ -337,20 +381,28 @@
 
     half = (row_size // 2,) + block
     keep, send = run_product(
-        functools.partial(right_kernel, row_size, col_size), ANY,
-        *tile, turned, row_blocks, col_blocks,
+        right_kernel, row_size, ANY,
+        *tile, [[part] for part in turned], row_blocks, col_blocks,
         [shape(half, F32), shape(half, BF16)],
     )
+    pieces = {0: [shape(block, F32)]}
+    for k in range(2, row_size, 2):
+        far = 2 if k & (row_size // 2) and per % 2 == 0 else 1
+        kind = BF16 if k & 2 else F32
+        pieces[k] = [shape((per // far, size, width), kind)] * far
+    form = tuple(map(len, pieces.values()))
     sums = call(
-        core_sum_kernel, [shape(block, F32)] + [shape(block, BF16)] * (row_size // 2 - 1),
-        keep, swap(send, "row", 1),
-    )
-    came = [swap(sums[k // 2], "row", k) for k in range(2, row_size, 2)]
-    gram, _ = lax.optimization_barrier((gram, sums[-1]))
+        functools.partial(core_sum_kernel, form), jax.tree.leaves(list(pieces.values())), keep, swap(send, "row", 1)
+    )
+    terms = dict(zip(pieces, nested(form, sums)))
+    (own,) = terms.pop(0)
+    gram, _ = lax.optimization_barrier((gram, own))
+    came = collect_row(terms)
     grams = exchange(gram, "col", 1)
     inverse, left_panel = call(left_factor_kernel, (square, shape(block, BF16)), *grams, natural)
     right_flipped, gram = call(
-        functools.partial(right_sum_kernel, nodes_total), (shape(block, BF16), square), inverse, sums[0], *came
+        functools.partial(right_sum_kernel, tuple(map(len, came)), nodes_total),
+        (shape(block, BF16), square), inverse, own, *jax.tree.leaves(came),
     )
     gram = gram + swap(gram, "row", 1)
     gram = add_parts(exchange(gram, "col", 1))

time: 130 us -> 131 us (level)
  waiting for transfers between devices: 61.2 us -> 56.5 us
  starting transfers between devices: 41.4 us -> 44.9 us
    ppermute x31 -> x37, waiting for transfers between devices: 61.2 us -> 56.5 us  [swap(): return lax.ppermute(value, axis, [(i, i ^ mask) for i in range(size)])]
    ppermute x31 -> x37, starting transfers between devices: 41.4 us -> 44.9 us  [swap(): return lax.ppermute(value, axis, [(i, i ^ mask) for i in range(size)])]
  transfers between devices with their start and end apart: 31 -> 37, of which waited for: 19 -> 23; matrix products, arithmetic and copies ran while one was open for 0% -> 1% of each run, Pallas kernels for 5% -> 5%
where the time goes in v4:
time: 131 us
  waiting for transfers between devices  56.5 us (43%)
  starting transfers between devices  44.9 us (34%)
  Pallas kernels  21 us (16%)
  local copies, waits for them, and re-layouts  6.63 us (5%)
  between operations  1.49 us (1%)
    ppermute x37, waiting for transfers between devices, swap(): return lax.ppermute(value, axis, [(i, i ^ mask) for i in range(size)])  56.5 us
    ppermute x37, starting transfers between devices, swap(): return lax.ppermute(value, axis, [(i, i ^ mask) for i in range(size)])  44.9 us
    pallas_call x5, Pallas kernels, call(): pl.pallas_call(kernel, out_shape=out_shape, in_specs=[VMEM] * len(args),...  12.3 us
    pallas_call x2, Pallas kernels, run_product(): pl.pallas_call(functools.partial(kernel, form, other), out_shape=out_shap...  7.86 us
    unnamed x8, local copies, waits for them, and re-layouts  5.64 us
  transfers between devices with their start and end apart: 37, of which 23 were waited for; matrix products, arithmetic and copies ran while one was open for 1% of the time, Pallas kernels for 5%

profile of v4, /device:TPU:0, one launch (start us, length us, event | category | flops | bytes accessed | tf_op | source)
XLA Modules:
  0.0 130.6 jit_solution(18033572737701209817)
XLA Ops:
  0.6 3.1 %collective-permute-start.1 = (bf16[8,128,128]{2,1,0:T(8,128)(2,1)}, bf16[8,128,128]{2,1,0:T(8,128)(2,1)S(1)}, u32[]{:S(2)}, u32[]{:S(2)}) collective-permute-start(bf16[8,128,128]{2,1,0:T(8,128)(2,1)} %bitcast.5), channel_id=1, source_target_pairs={{0,8},{4,12},{8,0},{12,4},{16,24},{20,28},{24,16},{28,20},{1,9},{5... | collective-permute-start | bytes 786440 | tf_op jit(solution)/shard_map/ppermute | solution.py:35
  3.8 1.0 fusion.3
  4.8 2.7 %collective-permute-start.3 = (bf16[4,128,128]{2,1,0:T(8,128)(2,1)S(1)}, bf16[4,128,128]{2,1,0:T(8,128)(2,1)S(1)}, u32[]{:S(2)}, u32[]{:S(2)}) collective-permute-start(bf16[4,128,128]{2,1,0:T(8,128)(2,1)S(1)} %bitcast.10), channel_id=1, source_target_pairs={{0,16},{4,20},{8,24},{12,28},{16,0},{20,4},{24,8},{28,12},{1,17},{... | collective-permute-start | bytes 393224 | tf_op jit(solution)/shard_map/ppermute | solution.py:35
  7.4 0.3 collective-permute-start.4
  7.7 5.8 %collective-permute-done.3.refs_4_ = bf16[4,128,128]{2,1,0:T(8,128)(2,1)S(1)} collective-permute-done((bf16[4,128,128]{2,1,0:T(8,128)(2,1)S(1)}, bf16[4,128,128]{2,1,0:T(8,128)(2,1)S(1)}, u32[]{:S(2)}, u32[]{:S(2)}) %collective-permute-start.3) | collective-permute-done | bytes 131104 | tf_op jit(solution)/shard_map/ppermute | solution.py:35
  13.5 3.7 %collective-permute-start.7 = (bf16[4,128,128]{2,1,0:T(8,128)(2,1)S(1)}, bf16[4,128,128]{2,1,0:T(8,128)(2,1)S(1)}, u32[]{:S(2)}, u32[]{:S(2)}) collective-permute-start(bf16[4,128,128]{2,1,0:T(8,128)(2,1)S(1)} %collective-permute-done.3.refs_4_), channel_id=1, source_target_pairs={{0,8},{4,12},{8,0},{12,4},{16,24},{20,28},{24,16},{28,20},{1,9},{5... | collective-permute-start | bytes 393224 | tf_op jit(solution)/shard_map/ppermute | solution.py:35
  17.2 0.5 collective-permute-start.5
  17.7 1.3 collective-permute-done.4.refs_5_
  19.0 0.8 collective-permute-start.8
  19.8 1.1 collective-permute-done.7.refs_8_
  21.0 0.5 collective-permute-start.9
  21.5 2.5 %collective-permute-done.8.refs_9_ = bf16[4,128,128]{2,1,0:T(8,128)(2,1)S(1)} collective-permute-done((bf16[4,128,128]{2,1,0:T(8,128)(2,1)S(1)}, bf16[4,128,128]{2,1,0:T(8,128)(2,1)S(1)}, u32[]{:S(2)}, u32[]{:S(2)}) %collective-permute-start.8) | collective-permute-done | bytes 131104 | tf_op jit(solution)/shard_map/ppermute | solution.py:35
  24.7 4.3 %copy-done = bf16[1,1,352,128,128]{4,3,2,1,0:T(8,128)(2,1)S(1)} copy-done((bf16[1,1,352,128,128]{4,3,2,1,0:T(8,128)(2,1)S(1)}, bf16[1,1,352,128,128]{4,3,2,1,0:T(8,128)(2,1)}, u32[]{:S(2)}) %copy-start) | copy-done | bytes 11534360
  28.9 0.7 copy-done.2
  29.6 0.7 copy-done.3
  30.3 0.8 shard_map.68
  31.2 4.3 %shard_map.69 = (f32[8,128,128]{2,1,0:T(8,128)S(1)}, bf16[8,128,128]{2,1,0:T(8,128)(2,1)S(1)}, bf16[8,128,128]{2,1,0:T(8,128)(2,1)S(1)}, bf16[8,128,128]{2,1,0:T(8,128)(2,1)S(1)}) custom-call(s32[1,1]{1,0:T(1,128)S(6)} %copy.7.counts, s32[2,352]{1,0:T(2,128)S(1)} %get-tuple-element.29.lists, bf16[352,128,128]{2,1,0:T(8,128)(2,1)S(1)} %get-tuple-element.30.values, ...), custom_call_target="tpu_custom_call" | custom-call | flops 1476395008 | bytes 11534336 | tf_op jit(solution)/shard_map/pallas_call | solution.py:130
  35.5 1.5 %collective-permute-start.11 = (bf16[8,128,128]{2,1,0:T(8,128)(2,1)S(1)}, bf16[8,128,128]{2,1,0:T(8,128)(2,1)S(1)}, u32[]{:S(2)}, u32[]{:S(2)}) collective-permute-start(bf16[8,128,128]{2,1,0:T(8,128)(2,1)S(1)} %get-tuple-element.32), channel_id=1, source_target_pairs={{0,1},{1,0},{2,3},{3,2},{4,5},{5,4},{6,7},{7,6},{8,9},{9,8},{10,11... | collective-permute-start | bytes 786440 | tf_op jit(solution)/shard_map/ppermute | solution.py:35
  37.0 2.5 %collective-permute-start.12 = (bf16[8,128,128]{2,1,0:T(8,128)(2,1)S(1)}, bf16[8,128,128]{2,1,0:T(8,128)(2,1)S(1)}, u32[]{:S(2)}, u32[]{:S(2)}) collective-permute-start(bf16[8,128,128]{2,1,0:T(8,128)(2,1)S(1)} %get-tuple-element.33), channel_id=1, source_target_pairs={{0,2},{1,3},{2,0},{3,1},{4,6},{5,7},{6,4},{7,5},{8,10},{9,11},{10,... | collective-permute-start | bytes 786440 | tf_op jit(solution)/shard_map/ppermute | solution.py:35
  39.5 0.9 collective-permute-start.13
  40.5 2.0 %collective-permute-done.11.refs_0_ = bf16[8,128,128]{2,1,0:T(8,128)(2,1)S(1)} collective-permute-done((bf16[8,128,128]{2,1,0:T(8,128)(2,1)S(1)}, bf16[8,128,128]{2,1,0:T(8,128)(2,1)S(1)}, u32[]{:S(2)}, u32[]{:S(2)}) %collective-permute-start.11) | collective-permute-done | bytes 262176 | tf_op jit(solution)/shard_map/ppermute | solution.py:35
  42.5 8.7 %collective-permute-done.12.refs_1_ = bf16[8,128,128]{2,1,0:T(8,128)(2,1)S(1)} collective-permute-done((bf16[8,128,128]{2,1,0:T(8,128)(2,1)S(1)}, bf16[8,128,128]{2,1,0:T(8,128)(2,1)S(1)}, u32[]{:S(2)}, u32[]{:S(2)}) %collective-permute-start.12) | collective-permute-done | bytes 262176 | tf_op jit(solution)/shard_map/ppermute | solution.py:35
  51.1 1.9 %collective-permute-done.13.refs_2_ = bf16[8,128,128]{2,1,0:T(8,128)(2,1)S(1)} collective-permute-done((bf16[8,128,128]{2,1,0:T(8,128)(2,1)S(1)}, bf16[8,128,128]{2,1,0:T(8,128)(2,1)S(1)}, u32[]{:S(2)}, u32[]{:S(2)}) %collective-permute-start.13) | collective-permute-done | bytes 262176 | tf_op jit(solution)/shard_map/ppermute | solution.py:35
  53.0 0.3 shard_map.70
  53.4 1.2 collective-permute-done.14
  54.7 4.4 %collective-permute-start.17 = (bf16[128,128]{1,0:T(8,128)(2,1)S(1)}, bf16[128,128]{1,0:T(8,128)(2,1)S(1)}, u32[]{:S(2)}, u32[]{:S(2)}) collective-permute-start(bf16[128,128]{1,0:T(8,128)(2,1)S(1)} %get-tuple-element.60), channel_id=1, source_target_pairs={{0,24},{4,28},{8,16},{12,20},{16,8},{20,12},{24,0},{28,4},{1,25},{... | collective-permute-start | bytes 98312 | tf_op jit(solution)/shard_map/ppermute | solution.py:35
  59.1 0.6 collective-permute-start.15
  59.7 1.3 collective-permute-start.20
  61.0 0.5 collective-permute-start.19
  61.5 1.7 %collective-permute-start.18 = (bf16[8,128,128]{2,1,0:T(8,128)(2,1)S(1)}, bf16[8,128,128]{2,1,0:T(8,128)(2,1)S(1)}, u32[]{:S(2)}, u32[]{:S(2)}) collective-permute-start(bf16[8,128,128]{2,1,0:T(8,128)(2,1)S(1)} %get-tuple-element.38.refs_0_), channel_id=1, source_target_pairs={{0,1},{1,0},{2,3},{3,2},{4,5},{5,4},{6,7},{7,6},{8,9},{9,8},{10,11... | collective-permute-start | bytes 786440 | tf_op jit(solution)/shard_map/ppermute | solution.py:35
  63.2 0.7 collective-permute-done.16
  63.9 5.9 %collective-permute-done.20.refs_3_ = bf16[8,128,128]{2,1,0:T(8,128)(2,1)S(1)} collective-permute-done((bf16[8,128,128]{2,1,0:T(8,128)(2,1)S(1)}, bf16[8,128,128]{2,1,0:T(8,128)(2,1)S(1)}, u32[]{:S(2)}, u32[]{:S(2)}) %collective-permute-start.20) | collective-permute-done | bytes 262176 | tf_op jit(solution)/shard_map/ppermute | solution.py:35
  69.8 4.2 %collective-permute-done.19.refs_2_ = bf16[8,128,128]{2,1,0:T(8,128)(2,1)S(1)} collective-permute-done((bf16[8,128,128]{2,1,0:T(8,128)(2,1)S(1)}, bf16[8,128,128]{2,1,0:T(8,128)(2,1)S(1)}, u32[]{:S(2)}, u32[]{:S(2)}) %collective-permute-start.19) | collective-permute-done | bytes 262176 | tf_op jit(solution)/shard_map/ppermute | solution.py:35
  74.0 3.5 %shard_map.71 = (f32[4,8,128,128]{3,2,1,0:T(8,128)S(1)}, bf16[4,8,128,128]{3,2,1,0:T(8,128)(2,1)S(1)}) custom-call(s32[1,1]{1,0:T(1,128)S(6)} %copy.7.counts, s32[2,352]{1,0:T(2,128)S(1)} %get-tuple-element.29.lists, bf16[352,128,128]{2,1,0:T(8,128)(2,1)S(1)} %get-tuple-element.30.values, bf16[8,128,128]{2,1,0:T(8,128)(2,1)S(1)} %get-tuple-element.38.refs_0_, ...), custom_call_target="tpu_custom_call" | custom-call | flops 1476395008 | bytes 11534336 | tf_op jit(solution)/shard_map/pallas_call | solution.py:130
  77.5 3.0 %collective-permute-start.21 = (bf16[4,8,128,128]{3,2,1,0:T(8,128)(2,1)S(1)}, bf16[4,8,128,128]{3,2,1,0:T(8,128)(2,1)S(1)}, u32[]{:S(2)}, u32[]{:S(2)}) collective-permute-start(bf16[4,8,128,128]{3,2,1,0:T(8,128)(2,1)S(1)} %get-tuple-element.43), channel_id=1, source_target_pairs={{0,4},{4,0},{8,12},{12,8},{16,20},{20,16},{24,28},{28,24},{1,5},{5... | collective-permute-start | bytes 3145736 | tf_op jit(solution)/shard_map/ppermute | solution.py:35
  80.5 2.3 %collective-permute-done.21.came = bf16[4,8,128,128]{3,2,1,0:T(8,128)(2,1)S(1)} collective-permute-done((bf16[4,8,128,128]{3,2,1,0:T(8,128)(2,1)S(1)}, bf16[4,8,128,128]{3,2,1,0:T(8,128)(2,1)S(1)}, u32[]{:S(2)}, u32[]{:S(2)}) %collective-permute-start.21) | collective-permute-done | bytes 1048608 | tf_op jit(solution)/shard_map/ppermute | solution.py:35
  82.8 0.2 shard_map.72
  83.1 0.9 collective-permute-start.26
  83.9 1.2 collective-permute-start.28
  85.2 0.8 collective-permute-start.25
  86.0 3.5 %collective-permute-done.26 = bf16[4,128,128]{2,1,0:T(8,128)(2,1)S(1)} collective-permute-done((bf16[4,128,128]{2,1,0:T(8,128)(2,1)S(1)}, bf16[4,128,128]{2,1,0:T(8,128)(2,1)S(1)}, u32[]{:S(2)}, u32[]{:S(2)}) %collective-permute-start.26) | collective-permute-done | bytes 131104 | tf_op jit(solution)/shard_map/ppermute | solution.py:35
  89.5 0.8 collective-permute-start.27
  90.3 3.4 %collective-permute-done.28 = bf16[4,128,128]{2,1,0:T(8,128)(2,1)S(1)} collective-permute-done((bf16[4,128,128]{2,1,0:T(8,128)(2,1)S(1)}, bf16[4,128,128]{2,1,0:T(8,128)(2,1)S(1)}, u32[]{:S(2)}, u32[]{:S(2)}) %collective-permute-start.28) | collective-permute-done | bytes 131104 | tf_op jit(solution)/shard_map/ppermute | solution.py:35
  93.8 0.8 collective-permute-start.24
  94.6 2.3 %collective-permute-start.23 = (bf16[128,128]{1,0:T(8,128)(2,1)S(1)}, bf16[128,128]{1,0:T(8,128)(2,1)S(1)}, u32[]{:S(2)}, u32[]{:S(2)}) collective-permute-start(bf16[128,128]{1,0:T(8,128)(2,1)S(1)} %convert_element_type.46), channel_id=1, source_target_pairs={{0,2},{1,3},{2,0},{3,1},{4,6},{5,7},{6,4},{7,5},{8,10},{9,11},{10,... | collective-permute-start | bytes 98312 | tf_op jit(solution)/shard_map/ppermute | solution.py:35
  96.9 1.8 %collective-permute-done.24.refs_3_ = bf16[128,128]{1,0:T(8,128)(2,1)S(1)} collective-permute-done((bf16[128,128]{1,0:T(8,128)(2,1)S(1)}, bf16[128,128]{1,0:T(8,128)(2,1)S(1)}, u32[]{:S(2)}, u32[]{:S(2)}) %collective-permute-start.24) | collective-permute-done | bytes 32800 | tf_op jit(solution)/shard_map/ppermute | solution.py:35
  98.7 1.8 %collective-permute-start.22 = (bf16[128,128]{1,0:T(8,128)(2,1)S(1)}, bf16[128,128]{1,0:T(8,128)(2,1)S(1)}, u32[]{:S(2)}, u32[]{:S(2)}) collective-permute-start(bf16[128,128]{1,0:T(8,128)(2,1)S(1)} %convert_element_type.46), channel_id=1, source_target_pairs={{0,1},{1,0},{2,3},{3,2},{4,5},{5,4},{6,7},{7,6},{8,9},{9,8},{10,11... | collective-permute-start | bytes 98312 | tf_op jit(solution)/shard_map/ppermute | solution.py:35
  100.6 2.1 %collective-permute-done.22.refs_1_ = bf16[128,128]{1,0:T(8,128)(2,1)S(1)} collective-permute-done((bf16[128,128]{1,0:T(8,128)(2,1)S(1)}, bf16[128,128]{1,0:T(8,128)(2,1)S(1)}, u32[]{:S(2)}, u32[]{:S(2)}) %collective-permute-start.22) | collective-permute-done | bytes 32800 | tf_op jit(solution)/shard_map/ppermute | solution.py:35
  102.7 5.4 %shard_map.73 = (f32[128,128]{1,0:T(8,128)S(1)}, bf16[8,128,128]{2,1,0:T(8,128)(2,1)}) custom-call(f32[128,128]{1,0:T(8,128)S(1)} %convert_add_fusion.1.refs_0_, bf16[128,128]{1,0:T(8,128)(2,1)S(1)} %collective-permute-done.22.refs_1_, bf16[128,128]{1,0:T(8,128)(2,1)S(1)} %collective-permute-done.23.refs_2_, ...), custom_call_target="tpu_custom_call" | custom-call | tf_op jit(solution)/shard_map/pallas_call | solution.py:293
  108.1 1.2 shard_map.74
  109.4 1.2 collective-permute-done.30
  110.6 1.4 %collective-permute-start.33 = (bf16[128,128]{1,0:T(8,128)(2,1)S(1)}, bf16[128,128]{1,0:T(8,128)(2,1)S(1)}, u32[]{:S(2)}, u32[]{:S(2)}) collective-permute-start(bf16[128,128]{1,0:T(8,128)(2,1)S(1)} %get-tuple-element.58), channel_id=1, source_target_pairs={{0,3},{1,2},{2,1},{3,0},{4,7},{5,6},{6,5},{7,4},{8,11},{9,10},{10,... | collective-permute-start | bytes 98312 | tf_op jit(solution)/shard_map/ppermute | solution.py:35
  112.0 1.9 %collective-permute-start.32 = (bf16[128,128]{1,0:T(8,128)(2,1)S(1)}, bf16[128,128]{1,0:T(8,128)(2,1)S(1)}, u32[]{:S(2)}, u32[]{:S(2)}) collective-permute-start(bf16[128,128]{1,0:T(8,128)(2,1)S(1)} %get-tuple-element.58), channel_id=1, source_target_pairs={{0,2},{1,3},{2,0},{3,1},{4,6},{5,7},{6,4},{7,5},{8,10},{9,11},{10,... | collective-permute-start | bytes 98312 | tf_op jit(solution)/shard_map/ppermute | solution.py:35
  114.0 0.2 collective-permute-start.31
  114.2 1.3 %collective-permute-done.33 = bf16[128,128]{1,0:T(8,128)(2,1)S(1)} collective-permute-done((bf16[128,128]{1,0:T(8,128)(2,1)S(1)}, bf16[128,128]{1,0:T(8,128)(2,1)S(1)}, u32[]{:S(2)}, u32[]{:S(2)}) %collective-permute-start.33) | collective-permute-done | bytes 32800 | tf_op jit(solution)/shard_map/ppermute | solution.py:35
  115.5 0.4 collective-permute-done.32
  115.9 1.9 %collective-permute-done.31 = bf16[128,128]{1,0:T(8,128)(2,1)S(1)} collective-permute-done((bf16[128,128]{1,0:T(8,128)(2,1)S(1)}, bf16[128,128]{1,0:T(8,128)(2,1)S(1)}, u32[]{:S(2)}, u32[]{:S(2)}) %collective-permute-start.31) | collective-permute-done | bytes 32800 | tf_op jit(solution)/shard_map/ppermute | solution.py:35
  117.9 1.7 %collective-permute-start.36 = (bf16[128,128]{1,0:T(8,128)(2,1)S(1)}, bf16[128,128]{1,0:T(8,128)(2,1)S(1)}, u32[]{:S(2)}, u32[]{:S(2)}) collective-permute-start(bf16[128,128]{1,0:T(8,128)(2,1)S(1)} %get-tuple-element.56), channel_id=1, source_target_pairs={{0,24},{4,28},{8,16},{12,20},{16,8},{20,12},{24,0},{28,4},{1,25},{... | collective-permute-start | bytes 98312 | tf_op jit(solution)/shard_map/ppermute | solution.py:35
  119.6 2.0 %collective-permute-start.35 = (bf16[128,128]{1,0:T(8,128)(2,1)S(1)}, bf16[128,128]{1,0:T(8,128)(2,1)S(1)}, u32[]{:S(2)}, u32[]{:S(2)}) collective-permute-start(bf16[128,128]{1,0:T(8,128)(2,1)S(1)} %get-tuple-element.56), channel_id=1, source_target_pairs={{0,16},{4,20},{8,24},{12,28},{16,0},{20,4},{24,8},{28,12},{1,17},{... | collective-permute-start | bytes 98312 | tf_op jit(solution)/shard_map/ppermute | solution.py:35
  121.6 0.8 collective-permute-start.34
  122.4 1.4 %collective-permute-done.36.refs_3_ = bf16[128,128]{1,0:T(8,128)(2,1)S(1)} collective-permute-done((bf16[128,128]{1,0:T(8,128)(2,1)S(1)}, bf16[128,128]{1,0:T(8,128)(2,1)S(1)}, u32[]{:S(2)}, u32[]{:S(2)}) %collective-permute-start.36) | collective-permute-done | bytes 32800 | tf_op jit(solution)/shard_map/ppermute | solution.py:35
  123.8 1.0 collective-permute-done.35.refs_2_
  124.8 0.7 collective-permute-done.34.refs_1_
  125.5 5.1 %shard_map.75 = bf16[8,128,128]{2,1,0:T(8,128)(2,1)} custom-call(f32[128,128]{1,0:T(8,128)S(1)} %get-tuple-element.57.refs_0_, bf16[128,128]{1,0:T(8,128)(2,1)S(1)} %collective-permute-done.34.refs_1_, bf16[128,128]{1,0:T(8,128)(2,1)S(1)} %collective-permute-done.35.refs_2_, bf16[128,128]{1,0:T(8,128)(2,1)S(1)} %collective-permute-done.36.refs_3_, ...), custom_call_target="tpu_custom_call" | custom-call | tf_op jit(solution)/shard_map/pallas_call | solution.py:293
  (34 shorter events, 0.4 us)
Async XLA Ops:
  0.6 30.5 %copy-start.1 = (bf16[1024,128]{1,0:T(8,128)(2,1)S(1)}, bf16[1024,128]{1,0:T(8,128)(2,1)}, u32[]{:S(2)}) copy-start(bf16[1024,128]{1,0:T(8,128)(2,1)} %param.5) | copy-start | bytes 786436
  0.6 19.2 %collective-permute-start.1 = (bf16[8,128,128]{2,1,0:T(8,128)(2,1)}, bf16[8,128,128]{2,1,0:T(8,128)(2,1)S(1)}, u32[]{:S(2)}, u32[]{:S(2)}) collective-permute-start(bf16[8,128,128]{2,1,0:T(8,128)(2,1)} %bitcast.5), channel_id=1, source_target_pairs={{0,8},{4,12},{8,0},{12,4},{16,24},{20,28},{24,16},{28,20},{1,9},{5... | collective-permute-start | bytes 786440 | tf_op jit(solution)/shard_map/ppermute | solution.py:35
  4.8 8.8 %collective-permute-start.3 = (bf16[4,128,128]{2,1,0:T(8,128)(2,1)S(1)}, bf16[4,128,128]{2,1,0:T(8,128)(2,1)S(1)}, u32[]{:S(2)}, u32[]{:S(2)}) collective-permute-start(bf16[4,128,128]{2,1,0:T(8,128)(2,1)S(1)} %bitcast.10), channel_id=1, source_target_pairs={{0,16},{4,20},{8,24},{12,28},{16,0},{20,4},{24,8},{28,12},{1,17},{... | collective-permute-start | bytes 393224 | tf_op jit(solution)/shard_map/ppermute | solution.py:35
  7.4 11.6 %collective-permute-start.4 = (bf16[4,128,128]{2,1,0:T(8,128)(2,1)S(1)}, bf16[4,128,128]{2,1,0:T(8,128)(2,1)S(1)}, u32[]{:S(2)}, u32[]{:S(2)}) collective-permute-start(bf16[4,128,128]{2,1,0:T(8,128)(2,1)S(1)} %bitcast.9), channel_id=1, source_target_pairs={{0,16},{4,20},{8,24},{12,28},{16,0},{20,4},{24,8},{28,12},{1,17},{... | collective-permute-start | bytes 393224 | tf_op jit(solution)/shard_map/ppermute | solution.py:35
  13.5 7.4 %collective-permute-start.7 = (bf16[4,128,128]{2,1,0:T(8,128)(2,1)S(1)}, bf16[4,128,128]{2,1,0:T(8,128)(2,1)S(1)}, u32[]{:S(2)}, u32[]{:S(2)}) collective-permute-start(bf16[4,128,128]{2,1,0:T(8,128)(2,1)S(1)} %collective-permute-done.3.refs_4_), channel_id=1, source_target_pairs={{0,8},{4,12},{8,0},{12,4},{16,24},{20,28},{24,16},{28,20},{1,9},{5... | collective-permute-start | bytes 393224 | tf_op jit(solution)/shard_map/ppermute | solution.py:35
  17.2 13.9 %collective-permute-start = (bf16[8,128,128]{2,1,0:T(8,128)(2,1)}, bf16[8,128,128]{2,1,0:T(8,128)(2,1)S(1)}, u32[]{:S(2)}, u32[]{:S(2)}) collective-permute-start(bf16[8,128,128]{2,1,0:T(8,128)(2,1)} %bitcast.6), channel_id=1, source_target_pairs={{0,4},{4,0},{8,12},{12,8},{16,20},{20,16},{24,28},{28,24},{1,5},{5... | collective-permute-start | bytes 786440 | tf_op jit(solution)/shard_map/ppermute | solution.py:35
  17.2 3.7 %collective-permute-start.5 = (bf16[4,128,128]{2,1,0:T(8,128)(2,1)S(1)}, bf16[4,128,128]{2,1,0:T(8,128)(2,1)S(1)}, u32[]{:S(2)}, u32[]{:S(2)}) collective-permute-start(bf16[4,128,128]{2,1,0:T(8,128)(2,1)S(1)} %collective-permute-done.3.refs_4_), channel_id=1, source_target_pairs={{0,4},{4,0},{8,12},{12,8},{16,20},{20,16},{24,28},{28,24},{1,5},{5... | collective-permute-start | bytes 393224 | tf_op jit(solution)/shard_map/ppermute | solution.py:35
  19.0 5.0 %collective-permute-start.8 = (bf16[4,128,128]{2,1,0:T(8,128)(2,1)S(1)}, bf16[4,128,128]{2,1,0:T(8,128)(2,1)S(1)}, u32[]{:S(2)}, u32[]{:S(2)}) collective-permute-start(bf16[4,128,128]{2,1,0:T(8,128)(2,1)S(1)} %collective-permute-done.4.refs_5_), channel_id=1, source_target_pairs={{0,8},{4,12},{8,0},{12,4},{16,24},{20,28},{24,16},{28,20},{1,9},{5... | collective-permute-start | bytes 393224 | tf_op jit(solution)/shard_map/ppermute | solution.py:35
  19.8 11.3 %collective-permute-start.2 = (bf16[8,128,128]{2,1,0:T(8,128)(2,1)S(1)}, bf16[8,128,128]{2,1,0:T(8,128)(2,1)S(1)}, u32[]{:S(2)}, u32[]{:S(2)}) collective-permute-start(bf16[8,128,128]{2,1,0:T(8,128)(2,1)S(1)} %collective-permute-done.1.refs_2_), channel_id=1, source_target_pairs={{0,4},{4,0},{8,12},{12,8},{16,20},{20,16},{24,28},{28,24},{1,5},{5... | collective-permute-start | bytes 786440 | tf_op jit(solution)/shard_map/ppermute | solution.py:35
  20.9 10.1 %collective-permute-start.6 = (bf16[4,128,128]{2,1,0:T(8,128)(2,1)S(1)}, bf16[4,128,128]{2,1,0:T(8,128)(2,1)S(1)}, u32[]{:S(2)}, u32[]{:S(2)}) collective-permute-start(bf16[4,128,128]{2,1,0:T(8,128)(2,1)S(1)} %collective-permute-done.4.refs_5_), channel_id=1, source_target_pairs={{0,4},{4,0},{8,12},{12,8},{16,20},{20,16},{24,28},{28,24},{1,5},{5... | collective-permute-start | bytes 393224 | tf_op jit(solution)/shard_map/ppermute | solution.py:35
  21.0 10.2 %collective-permute-start.9 = (bf16[4,128,128]{2,1,0:T(8,128)(2,1)S(1)}, bf16[4,128,128]{2,1,0:T(8,128)(2,1)S(1)}, u32[]{:S(2)}, u32[]{:S(2)}) collective-permute-start(bf16[4,128,128]{2,1,0:T(8,128)(2,1)S(1)} %collective-permute-done.7.refs_8_), channel_id=1, source_target_pairs={{0,4},{4,0},{8,12},{12,8},{16,20},{20,16},{24,28},{28,24},{1,5},{5... | collective-permute-start | bytes 393224 | tf_op jit(solution)/shard_map/ppermute | solution.py:35
  24.0 7.1 %collective-permute-start.10 = (bf16[4,128,128]{2,1,0:T(8,128)(2,1)S(1)}, bf16[4,128,128]{2,1,0:T(8,128)(2,1)S(1)}, u32[]{:S(2)}, u32[]{:S(2)}) collective-permute-start(bf16[4,128,128]{2,1,0:T(8,128)(2,1)S(1)} %collective-permute-done.8.refs_9_), channel_id=1, source_target_pairs={{0,4},{4,0},{8,12},{12,8},{16,20},{20,16},{24,28},{28,24},{1,5},{5... | collective-permute-start | bytes 393224 | tf_op jit(solution)/shard_map/ppermute | solution.py:35
  24.7 4.3 %copy-start = (bf16[1,1,352,128,128]{4,3,2,1,0:T(8,128)(2,1)S(1)}, bf16[1,1,352,128,128]{4,3,2,1,0:T(8,128)(2,1)}, u32[]{:S(2)}) copy-start(bf16[1,1,352,128,128]{4,3,2,1,0:T(8,128)(2,1)} %values.1) | copy-start | bytes 34603012
  28.9 0.7 copy-start.2
  29.6 0.7 copy-start.3
  35.5 7.0 %collective-permute-start.11 = (bf16[8,128,128]{2,1,0:T(8,128)(2,1)S(1)}, bf16[8,128,128]{2,1,0:T(8,128)(2,1)S(1)}, u32[]{:S(2)}, u32[]{:S(2)}) collective-permute-start(bf16[8,128,128]{2,1,0:T(8,128)(2,1)S(1)} %get-tuple-element.32), channel_id=1, source_target_pairs={{0,1},{1,0},{2,3},{3,2},{4,5},{5,4},{6,7},{7,6},{8,9},{9,8},{10,11... | collective-permute-start | bytes 786440 | tf_op jit(solution)/shard_map/ppermute | solution.py:35
  37.0 14.1 %collective-permute-start.12 = (bf16[8,128,128]{2,1,0:T(8,128)(2,1)S(1)}, bf16[8,128,128]{2,1,0:T(8,128)(2,1)S(1)}, u32[]{:S(2)}, u32[]{:S(2)}) collective-permute-start(bf16[8,128,128]{2,1,0:T(8,128)(2,1)S(1)} %get-tuple-element.33), channel_id=1, source_target_pairs={{0,2},{1,3},{2,0},{3,1},{4,6},{5,7},{6,4},{7,5},{8,10},{9,11},{10,... | collective-permute-start | bytes 786440 | tf_op jit(solution)/shard_map/ppermute | solution.py:35
  39.5 13.5 %collective-permute-start.13 = (bf16[8,128,128]{2,1,0:T(8,128)(2,1)S(1)}, bf16[8,128,128]{2,1,0:T(8,128)(2,1)S(1)}, u32[]{:S(2)}, u32[]{:S(2)}) collective-permute-start(bf16[8,128,128]{2,1,0:T(8,128)(2,1)S(1)} %get-tuple-element.34), channel_id=1, source_target_pairs={{0,3},{1,2},{2,1},{3,0},{4,7},{5,6},{6,5},{7,4},{8,11},{9,10},{10,... | collective-permute-start | bytes 786440 | tf_op jit(solution)/shard_map/ppermute | solution.py:35
  53.4 1.3 %collective-permute-start.14 = (f32[128,128]{1,0:T(8,128)S(1)}, f32[128,128]{1,0:T(8,128)S(1)}, u32[]{:S(2)}, u32[]{:S(2)}) collective-permute-start(f32[128,128]{1,0:T(8,128)S(1)} %get-tuple-element.35), channel_id=1, source_target_pairs={{0,4},{4,0},{8,12},{12,8},{16,20},{20,16},{24,28},{28,24},{1,5},{5... | collective-permute-start | bytes 196616 | tf_op jit(solution)/shard_map/ppermute | solution.py:35
  54.7 6.8 %collective-permute-start.17 = (bf16[128,128]{1,0:T(8,128)(2,1)S(1)}, bf16[128,128]{1,0:T(8,128)(2,1)S(1)}, u32[]{:S(2)}, u32[]{:S(2)}) collective-permute-start(bf16[128,128]{1,0:T(8,128)(2,1)S(1)} %get-tuple-element.60), channel_id=1, source_target_pairs={{0,24},{4,28},{8,16},{12,20},{16,8},{20,12},{24,0},{28,4},{1,25},{... | collective-permute-start | bytes 98312 | tf_op jit(solution)/shard_map/ppermute | solution.py:35
  59.1 4.8 %collective-permute-start.16 = (bf16[128,128]{1,0:T(8,128)(2,1)S(1)}, bf16[128,128]{1,0:T(8,128)(2,1)S(1)}, u32[]{:S(2)}, u32[]{:S(2)}) collective-permute-start(bf16[128,128]{1,0:T(8,128)(2,1)S(1)} %get-tuple-element.60), channel_id=1, source_target_pairs={{0,16},{4,20},{8,24},{12,28},{16,0},{20,4},{24,8},{28,12},{1,17},{... | collective-permute-start | bytes 98312 | tf_op jit(solution)/shard_map/ppermute | solution.py:35
  59.1 4.8 %collective-permute-start.15 = (bf16[128,128]{1,0:T(8,128)(2,1)S(1)}, bf16[128,128]{1,0:T(8,128)(2,1)S(1)}, u32[]{:S(2)}, u32[]{:S(2)}) collective-permute-start(bf16[128,128]{1,0:T(8,128)(2,1)S(1)} %get-tuple-element.60), channel_id=1, source_target_pairs={{0,8},{4,12},{8,0},{12,4},{16,24},{20,28},{24,16},{28,20},{1,9},{5... | collective-permute-start | bytes 98312 | tf_op jit(solution)/shard_map/ppermute | solution.py:35
  59.7 10.1 %collective-permute-start.20 = (bf16[8,128,128]{2,1,0:T(8,128)(2,1)S(1)}, bf16[8,128,128]{2,1,0:T(8,128)(2,1)S(1)}, u32[]{:S(2)}, u32[]{:S(2)}) collective-permute-start(bf16[8,128,128]{2,1,0:T(8,128)(2,1)S(1)} %get-tuple-element.38.refs_0_), channel_id=1, source_target_pairs={{0,3},{1,2},{2,1},{3,0},{4,7},{5,6},{6,5},{7,4},{8,11},{9,10},{10,... | collective-permute-start | bytes 786440 | tf_op jit(solution)/shard_map/ppermute | solution.py:35
  61.0 13.0 %collective-permute-start.19 = (bf16[8,128,128]{2,1,0:T(8,128)(2,1)S(1)}, bf16[8,128,128]{2,1,0:T(8,128)(2,1)S(1)}, u32[]{:S(2)}, u32[]{:S(2)}) collective-permute-start(bf16[8,128,128]{2,1,0:T(8,128)(2,1)S(1)} %get-tuple-element.38.refs_0_), channel_id=1, source_target_pairs={{0,2},{1,3},{2,0},{3,1},{4,6},{5,7},{6,4},{7,5},{8,10},{9,11},{10,... | collective-permute-start | bytes 786440 | tf_op jit(solution)/shard_map/ppermute | solution.py:35
  61.5 12.5 %collective-permute-start.18 = (bf16[8,128,128]{2,1,0:T(8,128)(2,1)S(1)}, bf16[8,128,128]{2,1,0:T(8,128)(2,1)S(1)}, u32[]{:S(2)}, u32[]{:S(2)}) collective-permute-start(bf16[8,128,128]{2,1,0:T(8,128)(2,1)S(1)} %get-tuple-element.38.refs_0_), channel_id=1, source_target_pairs={{0,1},{1,0},{2,3},{3,2},{4,5},{5,4},{6,7},{7,6},{8,9},{9,8},{10,11... | collective-permute-start | bytes 786440 | tf_op jit(solution)/shard_map/ppermute | solution.py:35
  77.5 5.3 %collective-permute-start.21 = (bf16[4,8,128,128]{3,2,1,0:T(8,128)(2,1)S(1)}, bf16[4,8,128,128]{3,2,1,0:T(8,128)(2,1)S(1)}, u32[]{:S(2)}, u32[]{:S(2)}) collective-permute-start(bf16[4,8,128,128]{3,2,1,0:T(8,128)(2,1)S(1)} %get-tuple-element.43), channel_id=1, source_target_pairs={{0,4},{4,0},{8,12},{12,8},{16,20},{20,16},{24,28},{28,24},{1,5},{5... | collective-permute-start | bytes 3145736 | tf_op jit(solution)/shard_map/ppermute | solution.py:35
  83.1 6.4 %collective-permute-start.26 = (bf16[4,128,128]{2,1,0:T(8,128)(2,1)S(1)}, bf16[4,128,128]{2,1,0:T(8,128)(2,1)S(1)}, u32[]{:S(2)}, u32[]{:S(2)}) collective-permute-start(bf16[4,128,128]{2,1,0:T(8,128)(2,1)S(1)} %get-tuple-element.51), channel_id=1, source_target_pairs={{0,8},{4,12},{8,0},{12,4},{16,24},{20,28},{24,16},{28,20},{1,9},{5... | collective-permute-start | bytes 393224 | tf_op jit(solution)/shard_map/ppermute | solution.py:35
  83.9 9.8 %collective-permute-start.28 = (bf16[4,128,128]{2,1,0:T(8,128)(2,1)S(1)}, bf16[4,128,128]{2,1,0:T(8,128)(2,1)S(1)}, u32[]{:S(2)}, u32[]{:S(2)}) collective-permute-start(bf16[4,128,128]{2,1,0:T(8,128)(2,1)S(1)} %get-tuple-element.53), channel_id=1, source_target_pairs={{0,8},{4,12},{8,0},{12,4},{16,24},{20,28},{24,16},{28,20},{1,9},{5... | collective-permute-start | bytes 393224 | tf_op jit(solution)/shard_map/ppermute | solution.py:35
  85.2 22.9 %collective-permute-start.25 = (bf16[8,128,128]{2,1,0:T(8,128)(2,1)S(1)}, bf16[8,128,128]{2,1,0:T(8,128)(2,1)S(1)}, u32[]{:S(2)}, u32[]{:S(2)}) collective-permute-start(bf16[8,128,128]{2,1,0:T(8,128)(2,1)S(1)} %get-tuple-element.49), channel_id=1, source_target_pairs={{0,8},{4,12},{8,0},{12,4},{16,24},{20,28},{24,16},{28,20},{1,9},{5... | collective-permute-start | bytes 786440 | tf_op jit(solution)/shard_map/ppermute | solution.py:35
  89.5 18.5 %collective-permute-start.27 = (bf16[4,128,128]{2,1,0:T(8,128)(2,1)S(1)}, bf16[4,128,128]{2,1,0:T(8,128)(2,1)S(1)}, u32[]{:S(2)}, u32[]{:S(2)}) collective-permute-start(bf16[4,128,128]{2,1,0:T(8,128)(2,1)S(1)} %add_convert_fusion.1), channel_id=1, source_target_pairs={{0,16},{4,20},{8,24},{12,28},{16,0},{20,4},{24,8},{28,12},{1,17},{... | collective-permute-start | bytes 393224 | tf_op jit(solution)/shard_map/ppermute | solution.py:35
  93.8 14.3 %collective-permute-start.29 = (bf16[4,128,128]{2,1,0:T(8,128)(2,1)S(1)}, bf16[4,128,128]{2,1,0:T(8,128)(2,1)S(1)}, u32[]{:S(2)}, u32[]{:S(2)}) collective-permute-start(bf16[4,128,128]{2,1,0:T(8,128)(2,1)S(1)} %add_convert_fusion), channel_id=1, source_target_pairs={{0,16},{4,20},{8,24},{12,28},{16,0},{20,4},{24,8},{28,12},{1,17},{... | collective-permute-start | bytes 393224 | tf_op jit(solution)/shard_map/ppermute | solution.py:35
  93.8 4.9 %collective-permute-start.24 = (bf16[128,128]{1,0:T(8,128)(2,1)S(1)}, bf16[128,128]{1,0:T(8,128)(2,1)S(1)}, u32[]{:S(2)}, u32[]{:S(2)}) collective-permute-start(bf16[128,128]{1,0:T(8,128)(2,1)S(1)} %convert_element_type.46), channel_id=1, source_target_pairs={{0,3},{1,2},{2,1},{3,0},{4,7},{5,6},{6,5},{7,4},{8,11},{9,10},{10,... | collective-permute-start | bytes 98312 | tf_op jit(solution)/shard_map/ppermute | solution.py:35
  94.6 5.9 %collective-permute-start.23 = (bf16[128,128]{1,0:T(8,128)(2,1)S(1)}, bf16[128,128]{1,0:T(8,128)(2,1)S(1)}, u32[]{:S(2)}, u32[]{:S(2)}) collective-permute-start(bf16[128,128]{1,0:T(8,128)(2,1)S(1)} %convert_element_type.46), channel_id=1, source_target_pairs={{0,2},{1,3},{2,0},{3,1},{4,6},{5,7},{6,4},{7,5},{8,10},{9,11},{10,... | collective-permute-start | bytes 98312 | tf_op jit(solution)/shard_map/ppermute | solution.py:35
  98.7 3.9 %collective-permute-start.22 = (bf16[128,128]{1,0:T(8,128)(2,1)S(1)}, bf16[128,128]{1,0:T(8,128)(2,1)S(1)}, u32[]{:S(2)}, u32[]{:S(2)}) collective-permute-start(bf16[128,128]{1,0:T(8,128)(2,1)S(1)} %convert_element_type.46), channel_id=1, source_target_pairs={{0,1},{1,0},{2,3},{3,2},{4,5},{5,4},{6,7},{7,6},{8,9},{9,8},{10,11... | collective-permute-start | bytes 98312 | tf_op jit(solution)/shard_map/ppermute | solution.py:35
  109.3 1.3 %collective-permute-start.30 = (f32[128,128]{1,0:T(8,128)S(1)}, f32[128,128]{1,0:T(8,128)S(1)}, u32[]{:S(2)}, u32[]{:S(2)}) collective-permute-start(f32[128,128]{1,0:T(8,128)S(1)} %get-tuple-element.54), channel_id=1, source_target_pairs={{0,4},{4,0},{8,12},{12,8},{16,20},{20,16},{24,28},{28,24},{1,5},{5... | collective-permute-start | bytes 196616 | tf_op jit(solution)/shard_map/ppermute | solution.py:35
  110.6 4.9 %collective-permute-start.33 = (bf16[128,128]{1,0:T(8,128)(2,1)S(1)}, bf16[128,128]{1,0:T(8,128)(2,1)S(1)}, u32[]{:S(2)}, u32[]{:S(2)}) collective-permute-start(bf16[128,128]{1,0:T(8,128)(2,1)S(1)} %get-tuple-element.58), channel_id=1, source_target_pairs={{0,3},{1,2},{2,1},{3,0},{4,7},{5,6},{6,5},{7,4},{8,11},{9,10},{10,... | collective-permute-start | bytes 98312 | tf_op jit(solution)/shard_map/ppermute | solution.py:35
  112.0 3.9 %collective-permute-start.32 = (bf16[128,128]{1,0:T(8,128)(2,1)S(1)}, bf16[128,128]{1,0:T(8,128)(2,1)S(1)}, u32[]{:S(2)}, u32[]{:S(2)}) collective-permute-start(bf16[128,128]{1,0:T(8,128)(2,1)S(1)} %get-tuple-element.58), channel_id=1, source_target_pairs={{0,2},{1,3},{2,0},{3,1},{4,6},{5,7},{6,4},{7,5},{8,10},{9,11},{10,... | collective-permute-start | bytes 98312 | tf_op jit(solution)/shard_map/ppermute | solution.py:35
  114.0 3.9 %collective-permute-start.31 = (bf16[128,128]{1,0:T(8,128)(2,1)S(1)}, bf16[128,128]{1,0:T(8,128)(2,1)S(1)}, u32[]{:S(2)}, u32[]{:S(2)}) collective-permute-start(bf16[128,128]{1,0:T(8,128)(2,1)S(1)} %get-tuple-element.58), channel_id=1, source_target_pairs={{0,1},{1,0},{2,3},{3,2},{4,5},{5,4},{6,7},{7,6},{8,9},{9,8},{10,11... | collective-permute-start | bytes 98312 | tf_op jit(solution)/shard_map/ppermute | solution.py:35
  117.9 5.9 %collective-permute-start.36 = (bf16[128,128]{1,0:T(8,128)(2,1)S(1)}, bf16[128,128]{1,0:T(8,128)(2,1)S(1)}, u32[]{:S(2)}, u32[]{:S(2)}) collective-permute-start(bf16[128,128]{1,0:T(8,128)(2,1)S(1)} %get-tuple-element.56), channel_id=1, source_target_pairs={{0,24},{4,28},{8,16},{12,20},{16,8},{20,12},{24,0},{28,4},{1,25},{... | collective-permute-start | bytes 98312 | tf_op jit(solution)/shard_map/ppermute | solution.py:35
  119.6 5.2 %collective-permute-start.35 = (bf16[128,128]{1,0:T(8,128)(2,1)S(1)}, bf16[128,128]{1,0:T(8,128)(2,1)S(1)}, u32[]{:S(2)}, u32[]{:S(2)}) collective-permute-start(bf16[128,128]{1,0:T(8,128)(2,1)S(1)} %get-tuple-element.56), channel_id=1, source_target_pairs={{0,16},{4,20},{8,24},{12,28},{16,0},{20,4},{24,8},{28,12},{1,17},{... | collective-permute-start | bytes 98312 | tf_op jit(solution)/shard_map/ppermute | solution.py:35
  121.6 3.9 %collective-permute-start.34 = (bf16[128,128]{1,0:T(8,128)(2,1)S(1)}, bf16[128,128]{1,0:T(8,128)(2,1)S(1)}, u32[]{:S(2)}, u32[]{:S(2)}) collective-permute-start(bf16[128,128]{1,0:T(8,128)(2,1)S(1)} %get-tuple-element.56), channel_id=1, source_target_pairs={{0,8},{4,12},{8,0},{12,4},{16,24},{20,28},{24,16},{28,20},{1,9},{5... | collective-permute-start | bytes 98312 | tf_op jit(solution)/shard_map/ppermute | solution.py:35
